TPU v7x, 128 devices: a whole 4x4x4 slice. The times are simulated.
128 devices in a mesh: doc: 8 (over y, core), seq: 16 (over z, x).
Axes of the slice: x: 4, y: 4, z: 4, core: 2. Of those that a mesh axis runs over, the one named last changes fastest.
Arguments:
- hidden: bfloat16 [8, 8192, 768], P('doc', 'seq'), may hold values from -6 to 6
- token_ids: int32 [8, 8192], P('doc', 'seq'), may hold values from 0 to 50264, as said below
- w_query: bfloat16 [768, 768], replicated, may hold values from -0.625 to 0.625
- w_keyval: bfloat16 [768, 1536], replicated, may hold values from -0.21875 to 0.21875
- w_out: bfloat16 [768, 768], replicated, may hold values from -0.21875 to 0.21875
- x_query: bfloat16 [768, 768], replicated, may hold values from -0.21875 to 0.21875
- x_out: bfloat16 [768, 768], replicated, may hold values from -0.21875 to 0.21875
- shortlist: int32 [8, 320], P('doc'), may hold values from 0 to 36863, as said below
- code_row: int32 [36864], replicated, may hold values from 0 to 36863, as said below
- code_cache: bfloat16 [36864, 2, 8, 768], P(('doc', 'seq')), may hold values from -10 to 10
Outputs:
- refined: bfloat16 [8, 8192, 768], P('doc', 'seq')
- cand_score: float32 [8, 320], P('doc')
Inputs may be any that keep to these rules, and one draw needn't show every extreme that they name: `token_ids`: each summary is a run of ids of 1 or more followed by padding ids 0 up to its end; every summary has 2048 or more nonzero ids and one summary has no padding. `shortlist`: the candidates of one summary are distinct codes; at most 4 of them have code_row in one block of 288 rows (row // 288 equal), and for every summary some block holds exactly 4 of them. `code_row`: each row of the cache holds exactly one code.
All inputs are finite; a program needn't handle non-finite values.
Results may differ from a plain program's by a relative error of at most 0.018.
Values may be sent and summed in bfloat16 or wider, within the bound.
No kernel may reach another device: no remote copies, remote signals or barrier semaphores. Data moves between devices by JAX's collectives and lax.ppermute only.
A program may use at most 192 MiB of HBM per device.

v0:
```python
import math

import jax
import jax.numpy as jnp
from jax import lax
from jax.sharding import PartitionSpec as P

HEADS = 12
HALF_WIN = 256
DESC = 8


def extended(block, sides, width):
    for axis, dim in sides:
        count = lax.axis_size(axis)
        forward = [(i, i + 1) for i in range(count - 1)]
        backward = [(target, source) for source, target in forward]
        low = lax.ppermute(
            lax.slice_in_dim(block, block.shape[dim] - width, None, axis=dim), axis, forward
        )
        high = lax.ppermute(lax.slice_in_dim(block, 0, width, axis=dim), axis, backward)
        block = jnp.concatenate([low, block, high], axis=dim)
    return block


def layer_norm(values):
    centered = values - jnp.mean(values, axis=-1, keepdims=True)
    spread = jnp.mean(centered * centered, axis=-1, keepdims=True)
    return centered * lax.rsqrt(spread + 1e-05)


def attend(query, key_rows, value_rows, allowed, weigh):
    query_count, width = query.shape
    key_count = key_rows.shape[0]
    head_size = width // HEADS
    per_group = 4
    group_count = HEADS // per_group
    score_scale = 1.0 / math.sqrt(head_size)
    query_groups = query.reshape(query_count, group_count, per_group * head_size).transpose(1, 0, 2)
    key_groups = key_rows.reshape(key_count, group_count, per_group * head_size).transpose(1, 0, 2)
    value_groups = value_rows.reshape(key_count, group_count, per_group * head_size).transpose(
        1, 0, 2
    )

    def head_group(operands):
        group_query, group_keys, group_values = operands
        query_heads = group_query.reshape(query_count, per_group, head_size)
        key_heads = group_keys.reshape(key_count, per_group, head_size)
        value_heads = group_values.reshape(key_count, per_group, head_size)
        scores = (
            jnp.einsum("qhd,khd->hqk", query_heads, key_heads, preferred_element_type=jnp.float32)
            * score_scale
        )
        expd = jnp.where(allowed[None], jnp.exp(scores), 0.0)
        weights = expd / jnp.sum(expd, axis=-1, keepdims=True)
        context = jnp.einsum(
            "hqk,khd->qhd",
            weights.astype(jnp.bfloat16),
            value_heads,
            preferred_element_type=jnp.float32,
        )
        context = context.reshape(query_count, per_group * head_size).astype(jnp.bfloat16)
        if weigh is None:
            return (context, jnp.zeros((1,), jnp.float32))
        return (context, jnp.sum(jnp.where(weigh[None, :, None], weights, 0.0), axis=(0, 1)))

    contexts, masses = lax.map(head_group, (query_groups, key_groups, value_groups))
    context = contexts.transpose(1, 0, 2).reshape(query_count, width)
    return (context, jnp.sum(masses, axis=0))


def local(
    hidden, token_ids, w_query, w_keyval, w_out, x_query, x_out, shortlist, code_row, code_cache
):
    doc_hidden = hidden[0]
    doc_tokens = token_ids[0]
    tok_rows, width = doc_hidden.shape
    seq_count = lax.axis_size("seq")
    doc_count = lax.axis_size("doc")
    devices = seq_count * doc_count
    seq_index = lax.axis_index("seq")
    first_row = seq_index * tok_rows
    local_count = jnp.sum((doc_tokens != 0).astype(jnp.int32))
    length = lax.psum(local_count, "seq")
    normed = layer_norm(doc_hidden.astype(jnp.float32)).astype(jnp.bfloat16)
    query = jnp.dot(normed, w_query, preferred_element_type=jnp.float32).astype(jnp.bfloat16)
    keyval = jnp.dot(normed, w_keyval, preferred_element_type=jnp.float32).astype(jnp.bfloat16)
    padded = extended(keyval, (("seq", 0),), HALF_WIN)
    query_pos = first_row + jnp.arange(tok_rows, dtype=jnp.int32)
    key_pos = first_row - HALF_WIN + jnp.arange(tok_rows + 2 * HALF_WIN, dtype=jnp.int32)
    near = jnp.abs(query_pos[:, None] - key_pos[None, :]) <= HALF_WIN
    usable = ((key_pos >= 0) & (key_pos < length))[None, :] | (
        query_pos[:, None] == key_pos[None, :]
    )
    context, unused = attend(query, padded[:, :width], padded[:, width:], near & usable, None)
    middle = (
        doc_hidden.astype(jnp.float32) + jnp.dot(context, w_out, preferred_element_type=jnp.float32)
    ).astype(jnp.bfloat16)
    middle_wide = middle.astype(jnp.float32)
    cross_normed = layer_norm(middle_wide).astype(jnp.bfloat16)
    cross_query = jnp.dot(cross_normed, x_query, preferred_element_type=jnp.float32).astype(
        jnp.bfloat16
    )
    cand_count = shortlist.shape[1]
    code_dev = code_cache.shape[0]
    capacity = 8 * cand_count // (5 * devices)
    cache_rows = code_row[shortlist[0]]
    owner_dev = cache_rows // code_dev
    local_row = cache_rows % code_dev
    onehot = (owner_dev[:, None] == jnp.arange(devices, dtype=jnp.int32)[None, :]).astype(jnp.int32)
    slot_rank = jnp.sum((jnp.cumsum(onehot, axis=0) - 1) * onehot, axis=1)
    request = jnp.zeros((devices, capacity), jnp.int32).at[owner_dev, slot_rank].set(local_row)
    slot_live = jnp.zeros((devices, capacity), jnp.bool_).at[owner_dev, slot_rank].set(True)
    fetched_rows = lax.all_to_all(
        code_cache[
            lax.all_to_all(request, ("doc", "seq"), split_axis=0, concat_axis=0, tiled=True)
        ],
        ("doc", "seq"),
        split_axis=0,
        concat_axis=0,
        tiled=True,
    )
    live_keys = slot_live.reshape(-1)
    slot_index = owner_dev * capacity + slot_rank
    fetched_rows = fetched_rows.reshape(devices * capacity, 2, DESC, width)
    cand_keys = fetched_rows[:, 0].reshape(devices * capacity * DESC, width)
    cand_values = fetched_rows[:, 1].reshape(devices * capacity * DESC, width)
    key_live = jnp.repeat(live_keys, DESC)
    allowed = jnp.broadcast_to(key_live[None, :], (tok_rows, key_live.shape[0]))
    cross_context, key_mass = attend(
        cross_query, cand_keys, cand_values, allowed, query_pos < length
    )
    refined = (
        middle_wide + jnp.dot(cross_context, x_out, preferred_element_type=jnp.float32)
    ).astype(jnp.bfloat16)
    local_mass = jnp.sum(key_mass.reshape(devices * capacity, DESC), axis=1)
    slot_total = lax.psum(local_mass, "seq")
    cand_score = cand_count * slot_total[slot_index] / (HEADS * length.astype(jnp.float32))
    return (refined[None], cand_score[None])


def solution(mesh):
    return jax.shard_map(
        local,
        mesh=mesh,
        in_specs=(
            P("doc", "seq", None),
            P("doc", "seq"),
            P(),
            P(),
            P(),
            P(),
            P(),
            P("doc", None),
            P(),
            P(("doc", "seq"), None, None, None),
        ),
        out_specs=(P("doc", "seq", None), P("doc", None)),
        check_vma=False,
    )
```

profile of v0, /device:TPU:2, one launch (start us, length us, event | category | flops | bytes accessed | tf_op | source)
XLA Modules:
  0.0 577.0 jit_solution(14737333442104114275)
XLA Ops:
  0.6 0.8 fusion.44
  1.5 3.6 gather_fusion
  5.8 15.1 %scatter_fusion = s32[128,4]{0,1:T(4,128)S(1)} fusion(s32[128,4]{0,1:T(4,128)S(1)} %broadcast.287, s32[320]{0:T(512)S(1)} %get-tuple-element.144, s32[320]{0:T(512)S(1)} %get-tuple-element.195), kind=kCustom, calls=%fused_computation.3 | custom fusion | bytes 6400 | tf_op jit(solution)/shard_map/scatter | solution.py:112
  21.0 19.4 %all_to_all.17 = s32[128,1,4]{2,1,0:T(1,128)S(1)} all-to-all(s32[128,1,4]{2,1,0:T(1,128)S(1)} %copy.33), channel_id=1, replica_groups=mesh['doc'=8,'seq'=16] {'doc','seq'}, dimensions={0} | all-to-all | bytes 4096 | tf_op jit(solution)/shard_map/all_to_all | solution.py:116
  40.6 18.1 %gather_fusion.1 = bf16[512,2,8,768]{3,2,1,0:T(8,128)(2,1)} fusion(bf16[288,2,8,768]{3,2,1,0:T(8,128)(2,1)} %param.23, s32[1024]{0:T(1024)S(1)} %pad_clamp_fusion.1), kind=kCustom, calls=%fused_computation.1 | custom fusion | bytes 25167872 | tf_op jit(solution)/shard_map/gather | solution.py:115
  58.7 6.2 %all-to-all-start.1 = ((bf16[128,4,2,8,768]{4,3,2,1,0:T(8,128)(2,1)}), bf16[128,4,2,8,768]{4,3,2,1,0:T(8,128)(2,1)}, u32[]{:S(2)}, u32[]{:S(2)}) async-start(bf16[128,4,2,8,768]{4,3,2,1,0:T(8,128)(2,1)} %bitcast.122), calls=%async_computation.1 | async-start | bytes 25165824 | tf_op jit(solution)/shard_map/all_to_all | solution.py:114
  65.5 1.5 convolution_convert_fusion
  67.0 1.2 copy-done.2
  68.2 1.2 fusion.53
  69.4 3.4 collective-permute-start
  72.8 3.3 collective-permute-start.1
  76.8 181.6 %psum.14 = s32[]{:T(128)} all-reduce(s32[]{:T(128)} %fusion.42), channel_id=1, replica_groups=mesh['doc'=8,'seq'=16] {'seq'}, use_global_device_ids=true, to_apply=%region_3.0 | all-reduce | flops 1 | bytes 8 | tf_op jit(solution)/shard_map/psum | solution.py:84
  258.5 1.8 convolution_convert_fusion.2
  260.2 1.5 copy.29
  261.8 15.7 %scatter_fusion.1 = pred[128,4]{0,1:T(4,128)(4,1)S(1)} fusion(pred[128,4]{0,1:T(4,128)(4,1)S(1)} %broadcast_in_dim.57, s32[320]{0:T(512)S(1)} %get-tuple-element.144, pred[320]{0:T(512)(128)(4,1)S(1)} %broadcast.330), kind=kCustom, calls=%fused_computation.4 | custom fusion | bytes 3520 | tf_op jit(solution)/shard_map/scatter | solution.py:113
  280.0 1.5 pad_maximum_fusion
  281.5 1.4 fusion.52
  282.8 2.6 copy.28
  285.4 1.6 copy.30
  287.1 0.9 broadcast.284.clone
  288.0 23.4 %while.24 = (s32[]{:T(128)}, bf16[3,512,256]{1,2,0:T(8,128)(2,1)}, bf16[3,1024,256]{1,2,0:T(8,128)(2,1)}, bf16[3,512,256]{1,2,0:T(8,128)(2,1)S(1)}, bf16[3,1024,...) while((s32[]{:T(128)}, bf16[3,512,256]{1,2,0:T(8,128)(2,1)}, ...), condition=%wide.region_6.7_spmd.clone, body=%wide.region_4.6_spmd.clone.sunk | while | flops 554825728 | bytes 23092836 | solution.py:67
  288.0 1.3 constant_dynamic-slice_fusion.10
  289.3 0.9 fusion.82
  290.2 2.5 fusion.83
  292.7 2.4 fusion.84
  295.1 0.7 constant_dynamic-update-slice_fusion.4
  295.8 1.3 constant_dynamic-slice_fusion.10
  297.1 0.9 fusion.82
  298.0 2.5 fusion.83
  300.5 2.4 fusion.84
  302.9 0.7 constant_dynamic-update-slice_fusion.4
  303.6 1.3 constant_dynamic-slice_fusion.10
  304.9 0.9 fusion.82
  305.8 2.5 fusion.83
  308.3 2.4 fusion.84
  310.7 0.7 constant_dynamic-update-slice_fusion.4
  311.5 2.7 convert_reduce_fusion
  314.6 0.8 convolution_convert_fusion.1
  315.7 6.3 %copy.34 = bf16[128,4,2,8,768]{4,3,1,0,2:T(8,128)(2,1)S(1)} copy(bf16[128,4,2,8,768]{4,3,2,1,0:T(8,128)(2,1)} %all-to-all-done.1) | data formatting | bytes 25165824 | tf_op jit(solution)/shard_map/all_to_all | solution.py:114
  322.0 5.1 fusion.51
  327.1 17.3 %reshape_reshape_squeeze.6 = bf16[4096,3,256]{2,1,0:T(4,128)(2,1)} reshape(bf16[512,1,8,768]{3,2,0,1:T(8,128)(2,1)} %get-tuple-element.190) | data formatting | bytes 12582912 | tf_op jit(solution)/shard_map/reshape;reshape;squeeze | solution.py:41
  344.4 13.1 %copy.37 = bf16[3,4096,256]{1,2,0:T(8,128)(2,1)} copy(bf16[3,4096,256]{2,0,1:T(4,128)(2,1)} %bitcast.124) | data formatting | bytes 12582912
  357.5 17.3 %reshape_reshape_squeeze.7 = bf16[4096,3,256]{2,1,0:T(4,128)(2,1)} reshape(bf16[512,1,8,768]{3,2,0,1:T(8,128)(2,1)} %get-tuple-element.189) | data formatting | bytes 12582912 | tf_op jit(solution)/shard_map/reshape;reshape;squeeze | solution.py:40
  374.8 13.1 %copy.38 = bf16[3,4096,256]{1,2,0:T(8,128)(2,1)} copy(bf16[3,4096,256]{2,0,1:T(4,128)(2,1)} %bitcast.125) | data formatting | bytes 12582912
  387.9 1.0 broadcast.284
  388.9 141.8 %while.25 = (s32[]{:T(128)}, bf16[3,512,256]{1,2,0:T(8,128)(2,1)}, f32[3,4096]{1,0:T(4,128)S(1)}, bf16[3,4096,256]{1,2,0:T(8,128)(2,1)}, bf16[3,512,256]{1,2,0:T...) while((s32[]{:T(128)}, bf16[3,512,256]{1,2,0:T(8,128)(2,1)}, ...), condition=%wide.region_17.18_spmd.clone, body=%wide.region_14.17_spmd.clone.sunk | while | flops 2248272896 | bytes 114906752 | solution.py:67
  388.9 2.6 constant_dynamic-slice_fusion.12
  391.5 14.1 %fusion.89 = (f32[4,512]{1,0:T(4,128)S(1)}, f32[4,512,4096]{2,1,0:T(8,128)}) fusion(pred[4096]{0:T(1024)(128)(4,1)S(1)} %get-tuple-element.374, bf16[512,4,64]{0,2,1:T(8,128)(2,1)S(1)} %bitcast.133, bf16[4096,4,64]{0,2,1:T(8,128)(2,1)S(1)} %bitcast.121), kind=kOutput, calls=%fused_computation.24.clone.1 | convolution fusion | flops 1098905600 | bytes 35926016 | tf_op jit(solution)/shard_map/while/body/eval_jaxpr/qhd,khd->hqk/dot_general | solution.py:51
  406.3 14.8 %select_reduce_fusion.2 = f32[4096]{0:T(1024)S(1)} fusion(pred[512]{0:T(512)(128)(4,1)S(1)} %add_compare_fusion.2, f32[4,512]{1,0:T(4,128)S(1)} %get-tuple-element.317, f32[4,512,4096]{2,1,0:T(8,128)} %get-tuple-element.318, pred[4096]{0:T(1024)(128)(4,1)S(1)} %get-tuple-element.374), kind=kLoop, calls=%fused_computation.21.clone.1 | loop fusion | flops 41938944 | bytes 33583616 | tf_op jit(solution)/shard_map/while/body/eval_jaxpr/reduce_sum | solution.py:65
  421.3 14.1 %fusion.90 = bf16[4,64,512]{2,1,0:T(8,128)(2,1)S(1)} fusion(bf16[4096,4,64]{0,2,1:T(8,128)(2,1)S(1)} %bitcast.120, f32[4,512]{1,0:T(4,128)S(1)} %get-tuple-element.317, f32[4,512,4096]{2,1,0:T(8,128)} %get-tuple-element.318, pred[4096]{0:T(1024)(128)(4,1)S(1)} %get-tuple-element.374), kind=kOutput, calls=%fused_computation.27.clone.1 | convolution fusion | flops 1107427328 | bytes 35926016 | tf_op jit(solution)/shard_map/while/body/eval_jaxpr/hqk,khd->qhd/dot_general | solution.py:56
  435.4 0.7 constant_dynamic-update-slice_fusion.5
  436.1 2.6 constant_dynamic-slice_fusion.12
  438.8 14.1 %fusion.89 = (f32[4,512]{1,0:T(4,128)S(1)}, f32[4,512,4096]{2,1,0:T(8,128)}) fusion(pred[4096]{0:T(1024)(128)(4,1)S(1)} %get-tuple-element.374, bf16[512,4,64]{0,2,1:T(8,128)(2,1)S(1)} %bitcast.133, bf16[4096,4,64]{0,2,1:T(8,128)(2,1)S(1)} %bitcast.121), kind=kOutput, calls=%fused_computation.24.clone.1 | convolution fusion | flops 1098905600 | bytes 35926016 | tf_op jit(solution)/shard_map/while/body/eval_jaxpr/qhd,khd->hqk/dot_general | solution.py:51
  453.6 14.8 %select_reduce_fusion.2 = f32[4096]{0:T(1024)S(1)} fusion(pred[512]{0:T(512)(128)(4,1)S(1)} %add_compare_fusion.2, f32[4,512]{1,0:T(4,128)S(1)} %get-tuple-element.317, f32[4,512,4096]{2,1,0:T(8,128)} %get-tuple-element.318, pred[4096]{0:T(1024)(128)(4,1)S(1)} %get-tuple-element.374), kind=kLoop, calls=%fused_computation.21.clone.1 | loop fusion | flops 41938944 | bytes 33583616 | tf_op jit(solution)/shard_map/while/body/eval_jaxpr/reduce_sum | solution.py:65
  468.6 14.1 %fusion.90 = bf16[4,64,512]{2,1,0:T(8,128)(2,1)S(1)} fusion(bf16[4096,4,64]{0,2,1:T(8,128)(2,1)S(1)} %bitcast.120, f32[4,512]{1,0:T(4,128)S(1)} %get-tuple-element.317, f32[4,512,4096]{2,1,0:T(8,128)} %get-tuple-element.318, pred[4096]{0:T(1024)(128)(4,1)S(1)} %get-tuple-element.374), kind=kOutput, calls=%fused_computation.27.clone.1 | convolution fusion | flops 1107427328 | bytes 35926016 | tf_op jit(solution)/shard_map/while/body/eval_jaxpr/hqk,khd->qhd/dot_general | solution.py:56
  482.7 0.7 constant_dynamic-update-slice_fusion.5
  483.4 2.6 constant_dynamic-slice_fusion.12
  486.0 14.1 %fusion.89 = (f32[4,512]{1,0:T(4,128)S(1)}, f32[4,512,4096]{2,1,0:T(8,128)}) fusion(pred[4096]{0:T(1024)(128)(4,1)S(1)} %get-tuple-element.374, bf16[512,4,64]{0,2,1:T(8,128)(2,1)S(1)} %bitcast.133, bf16[4096,4,64]{0,2,1:T(8,128)(2,1)S(1)} %bitcast.121), kind=kOutput, calls=%fused_computation.24.clone.1 | convolution fusion | flops 1098905600 | bytes 35926016 | tf_op jit(solution)/shard_map/while/body/eval_jaxpr/qhd,khd->hqk/dot_general | solution.py:51
  500.8 14.8 %select_reduce_fusion.2 = f32[4096]{0:T(1024)S(1)} fusion(pred[512]{0:T(512)(128)(4,1)S(1)} %add_compare_fusion.2, f32[4,512]{1,0:T(4,128)S(1)} %get-tuple-element.317, f32[4,512,4096]{2,1,0:T(8,128)} %get-tuple-element.318, pred[4096]{0:T(1024)(128)(4,1)S(1)} %get-tuple-element.374), kind=kLoop, calls=%fused_computation.21.clone.1 | loop fusion | flops 41938944 | bytes 33583616 | tf_op jit(solution)/shard_map/while/body/eval_jaxpr/reduce_sum | solution.py:65
  515.9 14.1 %fusion.90 = bf16[4,64,512]{2,1,0:T(8,128)(2,1)S(1)} fusion(bf16[4096,4,64]{0,2,1:T(8,128)(2,1)S(1)} %bitcast.120, f32[4,512]{1,0:T(4,128)S(1)} %get-tuple-element.317, f32[4,512,4096]{2,1,0:T(8,128)} %get-tuple-element.318, pred[4096]{0:T(1024)(128)(4,1)S(1)} %get-tuple-element.374), kind=kOutput, calls=%fused_computation.27.clone.1 | convolution fusion | flops 1107427328 | bytes 35926016 | tf_op jit(solution)/shard_map/while/body/eval_jaxpr/hqk,khd->qhd/dot_general | solution.py:56
  530.0 0.7 constant_dynamic-update-slice_fusion.5
  531.1 39.7 %psum.15 = f32[512]{0:T(512)S(1)} all-reduce(f32[512]{0:T(512)S(1)} %reduce_sum.109), channel_id=1, replica_groups=mesh['doc'=8,'seq'=16] {'seq'}, use_global_device_ids=true, to_apply=%region_20.21 | all-reduce | flops 512 | bytes 4096 | tf_op jit(solution)/shard_map/psum | solution.py:137
  570.7 2.4 gather_fusion.2
  573.8 3.2 fusion.34
  (77 shorter events, 8.3 us)
Async XLA Ops:
  0.6 64.9 %copy-start = (bf16[768,1536]{1,0:T(8,128)(2,1)S(1)}, bf16[768,1536]{1,0:T(8,128)(2,1)}, u32[]{:S(2)}) copy-start(bf16[768,1536]{1,0:T(8,128)(2,1)} %param.17) | copy-start | bytes 7077892
  58.7 6.2 %copy-start.4 = (bf16[1,512,768]{2,1,0:T(8,128)(2,1)S(1)}, bf16[1,512,768]{2,1,0:T(8,128)(2,1)}, u32[]{:S(2)}) copy-start(bf16[1,512,768]{2,1,0:T(8,128)(2,1)} %param.14) | copy-start | bytes 2359300
  58.7 257.1 %all-to-all-start.1 = ((bf16[128,4,2,8,768]{4,3,2,1,0:T(8,128)(2,1)}), bf16[128,4,2,8,768]{4,3,2,1,0:T(8,128)(2,1)}, u32[]{:S(2)}, u32[]{:S(2)}) async-start(bf16[128,4,2,8,768]{4,3,2,1,0:T(8,128)(2,1)} %bitcast.122), calls=%async_computation.1 | async-start | bytes 25165824 | tf_op jit(solution)/shard_map/all_to_all | solution.py:114
  67.0 1.2 copy-start.2
  68.2 8.0 %copy-start.8 = (s32[1,512]{1,0:T(1,128)S(1)}, s32[1,512]{1,0:T(1,128)}, u32[]{:S(2)}) copy-start(s32[1,512]{1,0:T(1,128)} %param.15) | copy-start | bytes 6148
  68.2 190.3 %copy-start.9 = (bf16[768,768]{1,0:T(8,128)(2,1)S(1)}, bf16[768,768]{1,0:T(8,128)(2,1)}, u32[]{:S(2)}) copy-start(bf16[768,768]{1,0:T(8,128)(2,1)} %param.16) | copy-start | bytes 3538948
  69.4 210.5 %collective-permute-start = (bf16[256,1536]{1,0:T(8,128)(2,1)}, bf16[256,1536]{1,0:T(8,128)(2,1)}, u32[]{:S(2)}, u32[]{:S(2)}) collective-permute-start(bf16[256,1536]{1,0:T(8,128)(2,1)} %get-tuple-element.193), channel_id=1, source_target_pairs={{0,1},{1,2},{2,3},{3,4},{4,5},{5,6},{6,7},{7,8},{8,9},{9,10},{10,1... | collective-permute-start | bytes 2359304 | tf_op jit(solution)/shard_map/ppermute | solution.py:18
  72.8 207.1 %collective-permute-start.1 = (bf16[256,1536]{1,0:T(8,128)(2,1)}, bf16[256,1536]{1,0:T(8,128)(2,1)}, u32[]{:S(2)}, u32[]{:S(2)}) collective-permute-start(bf16[256,1536]{1,0:T(8,128)(2,1)} %get-tuple-element.194), channel_id=1, source_target_pairs={{1,0},{2,1},{3,2},{4,3},{5,4},{6,5},{7,6},{8,7},{9,8},{10,9},{11,1... | collective-permute-start | bytes 2359304 | tf_op jit(solution)/shard_map/ppermute | solution.py:21
  260.2 19.7 %copy-start.3 = (bf16[512,1536]{1,0:T(8,128)(2,1)S(1)}, bf16[512,1536]{1,0:T(8,128)(2,1)}, u32[]{:S(2)}) copy-start(bf16[512,1536]{1,0:T(8,128)(2,1)} %copy-done.2) | copy-start | bytes 4718596
  311.5 3.1 copy-start.10
  314.2 1.3 copy-start.5
  388.9 181.9 %copy-start.7 = (s32[1024]{0:T(1024)S(1)}, s32[1024]{0:T(1024)}, u32[]{:S(2)}) copy-start(s32[1024]{0:T(1024)} %pad_clamp_fusion) | copy-start | bytes 12292
  530.7 43.1 %copy-start.6 = (bf16[512,768]{1,0:T(8,128)(2,1)S(1)}, bf16[512,768]{1,0:T(8,128)(2,1)}, u32[]{:S(2)}) copy-start(bf16[512,768]{1,0:T(8,128)(2,1)} %copy-done.5) | copy-start | bytes 2359300
  570.7 6.3 %copy-start.1 = (bf16[768,1536]{1,0:T(8,128)(2,1)S(1)}, bf16[768,1536]{1,0:T(8,128)(2,1)}, u32[]{:S(2)}) copy-start(bf16[768,1536]{1,0:T(8,128)(2,1)} %param.17) | copy-start | bytes 7077892
where the time goes:
time: 589 us; the launch traced here: 577 us
  blocking collectives  241 us (41%)
  local copies, waits for them, and re-layouts  157 us (27%)
  matrix products  109 us (19%)
  other arithmetic  54.9 us (9%)
  starting transfers between devices  12.9 us (2%)
    psum x1, blocking collectives, local(): length = lax.psum(local_count, 'seq')  182 us
    dot_general x6, matrix products, head_group(): jnp.einsum('qhd,khd->hqk', query_heads, key_heads, preferred_element_type...  49.9 us
    dot_general x6, matrix products, head_group(): jnp.einsum('hqk,khd->qhd', weights.astype(jnp.bfloat16), value_heads, pre...  49.4 us
    reduce_sum x3, other arithmetic, head_group(): jnp.sum(jnp.where(weigh[None, :, None], weights, 0.0), axis=(0, 1))  44.4 us
    psum x1, blocking collectives, local(): slot_total = lax.psum(local_mass, 'seq')  39.7 us
    unnamed x24, local copies, waits for them, and re-layouts  27.4 us
    all_to_all x1, blocking collectives, local(): lax.all_to_all(request, ('doc', 'seq'), split_axis=0, concat_axis=0, tile...  19.4 us
    gather x1, local copies, waits for them, and re-layouts, local(): code_cache[lax.all_to_all(request, ('doc', 'seq'), split_axis=0, concat_a...  18.1 us
  transfers between devices with their start and end apart: 3, of which 0 were waited for; matrix products, arithmetic and copies ran while one was open for 10% of the time, Pallas kernels for 0%

commit v1 on v0

v1 whole, which is shorter than its diff:
```python
import functools
import math

import jax
import jax.numpy as jnp
from jax import lax
from jax.experimental import pallas as pl
from jax.experimental.pallas import tpu as pltpu
from jax.sharding import PartitionSpec as P

HEADS = 12
HALF_WIN = 256
DESC = 8
GRID = 4
LANES = 128
HALF = 64
SCALE = math.log2(math.e) / 8.0
BF = jnp.bfloat16
F32 = jnp.float32
I32 = jnp.int32


def iota(shape, dim):
    return lax.broadcasted_iota(I32, shape, dim)


def dot(a, b):
    return jnp.dot(a, b, preferred_element_type=F32)


def dot_t(a, b):
    return lax.dot_general(a, b, (((1,), (1,)), ((), ())), preferred_element_type=F32)


def params(mib):
    return pltpu.CompilerParams(vmem_limit_bytes=mib << 20)


def vmem():
    return pl.BlockSpec(memory_space=pltpu.VMEM)


def smem():
    return pl.BlockSpec(memory_space=pltpu.SMEM)


def cost(flops, exps, bytes_):
    return pl.CostEstimate(flops=flops, transcendentals=exps, bytes_accessed=bytes_)


def split_table(table):
    high = table >> 8
    return jnp.concatenate([high, table - (high << 8)], axis=1).astype(F32).astype(BF)


def look_up(code, table):
    n = code.shape[1]
    picks = (iota((table.shape[0], n), 0) == (code >> 7)).astype(F32).astype(BF)
    found = lax.dot_general(table, picks, (((0,), (0,)), ((), ())), preferred_element_type=F32)
    here = iota((LANES, n), 0) == (code & 127)
    value = jnp.where(here, found[:LANES] * 256.0 + found[LANES:], 0.0)
    return jnp.sum(value, axis=0, keepdims=True)


def ranks(row, count, code_dev, devices, upper):
    n = row.shape[1]
    owner = jnp.floor((row + 0.5) * (1.0 / code_dev))
    local = (row - owner * code_dev).astype(I32)
    owner = jnp.where(iota((1, n), 1) < count, owner.astype(I32), 2 * devices)
    sub = iota((devices, n), 0)
    mine = owner == sub
    starts = jnp.sum((owner < sub).astype(F32), axis=1, keepdims=True)
    before = dot(mine.astype(F32).astype(BF), upper)
    rank = jnp.sum(jnp.where(mine, starts + before, 0.0), axis=0, keepdims=True)
    return owner, local, rank.astype(I32), mine


def upper_ones(n):
    return (iota((n, n), 0) < iota((n, n), 1)).astype(F32).astype(BF)


def own_kernel(count, code_dev, devices, where_ref, code_ref, table_ref, slot_ref, pos_ref):
    n = code_ref.shape[1]
    row = look_up(code_ref[...], split_table(table_ref[...]))
    owner, local, rank, mine = ranks(row, count, code_dev, devices, upper_ones(n))
    part = rank & (GRID - 1)
    spot = rank >> 2
    live = jnp.where(part == where_ref[1], (spot + 1).astype(F32), 0.0)
    place = jnp.sum(jnp.where(mine, live, 0.0), axis=1, keepdims=True)
    width = devices * DESC
    spread = jnp.where(iota((devices, width), 0) == iota((devices, width), 1) // DESC, place, 0.0)
    spread = jnp.sum(spread, axis=0, keepdims=True).astype(I32)
    inner = iota((1, width), 1) & (DESC - 1)
    slot_ref[...] = jnp.where(spread > 0, (spread - 1) * DESC + inner, -1)
    pos_ref[...] = part * (count // GRID) + spot


def route_kernel(
    count, code_dev, devices, where_ref, codes_ref, table_ref, cache_ref, send_ref, rows, picks, picked, sems, sem
):
    docs, _, n = codes_ref.shape
    table = split_table(table_ref[...])
    upper = upper_ones(n)
    lane = iota((1, LANES), 1)
    for d in range(docs):
        row = look_up(codes_ref[d], table)
        owner, local, rank, _ = ranks(row, count, code_dev, devices, upper)
        wanted = jnp.where(owner == where_ref[0], local + 1, 0).astype(F32)
        part = rank & (GRID - 1)
        line = jnp.zeros((1, LANES), F32)
        for z in range(GRID):
            one = jnp.sum(jnp.where(part == z, wanted, 0.0), axis=1, keepdims=True)
            line = line + jnp.where(lane == z, one, 0.0)
        picks[pl.ds(d, 1), :] = jnp.maximum(line.astype(I32) - 1, 0)
    to_scalars = pltpu.make_async_copy(picks, picked, sem)
    to_scalars.start()
    to_scalars.wait()
    copies = []
    for d in range(docs):
        for z in range(GRID):
            k = d * GRID + z
            copies.append(pltpu.make_async_copy(cache_ref.at[picked[d, z]], rows.at[k], sems.at[k]))
            copies[-1].start()
    for copy in copies:
        copy.wait()
    low = iota((docs * GRID, DESC, LANES), 2) < HALF
    for p in range(HEADS // 2):
        cols = pl.ds(p * LANES, LANES)
        keys = rows[:, 0, :, cols].astype(F32)
        values = rows[:, 1, :, cols].astype(F32)
        keys_turned = pltpu.roll(keys, HALF, 2)
        values_turned = pltpu.roll(values, HALF, 2)
        for s in range(2):
            head = 2 * p + s
            group, inner = head // 3, head % 3
            key_low = keys if s == 0 else keys_turned
            key_high = keys_turned if s == 0 else keys
            value_low = values if s == 0 else values_turned
            value_high = values_turned if s == 0 else values
            if inner == 1:
                tile = jnp.where(low, value_low, key_high)
            else:
                tile = jnp.where(low, key_low, value_high)
            send_ref[:, group, :, pl.ds(inner * LANES, LANES)] = tile.astype(BF)


def compact_kernel(slot_ref, got_ref, *out_refs):
    rows = out_refs[0].shape[0]
    pick = (iota((rows, got_ref.shape[0]), 0) == slot_ref[...]).astype(F32).astype(BF)
    packed = dot(pick, got_ref[...]).astype(BF)
    for k, out in enumerate(out_refs):
        out[...] = packed[:, k * LANES : (k + 1) * LANES]


def layer_norm(values):
    centered = values - jnp.mean(values, axis=-1, keepdims=True)
    spread = jnp.mean(centered * centered, axis=-1, keepdims=True)
    return centered * lax.rsqrt(spread + 1e-05)


def window_kernel(
    low_ref, hidden_ref, high_ref, flag_ref, wq_ref, wkv_ref, wo_ref, xq_ref, middle_ref, query_ref, keys, values, queries, context, bias
):
    tok, width = hidden_ref.shape
    win = HALF_WIN
    span = 3 * win
    pairs = width // LANES
    wkv = wkv_ref[...]
    for ref, start, rows in ((low_ref, 0, win), (hidden_ref, win, tok), (high_ref, win + tok, win)):
        for r in range(0, rows, win):
            normed = layer_norm(ref[r : r + win, :].astype(F32)).astype(BF)
            keyval = dot(normed, wkv).astype(BF)
            at = start + r
            keys[at : at + win, :] = keyval[:, :width]
            for p in range(pairs):
                part = keyval[:, width + p * LANES : width + (p + 1) * LANES].astype(F32) * 2.0**-8
                values[at : at + win, 2 * p * LANES : (2 * p + 1) * LANES] = part.astype(BF)
                values[at : at + win, (2 * p + 1) * LANES : (2 * p + 2) * LANES] = jnp.ones((win, LANES), BF)
            if ref is hidden_ref:
                queries[r : r + win, :] = (dot(normed, wq_ref[...]) * SCALE).astype(BF)
    flags = jnp.concatenate(
        [low_ref[win : win + 1, :win].astype(F32), flag_ref[...], high_ref[win : win + 1, :win].astype(F32)], axis=1
    )
    gap = iota((win, span), 1) - iota((win, span), 0)
    near = (gap >= 0) & (gap <= 2 * win)
    for b in range(tok // win):
        usable = (flags[:, b * win : b * win + span] > 0.0) | (gap == win)
        bias[b] = jnp.where(near & usable, 0.0, -1e30)
    low = iota((win, LANES), 1) < HALF
    for b in range(tok // win):
        for p in range(pairs):
            cols = slice(p * LANES, (p + 1) * LANES)
            query = queries[b * win : (b + 1) * win, cols]
            key = keys[b * win : b * win + span, cols]
            value = values[b * win : b * win + span, 2 * p * LANES : (2 * p + 2) * LANES]
            both = []
            for s in range(2):
                one = jnp.where(low if s == 0 else ~low, query, jnp.zeros_like(query))
                expd = jnp.exp2(dot_t(one, key) + bias[b]).astype(BF)
                out = dot(expd, value)
                both.append(out[:, :LANES] / out[:, LANES:] * 256.0)
            context[b * win : (b + 1) * win, cols] = jnp.where(low, both[0], both[1]).astype(BF)
    valid = jnp.transpose(jnp.broadcast_to(flag_ref[...], (LANES, tok)))
    for b in range(tok // win):
        rows = slice(b * win, (b + 1) * win)
        mixed = hidden_ref[rows, :].astype(F32) + dot(context[rows, :], wo_ref[...])
        mixed = mixed.astype(BF)
        middle_ref[rows, :] = mixed
        cross = dot(layer_norm(mixed.astype(F32)).astype(BF), xq_ref[...]) * SCALE
        tiles = [cross[:, p * LANES : (p + 1) * LANES] for p in range(pairs)]
        turned = [pltpu.roll(t, HALF, 1) for t in tiles]

        def placed(head, upper):
            return (turned if (head % 2 == 1) != upper else tiles)[head // 2]

        for g in range(GRID):
            first = jnp.where(low, placed(3 * g, False), placed(3 * g + 1, True))
            second = jnp.where(low, placed(3 * g + 2, False), valid[rows, :])
            query_ref[g, rows, :LANES] = first.astype(BF)
            query_ref[g, rows, LANES:] = second.astype(BF)


def cross_kernel(inner, count, where_ref, pos_ref, query_ref, *refs):
    kv_refs, refs = refs[:GRID], refs[GRID:]
    before = refs[0] if inner else None
    refs = refs[1:] if inner else refs
    earlier = refs[0] if inner == 1 else None
    refs = refs[1:] if inner == 1 else refs
    out_ref, mass_ref, values, expds, total = refs
    keys_here = kv_refs[0].shape[0]
    step = 256
    groups, tok, _ = query_ref.shape
    value_low = inner == 1
    lane = iota((keys_here, LANES), 1)
    of_value = (lane < HALF) if value_low else (lane >= HALF)
    for c in range(GRID):
        scaled = kv_refs[c][...].astype(F32) * 2.0**-4
        values[c] = jnp.where(of_value, scaled, 1.0).astype(BF)
    if before is None:
        total[...] = jnp.zeros_like(total)
    else:
        total[...] = before[...]
    tile = LANES if inner == 2 else 0
    small = iota((step, LANES), 1)
    of_query = (small >= HALF) if value_low else (small < HALF)
    out_here = (small < HALF) if value_low else (small >= HALF)
    sum_lane = LANES - 1 if value_low else 0
    per = tok // step

    def body(i, carry):
        g = i // per
        rows = pl.ds(pl.multiple_of((i % per) * step, step), step)
        query = query_ref[g, rows, tile : tile + LANES]
        valid = query_ref[g, rows, 2 * LANES - 1 :].astype(F32)
        query = jnp.where(of_query, query, jnp.zeros_like(query))
        acc = jnp.zeros((step, LANES), F32)
        for c in range(GRID):
            expd = jnp.exp2(dot_t(query, kv_refs[c][...])).astype(BF)
            expds[c] = expd
            acc = acc + dot(expd, values[c])
        inverse = 1.0 / acc[:, sum_lane : sum_lane + 1]
        out = (acc * inverse) * 16.0
        rest = earlier[g, rows, :].astype(F32) if inner == 1 else jnp.zeros_like(out)
        out_ref[g, rows, :] = jnp.where(out_here, out, rest).astype(BF)
        share = inverse * valid
        for c in range(GRID):
            mass = jnp.sum(expds[c].astype(F32) * share, axis=0, keepdims=True)
            total[c : c + 1, :] = total[c : c + 1, :] + mass
        return carry

    lax.fori_loop(0, groups * per, body, 0)
    if inner < 2:
        mass_ref[...] = total[...]
        return
    score = jnp.zeros((8, pos_ref.shape[1]), F32)
    line = iota((8, keys_here), 0)
    for c in range(GRID):
        mass = jnp.broadcast_to(total[c : c + 1, :], (8, keys_here))
        first = mass.astype(BF).astype(F32)
        second = (mass - first).astype(BF).astype(F32)
        third = mass - first - second
        parts = jnp.where(line == 0, first, jnp.where(line == 1, second, jnp.where(line == 2, third, 0.0)))
        origin = (where_ref[1] + GRID - c) & (GRID - 1)
        at = iota((keys_here, pos_ref.shape[1]), 0) // DESC + origin * (count // GRID)
        score = score + dot(parts.astype(BF), (at == pos_ref[...]).astype(F32).astype(BF))
    mass_ref[...] = jnp.sum(score, axis=0, keepdims=True)


def final_kernel(middle_ref, first_ref, second_ref, weight_ref, out_ref):
    groups = first_ref.shape[0]
    size = 3 * HALF
    acc = middle_ref[...].astype(F32)
    for g in range(groups):
        at = g * size
        crossed = jnp.concatenate([weight_ref[at + HALF : at + 2 * HALF, :], weight_ref[at : at + HALF, :]], axis=0)
        acc = acc + dot(first_ref[g], crossed)
        acc = acc + dot(second_ref[g], weight_ref[at + HALF : at + size, :])
    out_ref[...] = acc.astype(BF)


def local(hidden, token_ids, w_query, w_keyval, w_out, x_query, x_out, shortlist, code_row, code_cache):
    doc_hidden = hidden[0]
    tok, width = doc_hidden.shape
    seq_count = lax.axis_size("seq")
    docs = lax.axis_size("doc")
    devices = docs * seq_count
    seq_index = lax.axis_index("seq")
    own = lax.axis_index("doc") * seq_count + seq_index
    where = jnp.stack([own, seq_index // GRID]).astype(I32)
    count = shortlist.shape[1]
    padded = -(-count // LANES) * LANES
    code_dev = code_cache.shape[0]
    held = count // GRID * DESC
    table = code_row.reshape(-1, LANES)

    codes = jnp.pad(shortlist, ((0, 0), (0, padded - count)), constant_values=-1)
    all_codes = lax.all_gather(codes, "doc", axis=0, tiled=False)

    flag = (token_ids != 0).astype(BF)
    rows8 = jnp.zeros((8, width), BF)
    forward = [(i, i + 1) for i in range(seq_count - 1)]
    backward = [(t, s) for s, t in forward]
    tail = jnp.concatenate([doc_hidden[tok - HALF_WIN :], rows8.at[:1, :HALF_WIN].set(flag[:, tok - HALF_WIN :])], axis=0)
    head = jnp.concatenate([doc_hidden[:HALF_WIN], rows8.at[:1, :HALF_WIN].set(flag[:, :HALF_WIN])], axis=0)
    low = lax.ppermute(tail, "seq", forward)
    high = lax.ppermute(head, "seq", backward)

    send = pl.pallas_call(
        functools.partial(route_kernel, count, code_dev, devices),
        name="route",
        out_shape=jax.ShapeDtypeStruct((docs * GRID, GRID, DESC, 3 * LANES), BF),
        in_specs=[smem(), vmem(), vmem(), pl.BlockSpec(memory_space=pl.ANY)],
        out_specs=vmem(),
        scratch_shapes=[
            pltpu.VMEM((docs * GRID, 2, DESC, width), BF),
            pltpu.VMEM((docs, LANES), I32),
            pltpu.SMEM((docs, LANES), I32),
            pltpu.SemaphoreType.DMA((docs * GRID,)),
            pltpu.SemaphoreType.DMA,
        ],
        compiler_params=params(24),
        cost_estimate=cost(10**9, 0, 2 * 10**6),
    )(where, all_codes, table, code_cache)
    got = lax.all_to_all(
        send.reshape(devices, DESC, 3 * LANES), ("doc", "seq"), split_axis=0, concat_axis=0, tiled=True
    )

    slots, pos = pl.pallas_call(
        functools.partial(own_kernel, count, code_dev, devices),
        name="own",
        out_shape=(
            jax.ShapeDtypeStruct((1, devices * DESC), I32),
            jax.ShapeDtypeStruct((1, padded), I32),
        ),
        in_specs=[smem(), vmem(), vmem()],
        out_specs=(vmem(), vmem()),
        compiler_params=params(16),
        cost_estimate=cost(10**8, 0, 2 * 10**5),
    )(where, codes, table)

    middle, queries = pl.pallas_call(
        window_kernel,
        name="window",
        out_shape=(
            jax.ShapeDtypeStruct((tok, width), BF),
            jax.ShapeDtypeStruct((GRID, tok, 2 * LANES), BF),
        ),
        in_specs=[vmem()] * 8,
        out_specs=(vmem(), vmem()),
        scratch_shapes=[
            pltpu.VMEM((tok + 2 * HALF_WIN, width), BF),
            pltpu.VMEM((tok + 2 * HALF_WIN, 2 * width), BF),
            pltpu.VMEM((tok, width), BF),
            pltpu.VMEM((tok, width), BF),
            pltpu.VMEM((tok // HALF_WIN, HALF_WIN, 3 * HALF_WIN), F32),
        ],
        compiler_params=params(48),
        cost_estimate=cost(12 * 10**9, 5 * 10**6, 10**7),
    )(low, doc_hidden, high, flag.astype(F32), w_query, w_keyval, w_out, x_query)

    lines = [[GRID * z + x for x in range(GRID)] for z in range(GRID)]

    def across(block):
        return lax.all_to_all(
            block, "seq", split_axis=0, concat_axis=0, axis_index_groups=lines, tiled=True
        )

    queries = across(queries)

    blocks = pl.pallas_call(
        compact_kernel,
        name="compact",
        out_shape=(jax.ShapeDtypeStruct((held, LANES), BF),) * 3,
        in_specs=[vmem()] * 2,
        out_specs=(vmem(),) * 3,
        compiler_params=params(24),
        cost_estimate=cost(10**9, 0, 2 * 10**6),
    )(slots, got.reshape(devices * DESC, 3 * LANES))

    gathered = []
    for block in blocks:
        parts = [block]
        for shift in range(1, GRID):
            pairs = [(i, (i + GRID * shift) % seq_count) for i in range(seq_count)]
            parts.append(lax.ppermute(block, "seq", pairs))
        gathered.append(parts)

    mass, first, second = (), None, None
    for inner in range(3):
        last = inner == 2
        extra = ((mass,) if inner else ()) + ((first,) if inner == 1 else ())
        out, mass = pl.pallas_call(
            functools.partial(cross_kernel, inner, count),
            name="cross",
            out_shape=(
                jax.ShapeDtypeStruct((GRID, tok, LANES), BF),
                jax.ShapeDtypeStruct((1, padded) if last else (8, held), F32),
            ),
            in_specs=[smem()] + [vmem()] * (2 + GRID + len(extra)),
            out_specs=(vmem(), vmem()),
            scratch_shapes=[
                pltpu.VMEM((GRID, held, LANES), BF),
                pltpu.VMEM((GRID, 256, held), BF),
                pltpu.VMEM((8, held), F32),
            ],
            compiler_params=params(32),
            cost_estimate=cost(6 * 10**9, 5 * 10**6, 4 * 10**6),
        )(where, pos, queries, *gathered[inner], *extra)
        if inner == 1:
            first = across(out)
        elif inner == 0:
            first = out
        else:
            second = across(out)

    tokens_here = jnp.sum((token_ids != 0).astype(F32), axis=1, keepdims=True)
    partial = jnp.where(jnp.arange(padded)[None, :] == count, tokens_here, mass)
    sums = jnp.sum(lax.all_gather(partial, "seq", axis=0, tiled=True), axis=0, keepdims=True)
    cand_score = count * sums[:, :count] / (HEADS * sums[:, count : count + 1])

    refined = pl.pallas_call(
        final_kernel,
        name="final",
        out_shape=jax.ShapeDtypeStruct((tok, width), BF),
        in_specs=[vmem()] * 4,
        out_specs=vmem(),
        compiler_params=params(16),
        cost_estimate=cost(10**9, 0, 4 * 10**6),
    )(middle, first, second, x_out)
    return (refined[None], cand_score)


def solution(mesh):
    return jax.shard_map(
        local,
        mesh=mesh,
        in_specs=(
            P("doc", "seq", None),
            P("doc", "seq"),
            P(),
            P(),
            P(),
            P(),
            P(),
            P("doc", None),
            P(),
            P(("doc", "seq"), None, None, None),
        ),
        out_specs=(P("doc", "seq", None), P("doc", None)),
        check_vma=False,
    )
```

time: 589 us -> 160 us (0.27); the launches traced: 577 us -> 158 us
  blocking collectives: 241 us -> 33.1 us
  local copies, waits for them, and re-layouts: 157 us -> 9.02 us
  matrix products: 109 us -> 0 us
  Pallas kernels: 0 us -> 62.1 us
  other arithmetic: 54.9 us -> 4.18 us
  starting transfers between devices: 12.9 us -> 44.8 us
    psum x2 -> x0, blocking collectives: 221 us -> none  [the longest x1 182 us: local(): length = lax.psum(local_count, 'seq')]
    dot_general x17 -> x0, matrix products: 109 us -> none  [the longest x6 49.9 us: head_group(): jnp.einsum('qhd,khd->hqk', query_heads, key_heads, preferred_element_type...]
    pallas_call x0 -> x8, Pallas kernels: none -> 62.1 us  [the longest x3 36.6 us: local(): pl.pallas_call(functools.partial(cross_kernel, inner, count), name='cross...]
    reduce_sum x10 -> x2, other arithmetic: 46.3 us -> 0.64 us  [the longest x1 0.6 us: local(): tokens_here = jnp.sum((token_ids != 0).astype(F32), axis=1, keepdims=True)]
    another operation x7 -> x0, local copies, waits for them, and re-layouts: 36.6 us -> none  [the longest x1 17.3 us: attend(): value_rows.reshape(key_count, group_count, per_group * head_size)]
    all_gather x0 -> x2, blocking collectives: none -> 33.1 us  [the longest x1 21.1 us: local(): lax.all_gather(partial, 'seq', axis=0, tiled=True)]
    scatter x3 -> x0, local copies, waits for them, and re-layouts: 30.9 us -> none  [the longest x2 15.8 us: local(): jnp.zeros((devices, capacity), jnp.bool_).at[owner_dev, slot_rank].set(True)]
    gather x3 -> x0, local copies, waits for them, and re-layouts: 24.1 us -> none  [the longest x1 18.1 us: local(): code_cache[lax.all_to_all(request, ('doc', 'seq'), split_axis=0, concat_a...]
  transfers between devices with their start and end apart: 3 -> 15, of which waited for: 0 -> 2; matrix products, arithmetic and copies ran while one was open for 10% -> 2% of each run, Pallas kernels for 0% -> 38%
where the time goes in v1:
time: 160 us; the launch traced here: 158 us
  Pallas kernels  62.1 us (39%)
  starting transfers between devices  44.8 us (28%)
  blocking collectives  33.1 us (21%)
  local copies, waits for them, and re-layouts  9.02 us (6%)
  other arithmetic  4.18 us (3%)
  waiting for transfers between devices  3.31 us (2%)
    pallas_call x3, Pallas kernels, local(): pl.pallas_call(functools.partial(cross_kernel, inner, count), name='cross...  36.6 us
    all_gather x1, blocking collectives, local(): lax.all_gather(partial, 'seq', axis=0, tiled=True)  21.1 us
    ppermute x9, starting transfers between devices, local(): parts.append(lax.ppermute(block, 'seq', pairs))  15 us
    all_to_all x3, starting transfers between devices, across(): lax.all_to_all(block, 'seq', split_axis=0, concat_axis=0, axis_index_grou...  14.5 us
    pallas_call x1, Pallas kernels, local(): pl.pallas_call(window_kernel, name='window', out_shape=(jax.ShapeDtypeStr...  13.9 us
    all_gather x1, blocking collectives, local(): all_codes = lax.all_gather(codes, 'doc', axis=0, tiled=False)  12 us
    all_to_all x1, starting transfers between devices, local(): lax.all_to_all(send.reshape(devices, DESC, 3 * LANES), ('doc', 'seq'), sp...  9.38 us
    unnamed x23, local copies, waits for them, and re-layouts  7.25 us
  transfers between devices with their start and end apart: 15, of which 2 were waited for; matrix products, arithmetic and copies ran while one was open for 2% of the time, Pallas kernels for 38%

profile of v1, /device:TPU:2, one launch (start us, length us, event | category | flops | bytes accessed | tf_op | source)
XLA Modules:
  0.0 157.9 jit_solution(11972049219139764504)
XLA Ops:
  0.6 0.7 fusion.7
  1.3 1.2 slice_bitcast_fusion
  2.5 0.0 copy-start.10
  2.5 0.0 copy-start.6
  2.5 0.8 fusion.2
  3.3 3.4 %collective-permute-start = (bf16[264,768]{1,0:T(8,128)(2,1)}, bf16[264,768]{1,0:T(8,128)(2,1)S(1)}, u32[]{:S(2)}, u32[]{:S(2)}) collective-permute-start(bf16[264,768]{1,0:T(8,128)(2,1)} %fusion.2), channel_id=1, source_target_pairs={{0,1},{1,2},{2,3},{3,4},{4,5},{5,6},{6,7},{7,8},{8,9},{9,10},{10,1... | collective-permute-start | bytes 1216520 | tf_op jit(solution)/shard_map/ppermute | solution.py:325
  6.7 0.8 fusion.3
  7.5 2.5 %collective-permute-start.1 = (bf16[264,768]{1,0:T(8,128)(2,1)}, bf16[264,768]{1,0:T(8,128)(2,1)S(1)}, u32[]{:S(2)}, u32[]{:S(2)}) collective-permute-start(bf16[264,768]{1,0:T(8,128)(2,1)} %fusion.3), channel_id=1, source_target_pairs={{1,0},{2,1},{3,2},{4,3},{5,4},{6,5},{7,6},{8,7},{9,8},{10,9},{11,1... | collective-permute-start | bytes 1216520 | tf_op jit(solution)/shard_map/ppermute | solution.py:326
  9.9 0.0 copy-done.10
  10.0 12.0 %all-gather.1.codes_ref = s32[8,1,384]{2,1,0:T(1,128)S(1)} all-gather(s32[1,1,384]{2,1,0:T(1,128)S(1)} %get-tuple-element.58), channel_id=2, replica_groups=mesh['doc'=8,'seq'=16] {'doc'}, dimensions={0}, use_global_device_ids=true | all-gather | bytes 13824 | tf_op jit(solution)/shard_map/all_gather | solution.py:317
  22.0 0.1 pad_add_fusion.where_ref
  22.0 0.0 copy-done.6
  22.0 3.0 %copy-done = bf16[288,2,8,768]{3,2,1,0:T(8,128)(2,1)S(1)} copy-done((bf16[288,2,8,768]{3,2,1,0:T(8,128)(2,1)S(1)}, bf16[288,2,8,768]{3,2,1,0:T(8,128)(2,1)}, u32[]{:S(2)}) %copy-start) | copy-done | bytes 7077912
  25.0 6.9 %route.1 = bf16[32,4,8,384]{3,2,1,0:T(8,128)(2,1)} custom-call(s32[2]{0:T(128)S(1)} %pad_add_fusion.where_ref, s32[8,1,384]{2,1,0:T(1,128)S(1)} %all-gather.1.codes_ref, s32[288,128]{1,0:T(8,128)S(1)} %bitcast.18, bf16[288,2,8,768]{3,2,1,0:T(8,128)(2,1)S(1)} %copy-done), custom_call_target="tpu_custom_call" | custom-call | flops 1000000000 | bytes 2000000 | tf_op jit(solution)/shard_map/route/pallas_call | solution.py:328
  31.9 0.0 copy-start.2
  31.9 9.4 %all-to-all-start.1 = ((bf16[128,8,384]{2,1,0:T(8,128)(2,1)}), bf16[128,8,384]{2,1,0:T(8,128)(2,1)S(1)}, u32[]{:S(2)}, u32[]{:S(2)}) async-start(bf16[128,8,384]{2,1,0:T(8,128)(2,1)} %bitcast.7), calls=%async_computation.1 | async-start | bytes 1572864 | tf_op jit(solution)/shard_map/all_to_all | solution.py:344
  41.3 0.0 collective-permute-done.low_ref
  41.3 0.0 collective-permute-done.1.high_ref
  41.3 0.0 copy-done.2
  41.4 0.0 copy-start.7
  41.4 1.3 copy-done.7
  42.6 1.3 copy-done.8
  43.9 13.9 %window.1 = (bf16[512,768]{1,0:T(8,128)(2,1)S(1)}, bf16[4,512,256]{2,1,0:T(8,128)(2,1)}) custom-call(bf16[264,768]{1,0:T(8,128)(2,1)S(1)} %collective-permute-done.low_ref, bf16[512,768]{1,0:T(8,128)(2,1)S(1)} %bitcast.16, bf16[264,768]{1,0:T(8,128)(2,1)S(1)} %collective-permute-done.1.high_ref, f32[1,512]{1,0:T(1,128)S(1)} %get-tuple-element.54.flag_ref, ...), custom_call_target="tpu_custom_call" | custom-call | flops 12000000000 | bytes 10000000 | tf_op jit(solution)/shard_map/window/pallas_call | solution.py:361
  57.8 0.9 copy-done.3
  58.7 0.0 all-to-all-done.1
  58.7 4.8 %all-to-all-start = ((bf16[4,512,256]{2,1,0:T(8,128)(2,1)}), bf16[4,512,256]{2,1,0:T(8,128)(2,1)S(1)}, u32[]{:S(2)}, u32[]{:S(2)}) async-start(bf16[4,512,256]{2,1,0:T(8,128)(2,1)} %get-tuple-element.41), calls=%async_computation | async-start | bytes 2097152 | tf_op jit(solution)/shard_map/all_to_all | solution.py:384
  63.5 1.2 own.1
  64.7 0.0 copy-start.9
  64.7 0.8 compact.1
  65.6 1.9 %collective-permute-start.5 = (bf16[640,128]{1,0:T(8,128)(2,1)S(1)}, bf16[640,128]{1,0:T(8,128)(2,1)S(1)}, u32[]{:S(2)}, u32[]{:S(2)}) collective-permute-start(bf16[640,128]{1,0:T(8,128)(2,1)S(1)} %get-tuple-element.44.refs_0_), channel_id=1, source_target_pairs={{0,4},{1,5},{2,6},{3,7},{4,8},{5,9},{6,10},{7,11},{8,12},{9,13},{1... | collective-permute-start | bytes 491528 | tf_op jit(solution)/shard_map/ppermute | solution.py:405
  67.5 3.2 %collective-permute-start.6 = (bf16[640,128]{1,0:T(8,128)(2,1)S(1)}, bf16[640,128]{1,0:T(8,128)(2,1)S(1)}, u32[]{:S(2)}, u32[]{:S(2)}) collective-permute-start(bf16[640,128]{1,0:T(8,128)(2,1)S(1)} %get-tuple-element.44.refs_0_), channel_id=1, source_target_pairs={{0,8},{1,9},{2,10},{3,11},{4,12},{5,13},{6,14},{7,15},{8,0},{9,1},... | collective-permute-start | bytes 491528 | tf_op jit(solution)/shard_map/ppermute | solution.py:405
  70.7 1.2 collective-permute-start.7
  71.9 0.0 copy-done.9
  71.9 0.6 fusion.4
  72.5 0.8 collective-permute-start.2
  73.3 0.6 collective-permute-start.3
  74.0 0.0 collective-permute-done.5.refs_1_
  74.0 2.4 %collective-permute-start.4 = (bf16[640,128]{1,0:T(8,128)(2,1)S(1)}, bf16[640,128]{1,0:T(8,128)(2,1)S(1)}, u32[]{:S(2)}, u32[]{:S(2)}) collective-permute-start(bf16[640,128]{1,0:T(8,128)(2,1)S(1)} %get-tuple-element.43.refs_0_), channel_id=1, source_target_pairs={{0,12},{1,13},{2,14},{3,15},{4,0},{5,1},{6,2},{7,3},{8,4},{9,5},{1... | collective-permute-start | bytes 491528 | tf_op jit(solution)/shard_map/ppermute | solution.py:405
  76.4 2.9 %collective-permute-done.6.refs_2_ = bf16[640,128]{1,0:T(8,128)(2,1)S(1)} collective-permute-done((bf16[640,128]{1,0:T(8,128)(2,1)S(1)}, bf16[640,128]{1,0:T(8,128)(2,1)S(1)}, u32[]{:S(2)}, u32[]{:S(2)}) %collective-permute-start.6) | collective-permute-done | bytes 163872 | tf_op jit(solution)/shard_map/ppermute | solution.py:405
  79.3 0.0 collective-permute-start.8
  79.3 0.3 collective-permute-done.7.refs_3_
  79.6 2.4 %collective-permute-start.9 = (bf16[640,128]{1,0:T(8,128)(2,1)S(1)}, bf16[640,128]{1,0:T(8,128)(2,1)S(1)}, u32[]{:S(2)}, u32[]{:S(2)}) collective-permute-start(bf16[640,128]{1,0:T(8,128)(2,1)S(1)} %get-tuple-element.48.refs_0_), channel_id=1, source_target_pairs={{0,8},{1,9},{2,10},{3,11},{4,12},{5,13},{6,14},{7,15},{8,0},{9,1},... | collective-permute-start | bytes 491528 | tf_op jit(solution)/shard_map/ppermute | solution.py:405
  82.0 0.0 all-to-all-done.query_ref
  82.0 11.8 %cross.3 = (bf16[4,512,128]{2,1,0:T(8,128)(2,1)S(1)}, f32[8,640]{1,0:T(8,128)S(1)}) custom-call(s32[2]{0:T(128)S(1)} %pad_add_fusion.where_ref, s32[1,384]{1,0:T(1,128)S(1)} %get-tuple-element.40.pos_ref, bf16[4,512,256]{2,1,0:T(8,128)(2,1)S(1)} %all-to-all-done.query_ref, bf16[640,128]{1,0:T(8,128)(2,1)S(1)} %get-tuple-element.44.refs_0_, ...), custom_call_target="tpu_custom_call" | custom-call | flops 6000000000 | bytes 4000000 | tf_op jit(solution)/shard_map/cross/pallas_call | solution.py:412
  93.8 0.0 collective-permute-done.2.refs_1_
  93.8 2.5 %collective-permute-start.10 = (bf16[640,128]{1,0:T(8,128)(2,1)S(1)}, bf16[640,128]{1,0:T(8,128)(2,1)S(1)}, u32[]{:S(2)}, u32[]{:S(2)}) collective-permute-start(bf16[640,128]{1,0:T(8,128)(2,1)S(1)} %get-tuple-element.48.refs_0_), channel_id=1, source_target_pairs={{0,12},{1,13},{2,14},{3,15},{4,0},{5,1},{6,2},{7,3},{8,4},{9,5},{1... | collective-permute-start | bytes 491528 | tf_op jit(solution)/shard_map/ppermute | solution.py:405
  96.3 0.0 collective-permute-done.3.refs_2_
  96.3 0.0 collective-permute-done.4.refs_3_
  96.3 12.6 %cross.4 = (bf16[4,512,128]{2,1,0:T(8,128)(2,1)}, f32[8,640]{1,0:T(8,128)S(1)}) custom-call(s32[2]{0:T(128)S(1)} %pad_add_fusion.where_ref, s32[1,384]{1,0:T(1,128)S(1)} %get-tuple-element.40.pos_ref, bf16[4,512,256]{2,1,0:T(8,128)(2,1)S(1)} %all-to-all-done.query_ref, bf16[640,128]{1,0:T(8,128)(2,1)S(1)} %get-tuple-element.43.refs_0_, ...), custom_call_target="tpu_custom_call" | custom-call | flops 6000000000 | bytes 4000000 | tf_op jit(solution)/shard_map/cross/pallas_call | solution.py:412
  108.9 4.8 %all-to-all-start.2 = ((bf16[4,512,128]{2,1,0:T(8,128)(2,1)}), bf16[4,512,128]{2,1,0:T(8,128)(2,1)S(1)}, u32[]{:S(2)}, u32[]{:S(2)}) async-start(bf16[4,512,128]{2,1,0:T(8,128)(2,1)} %get-tuple-element.47), calls=%async_computation.2 | async-start | bytes 1048576 | tf_op jit(solution)/shard_map/all_to_all | solution.py:384
  113.7 0.0 collective-permute-done.8.refs_1_
  113.7 0.0 collective-permute-done.9.refs_2_
  113.7 0.0 collective-permute-done.10.refs_3_
  113.7 0.0 copy-start.1
  113.7 12.2 %cross.5 = (bf16[4,512,128]{2,1,0:T(8,128)(2,1)S(1)}, f32[1,384]{1,0:T(1,128)S(1)}) custom-call(s32[2]{0:T(128)S(1)} %pad_add_fusion.where_ref, s32[1,384]{1,0:T(1,128)S(1)} %get-tuple-element.40.pos_ref, bf16[4,512,256]{2,1,0:T(8,128)(2,1)S(1)} %all-to-all-done.query_ref, bf16[640,128]{1,0:T(8,128)(2,1)S(1)} %get-tuple-element.48.refs_0_, ...), custom_call_target="tpu_custom_call" | custom-call | flops 6000000000 | bytes 4000000 | tf_op jit(solution)/shard_map/cross/pallas_call | solution.py:412
  125.9 0.8 copy-done.5
  126.7 0.0 all-to-all-done.2.first_ref
  126.7 4.9 %all-to-all-start.3 = ((bf16[4,512,128]{2,1,0:T(8,128)(2,1)}), bf16[4,512,128]{2,1,0:T(8,128)(2,1)S(1)}, u32[]{:S(2)}, u32[]{:S(2)}) async-start(bf16[4,512,128]{2,1,0:T(8,128)(2,1)} %copy-done.5), calls=%async_computation.3 | async-start | bytes 1048576 | tf_op jit(solution)/shard_map/all_to_all | solution.py:384
  131.7 0.6 fusion.5
  132.3 21.1 %all-gather.2 = f32[16,1,384]{2,1,0:T(1,128)S(1)} all-gather(f32[1,1,384]{2,1,0:T(1,128)S(1)} %fusion.5), channel_id=1, replica_groups=mesh['doc'=8,'seq'=16] {'seq'}, dimensions={0}, use_global_device_ids=true | all-gather | bytes 26112 | tf_op jit(solution)/shard_map/all_gather | solution.py:438
  153.5 0.6 slice.75
  154.7 0.6 fusion.6
  155.3 0.0 all-to-all-done.3.second_ref
  155.3 2.7 %final.1 = bf16[512,768]{1,0:T(8,128)(2,1)} custom-call(bf16[512,768]{1,0:T(8,128)(2,1)S(1)} %copy-done.4, bf16[4,512,128]{2,1,0:T(8,128)(2,1)S(1)} %all-to-all-done.2.first_ref, bf16[4,512,128]{2,1,0:T(8,128)(2,1)S(1)} %all-to-all-done.3.second_ref, bf16[768,768]{1,0:T(8,128)(2,1)S(1)} %copy-done.1), custom_call_target="tpu_custom_call" | custom-call | flops 1000000000 | bytes 4000000 | tf_op jit(solution)/shard_map/final/pallas_call | solution.py:441
  (11 shorter events, 0.1 us)
Async XLA Ops:
  2.5 7.4 %copy-start.10 = (s32[1,320]{1,0:T(1,128)S(1)}, s32[1,320]{1,0:T(1,128)}, u32[]{:S(2)}) copy-start(s32[1,320]{1,0:T(1,128)} %param.21) | copy-start | bytes 3844
  2.5 19.5 %copy-start.6 = (s32[36864]{0:T(1024)S(1)}, s32[36864]{0:T(1024)}, u32[]{:S(2)}) copy-start(s32[36864]{0:T(1024)} %param.22) | copy-start | bytes 442372
  3.3 38.0 %collective-permute-start = (bf16[264,768]{1,0:T(8,128)(2,1)}, bf16[264,768]{1,0:T(8,128)(2,1)S(1)}, u32[]{:S(2)}, u32[]{:S(2)}) collective-permute-start(bf16[264,768]{1,0:T(8,128)(2,1)} %fusion.2), channel_id=1, source_target_pairs={{0,1},{1,2},{2,3},{3,4},{4,5},{5,6},{6,7},{7,8},{8,9},{9,10},{10,1... | collective-permute-start | bytes 1216520 | tf_op jit(solution)/shard_map/ppermute | solution.py:325
  7.5 33.9 %collective-permute-start.1 = (bf16[264,768]{1,0:T(8,128)(2,1)}, bf16[264,768]{1,0:T(8,128)(2,1)S(1)}, u32[]{:S(2)}, u32[]{:S(2)}) collective-permute-start(bf16[264,768]{1,0:T(8,128)(2,1)} %fusion.3), channel_id=1, source_target_pairs={{1,0},{2,1},{3,2},{4,3},{5,4},{6,5},{7,6},{8,7},{9,8},{10,9},{11,1... | collective-permute-start | bytes 1216520 | tf_op jit(solution)/shard_map/ppermute | solution.py:326
  22.0 3.0 %copy-start = (bf16[288,2,8,768]{3,2,1,0:T(8,128)(2,1)S(1)}, bf16[288,2,8,768]{3,2,1,0:T(8,128)(2,1)}, u32[]{:S(2)}) copy-start(bf16[288,2,8,768]{3,2,1,0:T(8,128)(2,1)} %cache_ref.1) | copy-start | bytes 21233668
  31.9 9.4 %copy-start.2 = (bf16[1,512,768]{2,1,0:T(8,128)(2,1)S(1)}, bf16[1,512,768]{2,1,0:T(8,128)(2,1)}, u32[]{:S(2)}) copy-start(bf16[1,512,768]{2,1,0:T(8,128)(2,1)} %param.14) | copy-start | bytes 2359300
  31.9 26.8 %all-to-all-start.1 = ((bf16[128,8,384]{2,1,0:T(8,128)(2,1)}), bf16[128,8,384]{2,1,0:T(8,128)(2,1)S(1)}, u32[]{:S(2)}, u32[]{:S(2)}) async-start(bf16[128,8,384]{2,1,0:T(8,128)(2,1)} %bitcast.7), calls=%async_computation.1 | async-start | bytes 1572864 | tf_op jit(solution)/shard_map/all_to_all | solution.py:344
  41.4 1.3 copy-start.7
  42.6 1.3 copy-start.8
  57.8 0.9 copy-start.3
  58.7 23.3 %all-to-all-start = ((bf16[4,512,256]{2,1,0:T(8,128)(2,1)}), bf16[4,512,256]{2,1,0:T(8,128)(2,1)S(1)}, u32[]{:S(2)}, u32[]{:S(2)}) async-start(bf16[4,512,256]{2,1,0:T(8,128)(2,1)} %get-tuple-element.41), calls=%async_computation | async-start | bytes 2097152 | tf_op jit(solution)/shard_map/all_to_all | solution.py:384
  64.7 7.2 %copy-start.9 = (s32[1,512]{1,0:T(1,128)S(1)}, s32[1,512]{1,0:T(1,128)}, u32[]{:S(2)}) copy-start(s32[1,512]{1,0:T(1,128)} %param.15) | copy-start | bytes 6148
  65.6 8.4 %collective-permute-start.5 = (bf16[640,128]{1,0:T(8,128)(2,1)S(1)}, bf16[640,128]{1,0:T(8,128)(2,1)S(1)}, u32[]{:S(2)}, u32[]{:S(2)}) collective-permute-start(bf16[640,128]{1,0:T(8,128)(2,1)S(1)} %get-tuple-element.44.refs_0_), channel_id=1, source_target_pairs={{0,4},{1,5},{2,6},{3,7},{4,8},{5,9},{6,10},{7,11},{8,12},{9,13},{1... | collective-permute-start | bytes 491528 | tf_op jit(solution)/shard_map/ppermute | solution.py:405
  67.5 11.8 %collective-permute-start.6 = (bf16[640,128]{1,0:T(8,128)(2,1)S(1)}, bf16[640,128]{1,0:T(8,128)(2,1)S(1)}, u32[]{:S(2)}, u32[]{:S(2)}) collective-permute-start(bf16[640,128]{1,0:T(8,128)(2,1)S(1)} %get-tuple-element.44.refs_0_), channel_id=1, source_target_pairs={{0,8},{1,9},{2,10},{3,11},{4,12},{5,13},{6,14},{7,15},{8,0},{9,1},... | collective-permute-start | bytes 491528 | tf_op jit(solution)/shard_map/ppermute | solution.py:405
  70.7 8.9 %collective-permute-start.7 = (bf16[640,128]{1,0:T(8,128)(2,1)S(1)}, bf16[640,128]{1,0:T(8,128)(2,1)S(1)}, u32[]{:S(2)}, u32[]{:S(2)}) collective-permute-start(bf16[640,128]{1,0:T(8,128)(2,1)S(1)} %get-tuple-element.44.refs_0_), channel_id=1, source_target_pairs={{0,12},{1,13},{2,14},{3,15},{4,0},{5,1},{6,2},{7,3},{8,4},{9,5},{1... | collective-permute-start | bytes 491528 | tf_op jit(solution)/shard_map/ppermute | solution.py:405
  72.5 21.3 %collective-permute-start.2 = (bf16[640,128]{1,0:T(8,128)(2,1)S(1)}, bf16[640,128]{1,0:T(8,128)(2,1)S(1)}, u32[]{:S(2)}, u32[]{:S(2)}) collective-permute-start(bf16[640,128]{1,0:T(8,128)(2,1)S(1)} %get-tuple-element.43.refs_0_), channel_id=1, source_target_pairs={{0,4},{1,5},{2,6},{3,7},{4,8},{5,9},{6,10},{7,11},{8,12},{9,13},{1... | collective-permute-start | bytes 491528 | tf_op jit(solution)/shard_map/ppermute | solution.py:405
  73.3 22.9 %collective-permute-start.3 = (bf16[640,128]{1,0:T(8,128)(2,1)S(1)}, bf16[640,128]{1,0:T(8,128)(2,1)S(1)}, u32[]{:S(2)}, u32[]{:S(2)}) collective-permute-start(bf16[640,128]{1,0:T(8,128)(2,1)S(1)} %get-tuple-element.43.refs_0_), channel_id=1, source_target_pairs={{0,8},{1,9},{2,10},{3,11},{4,12},{5,13},{6,14},{7,15},{8,0},{9,1},... | collective-permute-start | bytes 491528 | tf_op jit(solution)/shard_map/ppermute | solution.py:405
  74.0 22.3 %collective-permute-start.4 = (bf16[640,128]{1,0:T(8,128)(2,1)S(1)}, bf16[640,128]{1,0:T(8,128)(2,1)S(1)}, u32[]{:S(2)}, u32[]{:S(2)}) collective-permute-start(bf16[640,128]{1,0:T(8,128)(2,1)S(1)} %get-tuple-element.43.refs_0_), channel_id=1, source_target_pairs={{0,12},{1,13},{2,14},{3,15},{4,0},{5,1},{6,2},{7,3},{8,4},{9,5},{1... | collective-permute-start | bytes 491528 | tf_op jit(solution)/shard_map/ppermute | solution.py:405
  79.3 34.4 %collective-permute-start.8 = (bf16[640,128]{1,0:T(8,128)(2,1)S(1)}, bf16[640,128]{1,0:T(8,128)(2,1)S(1)}, u32[]{:S(2)}, u32[]{:S(2)}) collective-permute-start(bf16[640,128]{1,0:T(8,128)(2,1)S(1)} %get-tuple-element.48.refs_0_), channel_id=1, source_target_pairs={{0,4},{1,5},{2,6},{3,7},{4,8},{5,9},{6,10},{7,11},{8,12},{9,13},{1... | collective-permute-start | bytes 491528 | tf_op jit(solution)/shard_map/ppermute | solution.py:405
  79.6 34.1 %collective-permute-start.9 = (bf16[640,128]{1,0:T(8,128)(2,1)S(1)}, bf16[640,128]{1,0:T(8,128)(2,1)S(1)}, u32[]{:S(2)}, u32[]{:S(2)}) collective-permute-start(bf16[640,128]{1,0:T(8,128)(2,1)S(1)} %get-tuple-element.48.refs_0_), channel_id=1, source_target_pairs={{0,8},{1,9},{2,10},{3,11},{4,12},{5,13},{6,14},{7,15},{8,0},{9,1},... | collective-permute-start | bytes 491528 | tf_op jit(solution)/shard_map/ppermute | solution.py:405
  93.8 19.9 %collective-permute-start.10 = (bf16[640,128]{1,0:T(8,128)(2,1)S(1)}, bf16[640,128]{1,0:T(8,128)(2,1)S(1)}, u32[]{:S(2)}, u32[]{:S(2)}) collective-permute-start(bf16[640,128]{1,0:T(8,128)(2,1)S(1)} %get-tuple-element.48.refs_0_), channel_id=1, source_target_pairs={{0,12},{1,13},{2,14},{3,15},{4,0},{5,1},{6,2},{7,3},{8,4},{9,5},{1... | collective-permute-start | bytes 491528 | tf_op jit(solution)/shard_map/ppermute | solution.py:405
  108.9 17.8 %all-to-all-start.2 = ((bf16[4,512,128]{2,1,0:T(8,128)(2,1)}), bf16[4,512,128]{2,1,0:T(8,128)(2,1)S(1)}, u32[]{:S(2)}, u32[]{:S(2)}) async-start(bf16[4,512,128]{2,1,0:T(8,128)(2,1)} %get-tuple-element.47), calls=%async_computation.2 | async-start | bytes 1048576 | tf_op jit(solution)/shard_map/all_to_all | solution.py:384
  113.7 41.6 %copy-start.1 = (bf16[768,768]{1,0:T(8,128)(2,1)S(1)}, bf16[768,768]{1,0:T(8,128)(2,1)}, u32[]{:S(2)}) copy-start(bf16[768,768]{1,0:T(8,128)(2,1)} %weight_ref.1) | copy-start | bytes 3538948
  125.9 0.8 copy-start.5
  126.7 28.6 %copy-start.4 = (bf16[512,768]{1,0:T(8,128)(2,1)S(1)}, bf16[512,768]{1,0:T(8,128)(2,1)}, u32[]{:S(2)}) copy-start(bf16[512,768]{1,0:T(8,128)(2,1)} %copy-done.3) | copy-start | bytes 2359300
  126.7 28.5 %all-to-all-start.3 = ((bf16[4,512,128]{2,1,0:T(8,128)(2,1)}), bf16[4,512,128]{2,1,0:T(8,128)(2,1)S(1)}, u32[]{:S(2)}, u32[]{:S(2)}) async-start(bf16[4,512,128]{2,1,0:T(8,128)(2,1)} %copy-done.5), calls=%async_computation.3 | async-start | bytes 1048576 | tf_op jit(solution)/shard_map/all_to_all | solution.py:384

commit v2 on v1

v2 whole, which is shorter than its diff:
```python
import functools
import math

import jax
import jax.numpy as jnp
from jax import lax
from jax.experimental import pallas as pl
from jax.experimental.pallas import tpu as pltpu
from jax.sharding import PartitionSpec as P

HEADS = 12
HALF_WIN = 256
DESC = 8
GRID = 4
LANES = 128
HALF = 64
SCALE = math.log2(math.e) / 8.0
BF = jnp.bfloat16
F32 = jnp.float32
I32 = jnp.int32


def iota(shape, dim):
    return lax.broadcasted_iota(I32, shape, dim)


def dot(a, b):
    return jnp.dot(a, b, preferred_element_type=F32)


def dot_t(a, b):
    return lax.dot_general(a, b, (((1,), (1,)), ((), ())), preferred_element_type=F32)


def params(mib):
    return pltpu.CompilerParams(vmem_limit_bytes=mib << 20)


def vmem():
    return pl.BlockSpec(memory_space=pltpu.VMEM)


def smem():
    return pl.BlockSpec(memory_space=pltpu.SMEM)


def cost(flops, exps, bytes_):
    return pl.CostEstimate(flops=flops, transcendentals=exps, bytes_accessed=bytes_)


def split_table(table):
    high = table >> 8
    return jnp.concatenate([high, table - (high << 8)], axis=1).astype(F32).astype(BF)


def look_up(code, table):
    n = code.shape[1]
    picks = (iota((table.shape[0], n), 0) == (code >> 7)).astype(F32).astype(BF)
    found = lax.dot_general(table, picks, (((0,), (0,)), ((), ())), preferred_element_type=F32)
    here = iota((LANES, n), 0) == (code & 127)
    value = jnp.where(here, found[:LANES] * 256.0 + found[LANES:], 0.0)
    return jnp.sum(value, axis=0, keepdims=True)


def ranks(row, count, code_dev, devices, upper):
    n = row.shape[1]
    owner = jnp.floor((row + 0.5) * (1.0 / code_dev))
    local = (row - owner * code_dev).astype(I32)
    owner = jnp.where(iota((1, n), 1) < count, owner.astype(I32), 2 * devices)
    sub = iota((devices, n), 0)
    mine = owner == sub
    starts = jnp.sum((owner < sub).astype(F32), axis=1, keepdims=True)
    before = dot(mine.astype(F32).astype(BF), upper)
    rank = jnp.sum(jnp.where(mine, starts + before, 0.0), axis=0, keepdims=True)
    return owner, local, rank.astype(I32)


def upper_ones(n):
    return (iota((n, n), 0) < iota((n, n), 1)).astype(F32).astype(BF)


def route_kernel(
    count, code_dev, devices, where_ref, codes_ref, table_ref, cache_ref, send_ref, slot_ref, pos_ref, table, rows, line, picks, picked, sems, sem
):
    docs = codes_ref.shape[0]
    n = line.shape[1]
    fetch = pltpu.make_async_copy(table_ref, table, sem.at[0])
    fetch.start()
    upper = upper_ones(n)
    lane = iota((1, LANES), 1)
    line[...] = jnp.full(line.shape, -1, I32)
    for d in range(docs):
        line[d : d + 1, :count] = codes_ref[d]
    fetch.wait()
    planes = split_table(table[...])
    doc = where_ref[2]
    owner_here = jnp.zeros((1, n), I32)
    rank_here = jnp.zeros((1, n), I32)
    for d in range(docs):
        row = look_up(line[d : d + 1, :], planes)
        owner, local, rank = ranks(row, count, code_dev, devices, upper)
        wanted = jnp.where(owner == where_ref[0], local + 1, 0).astype(F32)
        part = rank & (GRID - 1)
        found = jnp.zeros((1, LANES), F32)
        for z in range(GRID):
            one = jnp.sum(jnp.where(part == z, wanted, 0.0), axis=1, keepdims=True)
            found = found + jnp.where(lane == z, one, 0.0)
        picks[d : d + 1, :] = jnp.maximum(found.astype(I32) - 1, 0)
        owner_here = jnp.where(doc == d, owner, owner_here)
        rank_here = jnp.where(doc == d, rank, rank_here)
    to_scalars = pltpu.make_async_copy(picks, picked, sem.at[1])
    to_scalars.start()
    to_scalars.wait()
    copies = []
    for d in range(docs):
        for z in range(GRID):
            k = d * GRID + z
            copies.append(pltpu.make_async_copy(cache_ref.at[picked[d, z]], rows.at[k], sems.at[k]))
            copies[-1].start()

    part = rank_here & (GRID - 1)
    spot = rank_here >> 2
    live = jnp.where(part == where_ref[1], (spot + 1).astype(F32), 0.0)
    mine = owner_here == iota((devices, n), 0)
    place = jnp.sum(jnp.where(mine, live, 0.0), axis=1, keepdims=True)
    width = devices * DESC
    spread = jnp.where(iota((devices, width), 0) == iota((devices, width), 1) // DESC, place, 0.0)
    spread = jnp.sum(spread, axis=0, keepdims=True).astype(I32)
    inside = iota((1, width), 1) & (DESC - 1)
    slot_ref[...] = jnp.where(spread > 0, (spread - 1) * DESC + inside, -1)
    pos_ref[...] = part * (count // GRID) + spot

    low = iota((GRID, DESC, LANES), 2) < HALF
    for d in range(docs):
        for copy in copies[d * GRID : (d + 1) * GRID]:
            copy.wait()
        block = pl.ds(d * GRID, GRID)
        for p in range(HEADS // 2):
            cols = pl.ds(p * LANES, LANES)
            keys = rows[block, 0, :, cols].astype(F32)
            values = rows[block, 1, :, cols].astype(F32)
            keys_turned = pltpu.roll(keys, HALF, 2)
            values_turned = pltpu.roll(values, HALF, 2)
            for s in range(2):
                head = 2 * p + s
                group, inner = head // 3, head % 3
                key_low = keys if s == 0 else keys_turned
                key_high = keys_turned if s == 0 else keys
                value_low = values if s == 0 else values_turned
                value_high = values_turned if s == 0 else values
                if inner == 1:
                    tile = jnp.where(low, value_low, key_high)
                else:
                    tile = jnp.where(low, key_low, value_high)
                send_ref[block, group, :, pl.ds(inner * LANES, LANES)] = tile.astype(BF)


def compact_kernel(slot_ref, got_ref, first_ref, rest_ref):
    rows = first_ref.shape[0]
    pick = (iota((rows, got_ref.shape[0]), 0) == slot_ref[...]).astype(F32).astype(BF)
    packed = dot(pick, got_ref[...]).astype(BF)
    first_ref[...] = packed[:, :LANES]
    rest_ref[...] = packed[:, LANES:]


def layer_norm(values):
    centered = values - jnp.mean(values, axis=-1, keepdims=True)
    spread = jnp.mean(centered * centered, axis=-1, keepdims=True)
    return centered * lax.rsqrt(spread + 1e-05)


def window_kernel(
    low_ref, hidden_ref, high_ref, flag_ref, wkv_hbm, wq_hbm, wo_hbm, xq_hbm, middle_ref, query_ref, wkv_ref, wq_ref, wo_ref, xq_ref, normed, keys, values, queries, context, bias, sems
):
    tok, width = hidden_ref.shape
    win = HALF_WIN
    span = 3 * win
    total = tok + 2 * win
    pairs = width // LANES
    pieces = ((wkv_hbm, wkv_ref), (wq_hbm, wq_ref), (wo_hbm, wo_ref), (xq_hbm, xq_ref))
    copies = [pltpu.make_async_copy(src, dst, sems.at[k]) for k, (src, dst) in enumerate(pieces)]
    for copy in copies:
        copy.start()
    normed[:win, :] = layer_norm(low_ref[:win, :].astype(F32)).astype(BF)
    normed[win : win + tok, :] = layer_norm(hidden_ref[...].astype(F32)).astype(BF)
    normed[win + tok :, :] = layer_norm(high_ref[:win, :].astype(F32)).astype(BF)
    flags = jnp.concatenate(
        [low_ref[win : win + 1, :win].astype(F32), flag_ref[...], high_ref[win : win + 1, :win].astype(F32)], axis=1
    )
    gap = iota((win, span), 1) - iota((win, span), 0)
    near = (gap >= 0) & (gap <= 2 * win)
    for b in range(tok // win):
        usable = (flags[:, b * win : b * win + span] > 0.0) | (gap == win)
        bias[b] = jnp.where(near & usable, 0.0, -1e30)
    for p in range(pairs):
        values[:, (2 * p + 1) * LANES : (2 * p + 2) * LANES] = jnp.ones((total, LANES), BF)
    wide = 2 * LANES
    copies[0].wait()
    for c in range(0, width, wide):
        keys[:, c : c + wide] = dot(normed[...], wkv_ref[:, c : c + wide]).astype(BF)
    for c in range(0, width, wide):
        part = dot(normed[...], wkv_ref[:, width + c : width + c + wide]).astype(BF).astype(F32) * 2.0**-8
        part = part.astype(BF)
        values[:, 2 * c : 2 * c + LANES] = part[:, :LANES]
        values[:, 2 * c + wide : 2 * c + wide + LANES] = part[:, LANES:]
    copies[1].wait()
    for c in range(0, width, wide):
        queries[:, c : c + wide] = (dot(normed[win : win + tok, :], wq_ref[:, c : c + wide]) * SCALE).astype(BF)
    low = iota((win, LANES), 1) < HALF
    for b in range(tok // win):
        for p in range(pairs):
            cols = slice(p * LANES, (p + 1) * LANES)
            query = queries[b * win : (b + 1) * win, cols]
            key = keys[b * win : b * win + span, cols]
            value = values[b * win : b * win + span, 2 * p * LANES : (2 * p + 2) * LANES]
            nothing = jnp.zeros_like(query)
            both = jnp.concatenate([jnp.where(low, query, nothing), jnp.where(low, nothing, query)], axis=0)
            scores = dot_t(both, key).reshape(2, win, span) + bias[b][None]
            out = dot(jnp.exp2(scores).astype(BF).reshape(2 * win, span), value)
            out = out[:, :LANES] / out[:, LANES:] * 256.0
            context[b * win : (b + 1) * win, cols] = jnp.where(low, out[:win], out[win:]).astype(BF)
    copies[2].wait()
    copies[3].wait()
    valid = jnp.transpose(jnp.broadcast_to(flag_ref[...], (LANES, tok)))
    for b in range(tok // win):
        rows = slice(b * win, (b + 1) * win)
        mixed = hidden_ref[rows, :].astype(F32) + dot(context[rows, :], wo_ref[...])
        mixed = mixed.astype(BF)
        middle_ref[rows, :] = mixed
        cross = dot(layer_norm(mixed.astype(F32)).astype(BF), xq_ref[...]) * SCALE
        tiles = [cross[:, p * LANES : (p + 1) * LANES] for p in range(pairs)]
        turned = [pltpu.roll(t, HALF, 1) for t in tiles]

        def placed(head, upper):
            return (turned if (head % 2 == 1) != upper else tiles)[head // 2]

        for g in range(GRID):
            first = jnp.where(low, placed(3 * g, False), placed(3 * g + 1, True))
            second = jnp.where(low, placed(3 * g + 2, False), valid[rows, :])
            query_ref[g, rows, :LANES] = first.astype(BF)
            query_ref[g, rows, LANES:] = second.astype(BF)


def cross_kernel(heads, count, where_ref, pos_ref, query_ref, *refs):
    kv_refs, refs = refs[:GRID], refs[GRID:]
    last = 2 in heads
    if last:
        before_ref, earlier_ref, out_ref, keys, values, expds, total = refs
    else:
        out_ref, mass_ref, keys, values, expds, total = refs
    held = kv_refs[0].shape[0]
    groups, tok, _ = query_ref.shape
    small = iota((tok, LANES), 1) < HALF
    if last:
        total[...] = before_ref[...]
    else:
        total[...] = jnp.zeros_like(total)
    lower = iota((held, LANES), 1) < HALF
    for k, inner in enumerate(heads):
        for c in range(GRID):
            block = kv_refs[c][:, k * LANES : (k + 1) * LANES]
            scaled = block.astype(F32) * 2.0**-4
            keys[k, c * held : (c + 1) * held, :] = block
            values[k, c * held : (c + 1) * held, :] = jnp.where(lower == (inner == 1), scaled, 1.0).astype(BF)

    def one(g, k, slot):
        inner = heads[k]
        value_low = inner == 1
        tile = LANES if inner == 2 else 0
        query = query_ref[g, :, tile : tile + LANES]
        query = jnp.where(small != value_low, query, jnp.zeros_like(query))
        acc = jnp.zeros((tok, LANES), F32)
        for c in range(0, GRID * held, 512):
            expd = jnp.exp2(dot_t(query, keys[k, c : c + 512, :])).astype(BF)
            expds[slot, :, c : c + 512] = expd
            acc = acc + dot(expd, values[k, c : c + 512, :])
        at = LANES - 1 if value_low else 0
        inverse = 1.0 / acc[:, at : at + 1]
        out = jnp.where(small == value_low, (acc * inverse) * 16.0, 0.0)
        share = inverse * query_ref[g, :, 2 * LANES - 1 :].astype(F32)
        for c in range(0, GRID * held, 512):
            mass = jnp.sum(expds[slot, :, c : c + 512].astype(F32) * share, axis=0, keepdims=True)
            total[:1, c : c + 512] = total[:1, c : c + 512] + mass
        return out

    if not last:

        def body(i, carry):
            for u in range(2):
                out_ref[2 * i + u] = one(2 * i + u, 0, u).astype(BF)
            return carry

        lax.fori_loop(0, groups // 2, body, 0)
        mass_ref[...] = total[...]
        return

    def body(g, carry):
        first = jnp.where(small, one(g, 0, 0), earlier_ref[g].astype(F32))
        out_ref[g, :tok, :LANES] = first.astype(BF)
        out_ref[g, :tok, LANES:] = one(g, 1, 1).astype(BF)
        return carry

    lax.fori_loop(0, groups, body, 0)
    padded = pos_ref.shape[1]
    score = jnp.zeros((8, padded), F32)
    line = iota((8, held), 0)
    for c in range(GRID):
        mass = jnp.broadcast_to(total[:1, c * held : (c + 1) * held], (8, held))
        first, second, third = thirds(mass)
        parts = jnp.where(line == 0, first, jnp.where(line == 1, second, jnp.where(line == 2, third, 0.0)))
        origin = (where_ref[1] + GRID - c) & (GRID - 1)
        at = iota((held, padded), 0) // DESC + origin * (count // GRID)
        score = score + dot(parts.astype(BF), (at == pos_ref[...]).astype(F32).astype(BF))
    score = jnp.sum(score, axis=0, keepdims=True)
    tokens = jnp.zeros((1, 1), F32)
    for g in range(groups):
        tokens = tokens + jnp.sum(query_ref[g, :, 2 * LANES - 1 :].astype(F32), axis=0, keepdims=True)
    score = jnp.where(iota((1, padded), 1) == count, tokens, score)
    rest = out_ref.shape[1] - tok
    left = jnp.zeros((rest, 2 * LANES), F32)
    right = jnp.zeros((rest, LANES), F32)
    for k, part in enumerate(thirds(score)):
        left = jnp.where(iota(left.shape, 0) == k, part[:, : 2 * LANES], left)
        right = jnp.where(iota(right.shape, 0) == 3 + k, part[:, 2 * LANES :], right)
    tail = left + jnp.concatenate([right, jnp.zeros_like(right)], axis=1)
    for g in range(groups):
        out_ref[g, tok:, :] = tail.astype(BF)


def thirds(value):
    first = value.astype(BF).astype(F32)
    second = (value - first).astype(BF).astype(F32)
    return first, second, value - first - second


def mass_kernel(tail_ref, out_ref):
    tail = jnp.sum(tail_ref[...].astype(F32), axis=0)
    left = jnp.sum(tail[:3, :], axis=0, keepdims=True)
    right = jnp.sum(tail[3:6, :LANES], axis=0, keepdims=True)
    out_ref[...] = jnp.concatenate([left, right], axis=1)


def final_kernel(middle_ref, out_refs, weight_ref, out_ref):
    groups = out_refs.shape[0]
    tok = middle_ref.shape[0]
    size = 3 * HALF
    acc = middle_ref[...].astype(F32)
    for g in range(groups):
        at = g * size
        turned = jnp.concatenate(
            [
                weight_ref[at + HALF : at + 2 * HALF, :],
                weight_ref[at : at + HALF, :],
                weight_ref[at + HALF : at + size, :],
            ],
            axis=0,
        )
        acc = acc + dot(out_refs[g, :tok, :], turned)
    out_ref[...] = acc.astype(BF)


def local(hidden, token_ids, w_query, w_keyval, w_out, x_query, x_out, shortlist, code_row, code_cache):
    doc_hidden = hidden[0]
    tok, width = doc_hidden.shape
    seq_count = lax.axis_size("seq")
    docs = lax.axis_size("doc")
    devices = docs * seq_count
    seq_index = lax.axis_index("seq")
    own = lax.axis_index("doc") * seq_count + seq_index
    where = jnp.stack([own, seq_index // GRID, lax.axis_index("doc")]).astype(I32)
    count = shortlist.shape[1]
    padded = -(-count // LANES) * LANES
    code_dev = code_cache.shape[0]
    held = count // GRID * DESC
    table = code_row.reshape(-1, LANES)
    anywhere = pl.BlockSpec(memory_space=pl.ANY)

    all_codes = lax.all_gather(shortlist, "doc", axis=0, tiled=False)
    all_codes, doc_hidden, token_ids = lax.optimization_barrier((all_codes, doc_hidden, token_ids))

    flag = (token_ids != 0).astype(BF)
    forward = [(i, i + 1) for i in range(seq_count - 1)]
    backward = [(t, s) for s, t in forward]

    def with_flags(rows, flags):
        return jnp.concatenate([rows, jnp.pad(flags, ((0, 7), (0, width - HALF_WIN)))], axis=0)

    low = lax.ppermute(with_flags(doc_hidden[tok - HALF_WIN :], flag[:, tok - HALF_WIN :]), "seq", forward)
    high = lax.ppermute(with_flags(doc_hidden[:HALF_WIN], flag[:, :HALF_WIN]), "seq", backward)

    send, slots, pos = pl.pallas_call(
        functools.partial(route_kernel, count, code_dev, devices),
        name="route",
        out_shape=(
            jax.ShapeDtypeStruct((docs * GRID, GRID, DESC, 3 * LANES), BF),
            jax.ShapeDtypeStruct((1, devices * DESC), I32),
            jax.ShapeDtypeStruct((1, padded), I32),
        ),
        in_specs=[smem(), vmem(), anywhere, anywhere],
        out_specs=(vmem(),) * 3,
        scratch_shapes=[
            pltpu.VMEM(table.shape, I32),
            pltpu.VMEM((docs * GRID, 2, DESC, width), BF),
            pltpu.VMEM((docs, padded), I32),
            pltpu.VMEM((docs, LANES), I32),
            pltpu.SMEM((docs, LANES), I32),
            pltpu.SemaphoreType.DMA((docs * GRID,)),
            pltpu.SemaphoreType.DMA((2,)),
        ],
        compiler_params=params(24),
        cost_estimate=cost(10**9, 0, 2 * 10**6),
    )(where, all_codes, table, code_cache)
    got = lax.all_to_all(
        send.reshape(devices, DESC, 3 * LANES), ("doc", "seq"), split_axis=0, concat_axis=0, tiled=True
    )

    middle, queries = pl.pallas_call(
        window_kernel,
        name="window",
        out_shape=(
            jax.ShapeDtypeStruct((tok, width), BF),
            jax.ShapeDtypeStruct((GRID, tok, 2 * LANES), BF),
        ),
        in_specs=[vmem()] * 4 + [anywhere] * 4,
        out_specs=(vmem(), vmem()),
        scratch_shapes=[
            pltpu.VMEM((width, 2 * width), BF),
            pltpu.VMEM((width, width), BF),
            pltpu.VMEM((width, width), BF),
            pltpu.VMEM((width, width), BF),
            pltpu.VMEM((tok + 2 * HALF_WIN, width), BF),
            pltpu.VMEM((tok + 2 * HALF_WIN, width), BF),
            pltpu.VMEM((tok + 2 * HALF_WIN, 2 * width), BF),
            pltpu.VMEM((tok, width), BF),
            pltpu.VMEM((tok, width), BF),
            pltpu.VMEM((tok // HALF_WIN, HALF_WIN, 3 * HALF_WIN), F32),
            pltpu.SemaphoreType.DMA((4,)),
        ],
        compiler_params=params(48),
        cost_estimate=cost(12 * 10**9, 5 * 10**6, 10**7),
    )(low, doc_hidden, high, flag.astype(F32), w_keyval, w_query, w_out, x_query)

    lines = [[GRID * z + x for x in range(GRID)] for z in range(GRID)]

    def across(block):
        return lax.all_to_all(
            block, "seq", split_axis=0, concat_axis=0, axis_index_groups=lines, tiled=True
        )

    queries = across(queries)

    blocks = pl.pallas_call(
        compact_kernel,
        name="compact",
        out_shape=(jax.ShapeDtypeStruct((held, LANES), BF), jax.ShapeDtypeStruct((held, 2 * LANES), BF)),
        in_specs=[vmem()] * 2,
        out_specs=(vmem(),) * 2,
        compiler_params=params(24),
        cost_estimate=cost(10**9, 0, 2 * 10**6),
    )(slots, got.reshape(devices * DESC, 3 * LANES))

    def turns(block):
        parts = []
        for shift in range(1, GRID):
            pairs = [(i, (i + GRID * shift) % seq_count) for i in range(seq_count)]
            parts.append(lax.ppermute(block, "seq", pairs))
        return parts

    first, rest = [[block] + turns(block) for block in blocks]

    def cross(heads, parts, extra, outs):
        return pl.pallas_call(
            functools.partial(cross_kernel, heads, count),
            name="cross",
            out_shape=outs,
            in_specs=[smem()] + [vmem()] * (2 + GRID + len(extra)),
            out_specs=jax.tree.map(lambda _: vmem(), outs),
            scratch_shapes=[
                pltpu.VMEM((len(heads), GRID * held, LANES), BF),
                pltpu.VMEM((len(heads), GRID * held, LANES), BF),
                pltpu.VMEM((2, tok, GRID * held), BF),
                pltpu.VMEM((8, GRID * held), F32),
            ],
            compiler_params=params(40),
            cost_estimate=cost(len(heads) * 10**10, 5 * 10**6, 4 * 10**6),
        )(where, pos, queries, *parts, *extra)

    out, mass = cross(
        (0,),
        first,
        (),
        (jax.ShapeDtypeStruct((GRID, tok, LANES), BF), jax.ShapeDtypeStruct((8, GRID * held), F32)),
    )
    out = cross((1, 2), rest, (mass, out), jax.ShapeDtypeStruct((GRID, tok + 16, 2 * LANES), BF))
    out = across(out)

    mass = pl.pallas_call(
        mass_kernel,
        name="mass",
        grid=(1,),
        out_shape=jax.ShapeDtypeStruct((1, padded), F32),
        in_specs=[pl.BlockSpec((GRID, 16, 2 * LANES), lambda i: (0, tok // 16, 0))],
        out_specs=pl.BlockSpec((1, padded), lambda i: (0, 0)),
        cost_estimate=cost(10**5, 0, 10**5),
    )(out)
    one, two, three = turns(mass)
    sums = (mass + two) + (one + three)
    tokens = sums[:, count : count + 1] * (1.0 / GRID)
    cand_score = count * sums[:, :count] / (HEADS * tokens)

    refined = pl.pallas_call(
        final_kernel,
        name="final",
        out_shape=jax.ShapeDtypeStruct((tok, width), BF),
        in_specs=[vmem()] * 3,
        out_specs=vmem(),
        compiler_params=params(16),
        cost_estimate=cost(10**9, 0, 4 * 10**6),
    )(middle, out, x_out)
    return (refined[None], cand_score)


def solution(mesh):
    return jax.shard_map(
        local,
        mesh=mesh,
        in_specs=(
            P("doc", "seq", None),
            P("doc", "seq"),
            P(),
            P(),
            P(),
            P(),
            P(),
            P("doc", None),
            P(),
            P(("doc", "seq"), None, None, None),
        ),
        out_specs=(P("doc", "seq", None), P("doc", None)),
        check_vma=False,
    )
```

time: 160 us -> 141 us (0.88)
  Pallas kernels: 62.1 us -> 53.5 us
  starting transfers between devices: 44.8 us -> 36.3 us
  blocking collectives: 33.1 us -> 26.6 us
  waiting for transfers between devices: 3.31 us -> 7.5 us
  local copies, waits for them, and re-layouts: 9.02 us -> 12.1 us
  other arithmetic: 4.18 us -> 2.14 us
    all_gather x2 -> x1, blocking collectives: 33.1 us -> 12.1 us  [local(): all_codes = lax.all_gather(shortlist, 'doc', axis=0, tiled=False)]
    all_to_all x0 -> x1, blocking collectives: none -> 14.4 us  [across(): lax.all_to_all(block, 'seq', split_axis=0, concat_axis=0, axis_index_grou...]
    all_to_all x3 -> x1, starting transfers between devices: 14.5 us -> 4.81 us  [across(): lax.all_to_all(block, 'seq', split_axis=0, concat_axis=0, axis_index_grou...]
    pallas_call x4 -> x3, Pallas kernels: 37.8 us -> 29.4 us  [the longest x2 28 us: cross(): pl.pallas_call(functools.partial(cross_kernel, heads, count), name='cross...]
    ppermute x11, waiting for transfers between devices: 3.3 us -> 7.49 us  [the longest x9 7.49 us: turns(): parts.append(lax.ppermute(block, 'seq', pairs))]
    unnamed x23 -> x28, local copies, waits for them, and re-layouts: 7.25 us -> 10.3 us
  transfers between devices with their start and end apart: 15 -> 13, of which waited for: 2 -> 4; matrix products, arithmetic and copies ran while one was open for 2% -> 1% of each run, Pallas kernels for 38% -> 24%
where the time goes in v2:
time: 141 us; the launch traced here: 140 us
  Pallas kernels  53.5 us (38%)
  starting transfers between devices  36.3 us (26%)
  blocking collectives  26.6 us (19%)
  local copies, waits for them, and re-layouts  12.1 us (9%)
  waiting for transfers between devices  7.5 us (5%)
  other arithmetic  2.14 us (2%)
  between operations  1.46 us (1%)
    pallas_call x2, Pallas kernels, cross(): pl.pallas_call(functools.partial(cross_kernel, heads, count), name='cross...  28 us
    ppermute x9, starting transfers between devices, turns(): parts.append(lax.ppermute(block, 'seq', pairs))  16.1 us
    all_to_all x1, blocking collectives, across(): lax.all_to_all(block, 'seq', split_axis=0, concat_axis=0, axis_index_grou...  14.4 us
    pallas_call x1, Pallas kernels, local(): pl.pallas_call(window_kernel, name='window', out_shape=(jax.ShapeDtypeStr...  13.7 us
    all_gather x1, blocking collectives, local(): all_codes = lax.all_gather(shortlist, 'doc', axis=0, tiled=False)  12.1 us
    unnamed x28, local copies, waits for them, and re-layouts  10.3 us
    all_to_all x1, starting transfers between devices, local(): lax.all_to_all(send.reshape(devices, DESC, 3 * LANES), ('doc', 'seq'), sp...  9.39 us
    pallas_call x1, Pallas kernels, local(): pl.pallas_call(functools.partial(route_kernel, count, code_dev, devices),...  7.68 us
  transfers between devices with their start and end apart: 13, of which 4 were waited for; matrix products, arithmetic and copies ran while one was open for 1% of the time, Pallas kernels for 24%

profile of v2, /device:TPU:2, one launch (start us, length us, event | category | flops | bytes accessed | tf_op | source)
XLA Modules:
  0.0 139.5 jit_solution(16151890689705534410)
XLA Ops:
  0.6 12.1 %all-gather.1.codes_ref = s32[8,1,320]{2,1,0:T(1,128)S(1)} all-gather(s32[1,1,320]{2,1,0:T(1,128)} %bitcast.15), channel_id=2, replica_groups=mesh['doc'=8,'seq'=16] {'doc'}, dimensions={0}, use_global_device_ids=true | all-gather | bytes 11520 | tf_op jit(solution)/shard_map/all_gather | solution.py:378
  12.8 0.7 fusion.5
  13.5 1.2 fusion.6
  14.6 0.0 copy-start.4
  14.7 3.5 %collective-permute-start = (bf16[264,768]{1,0:T(8,128)(2,1)S(1)}, bf16[264,768]{1,0:T(8,128)(2,1)S(1)}, u32[]{:S(2)}, u32[]{:S(2)}) collective-permute-start(bf16[264,768]{1,0:T(8,128)(2,1)S(1)} %fusion.2), channel_id=1, source_target_pairs={{0,1},{1,2},{2,3},{3,4},{4,5},{5,6},{6,7},{7,8},{8,9},{9,10},{10,1... | collective-permute-start | bytes 1216520 | tf_op jit(solution)/shard_map/ppermute | solution.py:388
  18.2 0.8 fusion.3
  19.0 2.5 %collective-permute-start.1 = (bf16[264,768]{1,0:T(8,128)(2,1)}, bf16[264,768]{1,0:T(8,128)(2,1)S(1)}, u32[]{:S(2)}, u32[]{:S(2)}) collective-permute-start(bf16[264,768]{1,0:T(8,128)(2,1)} %fusion.3), channel_id=1, source_target_pairs={{1,0},{2,1},{3,2},{4,3},{5,4},{6,5},{7,6},{8,7},{9,8},{10,9},{11,1... | collective-permute-start | bytes 1216520 | tf_op jit(solution)/shard_map/ppermute | solution.py:389
  21.5 0.1 pad_add_fusion.where_ref
  21.5 0.0 copy-done.4
  21.5 3.0 %copy-done.1 = bf16[288,2,8,768]{3,2,1,0:T(8,128)(2,1)S(1)} copy-done((bf16[288,2,8,768]{3,2,1,0:T(8,128)(2,1)S(1)}, bf16[288,2,8,768]{3,2,1,0:T(8,128)(2,1)}, u32[]{:S(2)}) %copy-start.1) | copy-done | bytes 7077912
  24.6 7.7 %route.1 = (bf16[32,4,8,384]{3,2,1,0:T(8,128)(2,1)}, s32[1,1024]{1,0:T(1,128)S(1)}, s32[1,384]{1,0:T(1,128)S(1)}) custom-call(s32[3]{0:T(128)S(1)} %pad_add_fusion.where_ref, s32[8,1,320]{2,1,0:T(1,128)S(1)} %all-gather.1.codes_ref, s32[288,128]{1,0:T(8,128)S(1)} %bitcast.13, bf16[288,2,8,768]{3,2,1,0:T(8,128)(2,1)S(1)} %copy-done.1), custom_call_target="tpu_custom_call" | custom-call | flops 1000000000 | bytes 2000000 | tf_op jit(solution)/shard_map/route/pallas_call | solution.py:391
  32.2 0.0 copy-start.3
  32.3 9.4 %all-to-all-start.1 = ((bf16[128,8,384]{2,1,0:T(8,128)(2,1)}), bf16[128,8,384]{2,1,0:T(8,128)(2,1)S(1)}, u32[]{:S(2)}, u32[]{:S(2)}) async-start(bf16[128,8,384]{2,1,0:T(8,128)(2,1)} %bitcast.6), calls=%async_computation.1 | async-start | bytes 1572864 | tf_op jit(solution)/shard_map/all_to_all | solution.py:413
  41.6 0.0 collective-permute-done.low_ref
  41.7 0.0 collective-permute-done.1.high_ref
  41.7 0.0 copy-done.3
  41.7 0.0 copy-start.5
  41.7 1.3 copy-done.5
  43.0 0.0 copy-start.6
  43.0 1.3 copy-done.6
  44.2 13.7 %window.1 = (bf16[512,768]{1,0:T(8,128)(2,1)S(1)}, bf16[4,512,256]{2,1,0:T(8,128)(2,1)}) custom-call(bf16[264,768]{1,0:T(8,128)(2,1)S(1)} %collective-permute-done.low_ref, bf16[512,768]{1,0:T(8,128)(2,1)S(1)} %bitcast.11, bf16[264,768]{1,0:T(8,128)(2,1)S(1)} %collective-permute-done.1.high_ref, f32[1,512]{1,0:T(1,128)S(1)} %get-tuple-element.28.flag_ref, ...), custom_call_target="tpu_custom_call" | custom-call | flops 12000000000 | bytes 10000000 | tf_op jit(solution)/shard_map/window/pallas_call | solution.py:417
  57.9 0.0 all-to-all-done.1
  58.0 4.8 %all-to-all-start = ((bf16[4,512,256]{2,1,0:T(8,128)(2,1)}), bf16[4,512,256]{2,1,0:T(8,128)(2,1)S(1)}, u32[]{:S(2)}, u32[]{:S(2)}) async-start(bf16[4,512,256]{2,1,0:T(8,128)(2,1)} %get-tuple-element.19), calls=%async_computation | async-start | bytes 2097152 | tf_op jit(solution)/shard_map/all_to_all | solution.py:446
  62.8 0.8 compact.1
  63.6 1.7 %collective-permute-start.5 = (bf16[640,128]{1,0:T(8,128)(2,1)S(1)}, bf16[640,128]{1,0:T(8,128)(2,1)S(1)}, u32[]{:S(2)}, u32[]{:S(2)}) collective-permute-start(bf16[640,128]{1,0:T(8,128)(2,1)S(1)} %get-tuple-element.23.refs_0_), channel_id=1, source_target_pairs={{0,4},{1,5},{2,6},{3,7},{4,8},{5,9},{6,10},{7,11},{8,12},{9,13},{1... | collective-permute-start | bytes 491528 | tf_op jit(solution)/shard_map/ppermute | solution.py:466
  65.3 3.2 %collective-permute-start.6 = (bf16[640,128]{1,0:T(8,128)(2,1)S(1)}, bf16[640,128]{1,0:T(8,128)(2,1)S(1)}, u32[]{:S(2)}, u32[]{:S(2)}) collective-permute-start(bf16[640,128]{1,0:T(8,128)(2,1)S(1)} %get-tuple-element.23.refs_0_), channel_id=1, source_target_pairs={{0,8},{1,9},{2,10},{3,11},{4,12},{5,13},{6,14},{7,15},{8,0},{9,1},... | collective-permute-start | bytes 491528 | tf_op jit(solution)/shard_map/ppermute | solution.py:466
  68.5 1.2 collective-permute-start.7
  69.7 0.8 collective-permute-start.2
  70.5 0.6 collective-permute-start.3
  71.2 0.1 collective-permute-done.5.refs_1_
  71.2 0.0 copy-start.7
  71.3 0.7 copy-done.7
  71.9 2.9 %collective-permute-start.4 = (bf16[640,256]{1,0:T(8,128)(2,1)S(1)}, bf16[640,256]{1,0:T(8,128)(2,1)S(1)}, u32[]{:S(2)}, u32[]{:S(2)}) collective-permute-start(bf16[640,256]{1,0:T(8,128)(2,1)S(1)} %get-tuple-element.22.refs_0_), channel_id=1, source_target_pairs={{0,12},{1,13},{2,14},{3,15},{4,0},{5,1},{6,2},{7,3},{8,4},{9,5},{1... | collective-permute-start | bytes 983048 | tf_op jit(solution)/shard_map/ppermute | solution.py:466
  74.8 2.3 %collective-permute-done.6.refs_2_ = bf16[640,128]{1,0:T(8,128)(2,1)S(1)} collective-permute-done((bf16[640,128]{1,0:T(8,128)(2,1)S(1)}, bf16[640,128]{1,0:T(8,128)(2,1)S(1)}, u32[]{:S(2)}, u32[]{:S(2)}) %collective-permute-start.6) | collective-permute-done | bytes 163872 | tf_op jit(solution)/shard_map/ppermute | solution.py:466
  77.1 0.0 copy-start.9
  77.1 0.7 copy-done.9
  77.8 3.2 %collective-permute-done.7.refs_3_ = bf16[640,128]{1,0:T(8,128)(2,1)S(1)} collective-permute-done((bf16[640,128]{1,0:T(8,128)(2,1)S(1)}, bf16[640,128]{1,0:T(8,128)(2,1)S(1)}, u32[]{:S(2)}, u32[]{:S(2)}) %collective-permute-start.7) | collective-permute-done | bytes 163872 | tf_op jit(solution)/shard_map/ppermute | solution.py:466
  81.0 0.0 copy-start.11
  81.0 0.6 copy-done.11
  81.6 0.0 all-to-all-done.query_ref
  81.6 0.0 copy-start.8
  81.6 0.9 copy-done.8
  82.5 0.0 copy-start.10
  82.5 0.9 copy-done.10
  83.4 0.9 copy-done.12
  84.4 9.3 %cross.2 = (bf16[4,512,128]{2,1,0:T(8,128)(2,1)S(1)}, f32[8,2560]{1,0:T(8,128)S(1)}) custom-call(s32[3]{0:T(128)S(1)} %pad_add_fusion.where_ref, s32[1,384]{1,0:T(1,128)S(1)} %get-tuple-element.18.pos_ref, bf16[4,512,256]{2,1,0:T(8,128)(2,1)S(1)} %all-to-all-done.query_ref, bf16[640,128]{1,0:T(8,128)(2,1)S(1)} %get-tuple-element.23.refs_0_, ...), custom_call_target="tpu_custom_call" | custom-call | flops 10000000000 | bytes 4000000 | tf_op jit(solution)/shard_map/cross/pallas_call | solution.py:472
  93.7 0.0 collective-permute-done.2.refs_1_
  93.7 0.0 collective-permute-done.3.refs_2_
  93.7 0.0 collective-permute-done.4.refs_3_
  93.7 18.7 %cross.3 = bf16[4,528,256]{2,1,0:T(8,128)(2,1)S(1)} custom-call(s32[3]{0:T(128)S(1)} %pad_add_fusion.where_ref, s32[1,384]{1,0:T(1,128)S(1)} %get-tuple-element.18.pos_ref, bf16[4,512,256]{2,1,0:T(8,128)(2,1)S(1)} %all-to-all-done.query_ref, bf16[640,256]{1,0:T(8,128)(2,1)S(1)} %get-tuple-element.22.refs_0_, ...), custom_call_target="tpu_custom_call" | custom-call | flops 20000000000 | bytes 4000000 | tf_op jit(solution)/shard_map/cross/pallas_call | solution.py:472
  112.4 14.4 %all_to_all.15.out_refs.tail_ref = bf16[4,528,256]{2,1,0:T(8,128)(2,1)} all-to-all(bf16[4,528,256]{2,1,0:T(8,128)(2,1)S(1)} %cross.3), channel_id=1, replica_groups={{0,1,2,3},{4,5,6,7},{8,9,10,11},{12,13,14,15},{16,17,18,19},{20,21,22,2..., dimensions={0} | all-to-all | bytes 2162688 | tf_op jit(solution)/shard_map/all_to_all | solution.py:446
  126.8 1.4 %mass.1 = f32[1,384]{1,0:T(1,128)} custom-call(bf16[4,528,256]{2,1,0:T(8,128)(2,1)} %all_to_all.15.out_refs.tail_ref), custom_call_target="tpu_custom_call" | custom-call | flops 100000 | bytes 100000 | tf_op jit(solution)/shard_map/mass/pallas_call | solution.py:497
  128.2 2.1 %collective-permute-start.9 = (f32[1,384]{1,0:T(1,128)}, f32[1,384]{1,0:T(1,128)S(1)}, u32[]{:S(2)}, u32[]{:S(2)}) collective-permute-start(f32[1,384]{1,0:T(1,128)} %mass.1), channel_id=1, source_target_pairs={{0,4},{1,5},{2,6},{3,7},{4,8},{5,9},{6,10},{7,11},{8,12},{9,13},{1... | collective-permute-start | bytes 4616 | tf_op jit(solution)/shard_map/ppermute | solution.py:466
  130.4 2.1 %collective-permute-start.10 = (f32[1,384]{1,0:T(1,128)}, f32[1,384]{1,0:T(1,128)S(1)}, u32[]{:S(2)}, u32[]{:S(2)}) collective-permute-start(f32[1,384]{1,0:T(1,128)} %mass.1), channel_id=1, source_target_pairs={{0,12},{1,13},{2,14},{3,15},{4,0},{5,1},{6,2},{7,3},{8,4},{9,5},{1... | collective-permute-start | bytes 4616 | tf_op jit(solution)/shard_map/ppermute | solution.py:466
  132.4 1.5 %collective-permute-start.8 = (f32[1,384]{1,0:T(1,128)}, f32[1,384]{1,0:T(1,128)S(1)}, u32[]{:S(2)}, u32[]{:S(2)}) collective-permute-start(f32[1,384]{1,0:T(1,128)} %mass.1), channel_id=1, source_target_pairs={{0,8},{1,9},{2,10},{3,11},{4,12},{5,13},{6,14},{7,15},{8,0},{9,1},... | collective-permute-start | bytes 4616 | tf_op jit(solution)/shard_map/ppermute | solution.py:466
  133.9 0.0 copy-done.2
  133.9 0.0 copy-done
  133.9 1.9 %final.1 = bf16[512,768]{1,0:T(8,128)(2,1)} custom-call(bf16[512,768]{1,0:T(8,128)(2,1)S(1)} %get-tuple-element.16.middle_ref, bf16[4,528,256]{2,1,0:T(8,128)(2,1)S(1)} %copy-done, bf16[768,768]{1,0:T(8,128)(2,1)S(1)} %copy-done.2), custom_call_target="tpu_custom_call" | custom-call | flops 1000000000 | bytes 4000000 | tf_op jit(solution)/shard_map/final/pallas_call | solution.py:511
  135.8 0.0 collective-permute-done.9
  135.8 0.0 collective-permute-done.10
  135.8 1.9 %collective-permute-done.8 = f32[1,384]{1,0:T(1,128)S(1)} collective-permute-done((f32[1,384]{1,0:T(1,128)}, f32[1,384]{1,0:T(1,128)S(1)}, u32[]{:S(2)}, u32[]{:S(2)}) %collective-permute-start.8) | collective-permute-done | bytes 1568 | tf_op jit(solution)/shard_map/ppermute | solution.py:466
  137.7 0.0 copy-done.13
  137.7 0.6 slice.27
  139.0 0.6 fusion.4
  (8 shorter events, 0.0 us)
Async XLA Ops:
  14.6 6.9 %copy-start.4 = (s32[36864]{0:T(1024)S(1)}, s32[36864]{0:T(1024)}, u32[]{:S(2)}) copy-start(s32[36864]{0:T(1024)} %param.18) | copy-start | bytes 442372
  14.7 27.0 %collective-permute-start = (bf16[264,768]{1,0:T(8,128)(2,1)S(1)}, bf16[264,768]{1,0:T(8,128)(2,1)S(1)}, u32[]{:S(2)}, u32[]{:S(2)}) collective-permute-start(bf16[264,768]{1,0:T(8,128)(2,1)S(1)} %fusion.2), channel_id=1, source_target_pairs={{0,1},{1,2},{2,3},{3,4},{4,5},{5,6},{6,7},{7,8},{8,9},{9,10},{10,1... | collective-permute-start | bytes 1216520 | tf_op jit(solution)/shard_map/ppermute | solution.py:388
  19.0 22.7 %collective-permute-start.1 = (bf16[264,768]{1,0:T(8,128)(2,1)}, bf16[264,768]{1,0:T(8,128)(2,1)S(1)}, u32[]{:S(2)}, u32[]{:S(2)}) collective-permute-start(bf16[264,768]{1,0:T(8,128)(2,1)} %fusion.3), channel_id=1, source_target_pairs={{1,0},{2,1},{3,2},{4,3},{5,4},{6,5},{7,6},{8,7},{9,8},{10,9},{11,1... | collective-permute-start | bytes 1216520 | tf_op jit(solution)/shard_map/ppermute | solution.py:389
  21.5 3.0 %copy-start.1 = (bf16[288,2,8,768]{3,2,1,0:T(8,128)(2,1)S(1)}, bf16[288,2,8,768]{3,2,1,0:T(8,128)(2,1)}, u32[]{:S(2)}) copy-start(bf16[288,2,8,768]{3,2,1,0:T(8,128)(2,1)} %cache_ref.1) | copy-start | bytes 21233668
  32.2 9.4 %copy-start.3 = (bf16[1,512,768]{2,1,0:T(8,128)(2,1)S(1)}, bf16[1,512,768]{2,1,0:T(8,128)(2,1)}, u32[]{:S(2)}) copy-start(bf16[1,512,768]{2,1,0:T(8,128)(2,1)} %param.10) | copy-start | bytes 2359300
  32.3 25.7 %all-to-all-start.1 = ((bf16[128,8,384]{2,1,0:T(8,128)(2,1)}), bf16[128,8,384]{2,1,0:T(8,128)(2,1)S(1)}, u32[]{:S(2)}, u32[]{:S(2)}) async-start(bf16[128,8,384]{2,1,0:T(8,128)(2,1)} %bitcast.6), calls=%async_computation.1 | async-start | bytes 1572864 | tf_op jit(solution)/shard_map/all_to_all | solution.py:413
  41.7 1.3 copy-start.5
  43.0 1.3 copy-start.6
  58.0 23.7 %all-to-all-start = ((bf16[4,512,256]{2,1,0:T(8,128)(2,1)}), bf16[4,512,256]{2,1,0:T(8,128)(2,1)S(1)}, u32[]{:S(2)}, u32[]{:S(2)}) async-start(bf16[4,512,256]{2,1,0:T(8,128)(2,1)} %get-tuple-element.19), calls=%async_computation | async-start | bytes 2097152 | tf_op jit(solution)/shard_map/all_to_all | solution.py:446
  63.6 7.6 %collective-permute-start.5 = (bf16[640,128]{1,0:T(8,128)(2,1)S(1)}, bf16[640,128]{1,0:T(8,128)(2,1)S(1)}, u32[]{:S(2)}, u32[]{:S(2)}) collective-permute-start(bf16[640,128]{1,0:T(8,128)(2,1)S(1)} %get-tuple-element.23.refs_0_), channel_id=1, source_target_pairs={{0,4},{1,5},{2,6},{3,7},{4,8},{5,9},{6,10},{7,11},{8,12},{9,13},{1... | collective-permute-start | bytes 491528 | tf_op jit(solution)/shard_map/ppermute | solution.py:466
  65.3 11.8 %collective-permute-start.6 = (bf16[640,128]{1,0:T(8,128)(2,1)S(1)}, bf16[640,128]{1,0:T(8,128)(2,1)S(1)}, u32[]{:S(2)}, u32[]{:S(2)}) collective-permute-start(bf16[640,128]{1,0:T(8,128)(2,1)S(1)} %get-tuple-element.23.refs_0_), channel_id=1, source_target_pairs={{0,8},{1,9},{2,10},{3,11},{4,12},{5,13},{6,14},{7,15},{8,0},{9,1},... | collective-permute-start | bytes 491528 | tf_op jit(solution)/shard_map/ppermute | solution.py:466
  68.5 12.4 %collective-permute-start.7 = (bf16[640,128]{1,0:T(8,128)(2,1)S(1)}, bf16[640,128]{1,0:T(8,128)(2,1)S(1)}, u32[]{:S(2)}, u32[]{:S(2)}) collective-permute-start(bf16[640,128]{1,0:T(8,128)(2,1)S(1)} %get-tuple-element.23.refs_0_), channel_id=1, source_target_pairs={{0,12},{1,13},{2,14},{3,15},{4,0},{5,1},{6,2},{7,3},{8,4},{9,5},{1... | collective-permute-start | bytes 491528 | tf_op jit(solution)/shard_map/ppermute | solution.py:466
  69.7 24.0 %collective-permute-start.2 = (bf16[640,256]{1,0:T(8,128)(2,1)S(1)}, bf16[640,256]{1,0:T(8,128)(2,1)S(1)}, u32[]{:S(2)}, u32[]{:S(2)}) collective-permute-start(bf16[640,256]{1,0:T(8,128)(2,1)S(1)} %get-tuple-element.22.refs_0_), channel_id=1, source_target_pairs={{0,4},{1,5},{2,6},{3,7},{4,8},{5,9},{6,10},{7,11},{8,12},{9,13},{1... | collective-permute-start | bytes 983048 | tf_op jit(solution)/shard_map/ppermute | solution.py:466
  70.5 23.1 %collective-permute-start.3 = (bf16[640,256]{1,0:T(8,128)(2,1)S(1)}, bf16[640,256]{1,0:T(8,128)(2,1)S(1)}, u32[]{:S(2)}, u32[]{:S(2)}) collective-permute-start(bf16[640,256]{1,0:T(8,128)(2,1)S(1)} %get-tuple-element.22.refs_0_), channel_id=1, source_target_pairs={{0,8},{1,9},{2,10},{3,11},{4,12},{5,13},{6,14},{7,15},{8,0},{9,1},... | collective-permute-start | bytes 983048 | tf_op jit(solution)/shard_map/ppermute | solution.py:466
  71.2 0.7 copy-start.7
  71.9 21.8 %collective-permute-start.4 = (bf16[640,256]{1,0:T(8,128)(2,1)S(1)}, bf16[640,256]{1,0:T(8,128)(2,1)S(1)}, u32[]{:S(2)}, u32[]{:S(2)}) collective-permute-start(bf16[640,256]{1,0:T(8,128)(2,1)S(1)} %get-tuple-element.22.refs_0_), channel_id=1, source_target_pairs={{0,12},{1,13},{2,14},{3,15},{4,0},{5,1},{6,2},{7,3},{8,4},{9,5},{1... | collective-permute-start | bytes 983048 | tf_op jit(solution)/shard_map/ppermute | solution.py:466
  77.1 0.7 copy-start.9
  81.0 0.7 copy-start.11
  81.6 0.9 copy-start.8
  82.5 0.9 copy-start.10
  83.4 0.9 copy-start.12
  112.4 21.5 %copy-start.2 = (bf16[768,768]{1,0:T(8,128)(2,1)S(1)}, bf16[768,768]{1,0:T(8,128)(2,1)}, u32[]{:S(2)}) copy-start(bf16[768,768]{1,0:T(8,128)(2,1)} %weight_ref.1) | copy-start | bytes 3538948
  126.8 7.1 %copy-start = (bf16[4,528,256]{2,1,0:T(8,128)(2,1)S(1)}, bf16[4,528,256]{2,1,0:T(8,128)(2,1)}, u32[]{:S(2)}) copy-start(bf16[4,528,256]{2,1,0:T(8,128)(2,1)} %all_to_all.15.out_refs.tail_ref) | copy-start | bytes 3244036
  128.2 7.5 %collective-permute-start.9 = (f32[1,384]{1,0:T(1,128)}, f32[1,384]{1,0:T(1,128)S(1)}, u32[]{:S(2)}, u32[]{:S(2)}) collective-permute-start(f32[1,384]{1,0:T(1,128)} %mass.1), channel_id=1, source_target_pairs={{0,4},{1,5},{2,6},{3,7},{4,8},{5,9},{6,10},{7,11},{8,12},{9,13},{1... | collective-permute-start | bytes 4616 | tf_op jit(solution)/shard_map/ppermute | solution.py:466
  130.4 5.4 %collective-permute-start.10 = (f32[1,384]{1,0:T(1,128)}, f32[1,384]{1,0:T(1,128)S(1)}, u32[]{:S(2)}, u32[]{:S(2)}) collective-permute-start(f32[1,384]{1,0:T(1,128)} %mass.1), channel_id=1, source_target_pairs={{0,12},{1,13},{2,14},{3,15},{4,0},{5,1},{6,2},{7,3},{8,4},{9,5},{1... | collective-permute-start | bytes 4616 | tf_op jit(solution)/shard_map/ppermute | solution.py:466
  132.4 5.3 %collective-permute-start.8 = (f32[1,384]{1,0:T(1,128)}, f32[1,384]{1,0:T(1,128)S(1)}, u32[]{:S(2)}, u32[]{:S(2)}) collective-permute-start(f32[1,384]{1,0:T(1,128)} %mass.1), channel_id=1, source_target_pairs={{0,8},{1,9},{2,10},{3,11},{4,12},{5,13},{6,14},{7,15},{8,0},{9,1},... | collective-permute-start | bytes 4616 | tf_op jit(solution)/shard_map/ppermute | solution.py:466
  133.9 3.8 %copy-start.13 = (f32[1,384]{1,0:T(1,128)S(1)}, f32[1,384]{1,0:T(1,128)}, u32[]{:S(2)}) copy-start(f32[1,384]{1,0:T(1,128)} %mass.1) | copy-start | bytes 4612

commit v3 on v2

--- a/solution.py
+++ b/solution.py
@@ -42,6 +42,14 @@
 
 def smem():
     return pl.BlockSpec(memory_space=pltpu.SMEM)
+
+
+def pinned(array):
+    return pltpu.with_memory_space_constraint(array, pltpu.HBM)
+
+
+def hbm():
+    return pl.BlockSpec(memory_space=pltpu.HBM)
 
 
 def cost(flops, exps, bytes_):
@@ -169,8 +177,18 @@
     return centered * lax.rsqrt(spread + 1e-05)
 
 
+def halo_kernel(hidden_ref, tokens_ref, tail_ref, head_ref):
+    tok, width = hidden_ref.shape
+    win = HALF_WIN
+    flags = (tokens_ref[...] != 0).astype(F32)
+    for ref, start in ((tail_ref, tok - win), (head_ref, 0)):
+        ref[:win, :] = hidden_ref[start : start + win, :]
+        row = jnp.concatenate([flags[:, start : start + win], jnp.zeros((1, width - win), F32)], axis=1)
+        ref[win:, :] = jnp.broadcast_to(row, (8, width)).astype(BF)
+
+
 def window_kernel(
-    low_ref, hidden_ref, high_ref, flag_ref, wkv_hbm, wq_hbm, wo_hbm, xq_hbm, middle_ref, query_ref, wkv_ref, wq_ref, wo_ref, xq_ref, normed, keys, values, queries, context, bias, sems
+    low_ref, hidden_ref, high_ref, tokens_ref, wkv_hbm, wq_hbm, wo_hbm, xq_hbm, middle_ref, query_ref, wkv_ref, wq_ref, wo_ref, xq_ref, normed, keys, values, queries, context, bias, sems
 ):
     tok, width = hidden_ref.shape
     win = HALF_WIN
@@ -184,8 +202,9 @@
     normed[:win, :] = layer_norm(low_ref[:win, :].astype(F32)).astype(BF)
     normed[win : win + tok, :] = layer_norm(hidden_ref[...].astype(F32)).astype(BF)
     normed[win + tok :, :] = layer_norm(high_ref[:win, :].astype(F32)).astype(BF)
+    own_flags = (tokens_ref[...] != 0).astype(F32)
     flags = jnp.concatenate(
-        [low_ref[win : win + 1, :win].astype(F32), flag_ref[...], high_ref[win : win + 1, :win].astype(F32)], axis=1
+        [low_ref[win : win + 1, :win].astype(F32), own_flags, high_ref[win : win + 1, :win].astype(F32)], axis=1
     )
     gap = iota((win, span), 1) - iota((win, span), 0)
     near = (gap >= 0) & (gap <= 2 * win)
@@ -221,7 +240,7 @@
             context[b * win : (b + 1) * win, cols] = jnp.where(low, out[:win], out[win:]).astype(BF)
     copies[2].wait()
     copies[3].wait()
-    valid = jnp.transpose(jnp.broadcast_to(flag_ref[...], (LANES, tok)))
+    thirds_of = [[] for _ in range(GRID)]
     for b in range(tok // win):
         rows = slice(b * win, (b + 1) * win)
         mixed = hidden_ref[rows, :].astype(F32) + dot(context[rows, :], wo_ref[...])
@@ -236,21 +255,37 @@
 
         for g in range(GRID):
             first = jnp.where(low, placed(3 * g, False), placed(3 * g + 1, True))
-            second = jnp.where(low, placed(3 * g + 2, False), valid[rows, :])
-            query_ref[g, rows, :LANES] = first.astype(BF)
-            query_ref[g, rows, LANES:] = second.astype(BF)
+            query_ref[g, rows, :] = first.astype(BF)
+            thirds_of[g].append(placed(3 * g + 2, b == 1))
+    line = iota((16, LANES), 0)
+    marks = jnp.zeros((16, LANES), F32)
+    for k in range(tok // LANES):
+        marks = jnp.where(line == k, own_flags[:, k * LANES : (k + 1) * LANES], marks)
+    for g in range(GRID):
+        query_ref[g, tok : tok + win, :] = jnp.where(low, thirds_of[g][0], thirds_of[g][1]).astype(BF)
+        query_ref[g, tok + win :, :] = marks.astype(BF)
 
 
 def cross_kernel(heads, count, where_ref, pos_ref, query_ref, *refs):
     kv_refs, refs = refs[:GRID], refs[GRID:]
     last = 2 in heads
     if last:
-        before_ref, earlier_ref, out_ref, keys, values, expds, total = refs
+        before_ref, earlier_ref, out_ref, keys, values, expds, total, sems = refs
     else:
-        out_ref, mass_ref, keys, values, expds, total = refs
+        out_ref, mass_ref, keys, values, expds, total, sems = refs
     held = kv_refs[0].shape[0]
-    groups, tok, _ = query_ref.shape
+    tok = expds.shape[1]
+    groups = query_ref.shape[0]
+    half = tok // 2
+    copies = []
+    for k in range(len(heads)):
+        for c in range(GRID):
+            source = kv_refs[c].at[:, pl.ds(k * LANES, LANES)]
+            copy = pltpu.make_async_copy(source, keys.at[k, pl.ds(c * held, held), :], sems.at[k * GRID + c])
+            copy.start()
+            copies.append(copy)
     small = iota((tok, LANES), 1) < HALF
+    low = iota((half, LANES), 1) < HALF
     if last:
         total[...] = before_ref[...]
     else:
@@ -258,16 +293,20 @@
     lower = iota((held, LANES), 1) < HALF
     for k, inner in enumerate(heads):
         for c in range(GRID):
-            block = kv_refs[c][:, k * LANES : (k + 1) * LANES]
-            scaled = block.astype(F32) * 2.0**-4
-            keys[k, c * held : (c + 1) * held, :] = block
-            values[k, c * held : (c + 1) * held, :] = jnp.where(lower == (inner == 1), scaled, 1.0).astype(BF)
+            copies[k * GRID + c].wait()
+            rows = pl.ds(c * held, held)
+            scaled = keys[k, rows, :].astype(F32) * 2.0**-4
+            values[k, rows, :] = jnp.where(lower == (inner == 1), scaled, 1.0).astype(BF)
 
     def one(g, k, slot):
         inner = heads[k]
         value_low = inner == 1
-        tile = LANES if inner == 2 else 0
-        query = query_ref[g, :, tile : tile + LANES]
+        if inner == 2:
+            packed = query_ref[g, tok : tok + half, :]
+            turned = pltpu.roll(packed.astype(F32), HALF, 1).astype(BF)
+            query = jnp.concatenate([packed, turned], axis=0)
+        else:
+            query = query_ref[g, :tok, :]
         query = jnp.where(small != value_low, query, jnp.zeros_like(query))
         acc = jnp.zeros((tok, LANES), F32)
         for c in range(0, GRID * held, 512):
@@ -276,13 +315,17 @@
             acc = acc + dot(expd, values[k, c : c + 512, :])
         at = LANES - 1 if value_low else 0
         inverse = 1.0 / acc[:, at : at + 1]
-        out = jnp.where(small == value_low, (acc * inverse) * 16.0, 0.0)
-        share = inverse * query_ref[g, :, 2 * LANES - 1 :].astype(F32)
+        out = (acc * inverse) * 16.0
+        share = jnp.where(iota((tok, 1), 0).astype(F32) < tokens_of(g), inverse, 0.0)
         for c in range(0, GRID * held, 512):
             mass = jnp.sum(expds[slot, :, c : c + 512].astype(F32) * share, axis=0, keepdims=True)
             total[:1, c : c + 512] = total[:1, c : c + 512] + mass
         return out
 
+    def tokens_of(g):
+        marks = query_ref[g, tok + half :, :].astype(F32)
+        return jnp.sum(jnp.sum(marks, axis=0, keepdims=True), axis=1, keepdims=True)
+
     if not last:
 
         def body(i, carry):
@@ -295,9 +338,9 @@
         return
 
     def body(g, carry):
-        first = jnp.where(small, one(g, 0, 0), earlier_ref[g].astype(F32))
-        out_ref[g, :tok, :LANES] = first.astype(BF)
-        out_ref[g, :tok, LANES:] = one(g, 1, 1).astype(BF)
+        out_ref[g, :tok, :] = jnp.where(small, one(g, 0, 0), earlier_ref[g].astype(F32)).astype(BF)
+        out = one(g, 1, 1)
+        out_ref[g, tok : tok + half, :] = jnp.where(low, pltpu.roll(out[:half], HALF, 1), out[half:]).astype(BF)
         return carry
 
     lax.fori_loop(0, groups, body, 0)
@@ -312,19 +355,16 @@
         at = iota((held, padded), 0) // DESC + origin * (count // GRID)
         score = score + dot(parts.astype(BF), (at == pos_ref[...]).astype(F32).astype(BF))
     score = jnp.sum(score, axis=0, keepdims=True)
-    tokens = jnp.zeros((1, 1), F32)
+    tokens = tokens_of(0)
+    for g in range(1, groups):
+        tokens = tokens + tokens_of(g)
+    score = jnp.where(iota((1, padded), 1) == count, tokens, score)
+    tail = jnp.zeros((16, LANES), F32)
+    for k, part in enumerate(thirds(score)):
+        for j in range(padded // LANES):
+            tail = jnp.where(iota(tail.shape, 0) == 3 * j + k, part[:, j * LANES : (j + 1) * LANES], tail)
     for g in range(groups):
-        tokens = tokens + jnp.sum(query_ref[g, :, 2 * LANES - 1 :].astype(F32), axis=0, keepdims=True)
-    score = jnp.where(iota((1, padded), 1) == count, tokens, score)
-    rest = out_ref.shape[1] - tok
-    left = jnp.zeros((rest, 2 * LANES), F32)
-    right = jnp.zeros((rest, LANES), F32)
-    for k, part in enumerate(thirds(score)):
-        left = jnp.where(iota(left.shape, 0) == k, part[:, : 2 * LANES], left)
-        right = jnp.where(iota(right.shape, 0) == 3 + k, part[:, 2 * LANES :], right)
-    tail = left + jnp.concatenate([right, jnp.zeros_like(right)], axis=1)
-    for g in range(groups):
-        out_ref[g, tok:, :] = tail.astype(BF)
+        out_ref[g, tok + half :, :] = tail.astype(BF)
 
 
 def thirds(value):
@@ -333,29 +373,30 @@
     return first, second, value - first - second
 
 
-def mass_kernel(tail_ref, out_ref):
-    tail = jnp.sum(tail_ref[...].astype(F32), axis=0)
-    left = jnp.sum(tail[:3, :], axis=0, keepdims=True)
-    right = jnp.sum(tail[3:6, :LANES], axis=0, keepdims=True)
-    out_ref[...] = jnp.concatenate([left, right], axis=1)
-
-
-def final_kernel(middle_ref, out_refs, weight_ref, out_ref):
-    groups = out_refs.shape[0]
+def mass_kernel(out_hbm, line_ref, tail, sem):
+    groups, size, _ = tail.shape
+    copy = pltpu.make_async_copy(out_hbm.at[:, pl.ds(out_hbm.shape[1] - size, size), :], tail, sem)
+    copy.start()
+    copy.wait()
+    total = jnp.sum(tail[...].astype(F32), axis=0)
+    for j in range(line_ref.shape[1] // LANES):
+        line_ref[:, j * LANES : (j + 1) * LANES] = jnp.sum(total[3 * j : 3 * j + 3, :], axis=0, keepdims=True)
+
+
+def final_kernel(middle_ref, got_ref, weight_ref, out_ref):
     tok = middle_ref.shape[0]
+    half = tok // 2
     size = 3 * HALF
+    low = iota((half, LANES), 1) < HALF
     acc = middle_ref[...].astype(F32)
-    for g in range(groups):
+    for g in range(got_ref.shape[0]):
         at = g * size
-        turned = jnp.concatenate(
-            [
-                weight_ref[at + HALF : at + 2 * HALF, :],
-                weight_ref[at : at + HALF, :],
-                weight_ref[at + HALF : at + size, :],
-            ],
-            axis=0,
-        )
-        acc = acc + dot(out_refs[g, :tok, :], turned)
+        heads = [weight_ref[at + k * HALF : at + (k + 1) * HALF, :] for k in (1, 0, 2, 2)]
+        packed = got_ref[g, tok : tok + half, :]
+        nothing = jnp.zeros_like(packed)
+        third = jnp.concatenate([jnp.where(low, packed, nothing), jnp.where(low, nothing, packed)], axis=0)
+        lhs = jnp.concatenate([got_ref[g, :tok, :], third], axis=1)
+        acc = acc + dot(lhs, jnp.concatenate(heads, axis=0))
     out_ref[...] = acc.astype(BF)
 
 
@@ -372,21 +413,26 @@
     padded = -(-count // LANES) * LANES
     code_dev = code_cache.shape[0]
     held = count // GRID * DESC
+    message = tok + tok // 2 + 16
     table = code_row.reshape(-1, LANES)
-    anywhere = pl.BlockSpec(memory_space=pl.ANY)
-
-    all_codes = lax.all_gather(shortlist, "doc", axis=0, tiled=False)
-    all_codes, doc_hidden, token_ids = lax.optimization_barrier((all_codes, doc_hidden, token_ids))
-
-    flag = (token_ids != 0).astype(BF)
+
+    asked = jnp.broadcast_to(shortlist[None], (docs, 1, count))
+    asked, doc_hidden, token_ids = lax.optimization_barrier((asked, doc_hidden, token_ids))
+
     forward = [(i, i + 1) for i in range(seq_count - 1)]
     backward = [(t, s) for s, t in forward]
-
-    def with_flags(rows, flags):
-        return jnp.concatenate([rows, jnp.pad(flags, ((0, 7), (0, width - HALF_WIN)))], axis=0)
-
-    low = lax.ppermute(with_flags(doc_hidden[tok - HALF_WIN :], flag[:, tok - HALF_WIN :]), "seq", forward)
-    high = lax.ppermute(with_flags(doc_hidden[:HALF_WIN], flag[:, :HALF_WIN]), "seq", backward)
+    all_codes = lax.all_to_all(asked, "doc", split_axis=0, concat_axis=0, tiled=True)
+    tail, head = pl.pallas_call(
+        halo_kernel,
+        name="halo",
+        out_shape=(jax.ShapeDtypeStruct((HALF_WIN + 8, width), BF),) * 2,
+        in_specs=[vmem()] * 2,
+        out_specs=(vmem(),) * 2,
+        compiler_params=params(16),
+        cost_estimate=cost(10**5, 0, 16 * 10**5),
+    )(doc_hidden, token_ids)
+    low = lax.ppermute(tail, "seq", forward)
+    high = lax.ppermute(head, "seq", backward)
 
     send, slots, pos = pl.pallas_call(
         functools.partial(route_kernel, count, code_dev, devices),
@@ -396,7 +442,7 @@
             jax.ShapeDtypeStruct((1, devices * DESC), I32),
             jax.ShapeDtypeStruct((1, padded), I32),
         ),
-        in_specs=[smem(), vmem(), anywhere, anywhere],
+        in_specs=[smem(), vmem(), hbm(), hbm()],
         out_specs=(vmem(),) * 3,
         scratch_shapes=[
             pltpu.VMEM(table.shape, I32),
@@ -409,7 +455,7 @@
         ],
         compiler_params=params(24),
         cost_estimate=cost(10**9, 0, 2 * 10**6),
-    )(where, all_codes, table, code_cache)
+    )(where, all_codes, pinned(table), pinned(code_cache))
     got = lax.all_to_all(
         send.reshape(devices, DESC, 3 * LANES), ("doc", "seq"), split_axis=0, concat_axis=0, tiled=True
     )
@@ -419,9 +465,9 @@
         name="window",
         out_shape=(
             jax.ShapeDtypeStruct((tok, width), BF),
-            jax.ShapeDtypeStruct((GRID, tok, 2 * LANES), BF),
+            jax.ShapeDtypeStruct((GRID, message, LANES), BF),
         ),
-        in_specs=[vmem()] * 4 + [anywhere] * 4,
+        in_specs=[vmem()] * 4 + [hbm()] * 4,
         out_specs=(vmem(), vmem()),
         scratch_shapes=[
             pltpu.VMEM((width, 2 * width), BF),
@@ -436,9 +482,9 @@
             pltpu.VMEM((tok // HALF_WIN, HALF_WIN, 3 * HALF_WIN), F32),
             pltpu.SemaphoreType.DMA((4,)),
         ],
-        compiler_params=params(48),
+        compiler_params=params(32),
         cost_estimate=cost(12 * 10**9, 5 * 10**6, 10**7),
-    )(low, doc_hidden, high, flag.astype(F32), w_keyval, w_query, w_out, x_query)
+    )(low, doc_hidden, high, token_ids, *map(pinned, (w_keyval, w_query, w_out, x_query)))
 
     lines = [[GRID * z + x for x in range(GRID)] for z in range(GRID)]
 
@@ -473,15 +519,16 @@
             functools.partial(cross_kernel, heads, count),
             name="cross",
             out_shape=outs,
-            in_specs=[smem()] + [vmem()] * (2 + GRID + len(extra)),
+            in_specs=[smem()] + [vmem()] * 2 + [hbm()] * GRID + [vmem()] * len(extra),
             out_specs=jax.tree.map(lambda _: vmem(), outs),
             scratch_shapes=[
                 pltpu.VMEM((len(heads), GRID * held, LANES), BF),
                 pltpu.VMEM((len(heads), GRID * held, LANES), BF),
                 pltpu.VMEM((2, tok, GRID * held), BF),
                 pltpu.VMEM((8, GRID * held), F32),
+                pltpu.SemaphoreType.DMA((len(heads) * GRID,)),
             ],
-            compiler_params=params(40),
+            compiler_params=params(24),
             cost_estimate=cost(len(heads) * 10**10, 5 * 10**6, 4 * 10**6),
         )(where, pos, queries, *parts, *extra)
 
@@ -491,16 +538,16 @@
         (),
         (jax.ShapeDtypeStruct((GRID, tok, LANES), BF), jax.ShapeDtypeStruct((8, GRID * held), F32)),
     )
-    out = cross((1, 2), rest, (mass, out), jax.ShapeDtypeStruct((GRID, tok + 16, 2 * LANES), BF))
+    out = cross((1, 2), rest, (mass, out), jax.ShapeDtypeStruct((GRID, message, LANES), BF))
     out = across(out)
 
     mass = pl.pallas_call(
         mass_kernel,
         name="mass",
-        grid=(1,),
         out_shape=jax.ShapeDtypeStruct((1, padded), F32),
-        in_specs=[pl.BlockSpec((GRID, 16, 2 * LANES), lambda i: (0, tok // 16, 0))],
-        out_specs=pl.BlockSpec((1, padded), lambda i: (0, 0)),
+        in_specs=[hbm()],
+        out_specs=vmem(),
+        scratch_shapes=[pltpu.VMEM((GRID, 16, LANES), BF), pltpu.SemaphoreType.DMA],
         cost_estimate=cost(10**5, 0, 10**5),
     )(out)
     one, two, three = turns(mass)

time: 141 us -> 131 us (0.929)
  blocking collectives: 26.6 us -> 13.8 us
  waiting for transfers between devices: 7.5 us -> 17 us
  local copies, waits for them, and re-layouts: 12.1 us -> 5.05 us
  Pallas kernels: 53.5 us -> 55.1 us
    all_gather x1 -> x0, blocking collectives: 12.1 us -> none  [local(): all_codes = lax.all_gather(shortlist, 'doc', axis=0, tiled=False)]
    unnamed x28 -> x18, local copies, waits for them, and re-layouts: 10.3 us -> 3.86 us
    all_to_all x0 -> x1, waiting for transfers between devices: none -> 5.26 us  [local(): lax.all_to_all(asked, 'doc', split_axis=0, concat_axis=0, tiled=True)]
    all_to_all x0 -> x1, starting transfers between devices: none -> 4.48 us  [local(): lax.all_to_all(asked, 'doc', split_axis=0, concat_axis=0, tiled=True)]
    ppermute x9, starting transfers between devices: 16.1 us -> 11.7 us  [turns(): parts.append(lax.ppermute(block, 'seq', pairs))]
    ppermute x9, waiting for transfers between devices: 7.49 us -> 10.2 us  [turns(): parts.append(lax.ppermute(block, 'seq', pairs))]
    all_to_all x1, waiting for transfers between devices: 0.01 us -> 1.52 us  [local(): lax.all_to_all(send.reshape(devices, DESC, 3 * LANES), ('doc', 'seq'), sp...]
  transfers between devices with their start and end apart: 13 -> 14, of which waited for: 4 -> 6; matrix products, arithmetic and copies ran while one was open for 1% -> 0% of each run, Pallas kernels for 24% -> 27%
where the time goes in v3:
time: 131 us; the launch traced here: 129 us
  Pallas kernels  55.1 us (42%)
  starting transfers between devices  35.3 us (27%)
  waiting for transfers between devices  17 us (13%)
  blocking collectives  13.8 us (11%)
  local copies, waits for them, and re-layouts  5.05 us (4%)
  between operations  1.47 us (1%)
  other arithmetic  1.35 us (1%)
    pallas_call x2, Pallas kernels, cross(): pl.pallas_call(functools.partial(cross_kernel, heads, count), name='cross...  29.1 us
    all_to_all x1, blocking collectives, across(): lax.all_to_all(block, 'seq', split_axis=0, concat_axis=0, axis_index_grou...  13.8 us
    pallas_call x1, Pallas kernels, local(): pl.pallas_call(window_kernel, name='window', out_shape=(jax.ShapeDtypeStr...  13.6 us
    ppermute x9, starting transfers between devices, turns(): parts.append(lax.ppermute(block, 'seq', pairs))  11.7 us
    ppermute x9, waiting for transfers between devices, turns(): parts.append(lax.ppermute(block, 'seq', pairs))  10.2 us
    all_to_all x1, starting transfers between devices, local(): lax.all_to_all(send.reshape(devices, DESC, 3 * LANES), ('doc', 'seq'), sp...  8.47 us
    pallas_call x1, Pallas kernels, local(): pl.pallas_call(functools.partial(route_kernel, count, code_dev, devices),...  8.36 us
    all_to_all x1, waiting for transfers between devices, local(): lax.all_to_all(asked, 'doc', split_axis=0, concat_axis=0, tiled=True)  5.26 us
  transfers between devices with their start and end apart: 14, of which 6 were waited for; matrix products, arithmetic and copies ran while one was open for 0% of the time, Pallas kernels for 27%

profile of v3, /device:TPU:2, one launch (start us, length us, event | category | flops | bytes accessed | tf_op | source)
XLA Modules:
  0.0 129.1 jit_solution(2065276683789975282)
XLA Ops:
  0.6 0.7 reduce
  1.3 0.6 broadcast_in_dim.12
  1.9 0.0 copy-start.1
  1.9 1.1 copy-done.1
  3.1 0.0 copy-start.3
  3.1 0.7 copy-done.3
  3.8 0.1 halo.1
  3.8 3.4 %collective-permute-start = (bf16[264,768]{1,0:T(8,128)(2,1)S(1)}, bf16[264,768]{1,0:T(8,128)(2,1)S(1)}, u32[]{:S(2)}, u32[]{:S(2)}) collective-permute-start(bf16[264,768]{1,0:T(8,128)(2,1)S(1)} %get-tuple-element.18), channel_id=1, source_target_pairs={{0,1},{1,2},{2,3},{3,4},{4,5},{5,6},{6,7},{7,8},{8,9},{9,10},{10,1... | collective-permute-start | bytes 1216520 | tf_op jit(solution)/shard_map/ppermute | solution.py:434
  7.2 2.5 %collective-permute-start.1 = (bf16[264,768]{1,0:T(8,128)(2,1)S(1)}, bf16[264,768]{1,0:T(8,128)(2,1)S(1)}, u32[]{:S(2)}, u32[]{:S(2)}) collective-permute-start(bf16[264,768]{1,0:T(8,128)(2,1)S(1)} %get-tuple-element.19), channel_id=1, source_target_pairs={{1,0},{2,1},{3,2},{4,3},{5,4},{6,5},{7,6},{8,7},{9,8},{10,9},{11,1... | collective-permute-start | bytes 1216520 | tf_op jit(solution)/shard_map/ppermute | solution.py:435
  9.7 4.5 %all-to-all-start = ((s32[8,1,320]{2,1,0:T(1,128)}), s32[8,1,320]{2,1,0:T(1,128)S(1)}, u32[]{:S(2)}, u32[]{:S(2)}) async-start(s32[8,1,320]{2,1,0:T(1,128)} %broadcast_in_dim.12), calls=%async_computation | async-start | bytes 24576 | tf_op jit(solution)/shard_map/all_to_all | solution.py:424
  14.2 0.1 pad_add_fusion.where_ref
  14.3 5.3 %all-to-all-done.codes_ref = s32[8,1,320]{2,1,0:T(1,128)S(1)} async-done(((s32[8,1,320]{2,1,0:T(1,128)}), s32[8,1,320]{2,1,0:T(1,128)S(1)}, u32[]{:S(2)}, u32[]{:S(2)}) %all-to-all-start) | async-done | bytes 10272 | tf_op jit(solution)/shard_map/all_to_all | solution.py:424
  19.5 8.4 %route.1 = (bf16[32,4,8,384]{3,2,1,0:T(8,128)(2,1)}, s32[1,1024]{1,0:T(1,128)S(1)}, s32[1,384]{1,0:T(1,128)S(1)}) custom-call(s32[3]{0:T(128)S(1)} %pad_add_fusion.where_ref, s32[8,1,320]{2,1,0:T(1,128)S(1)} %all-to-all-done.codes_ref, s32[288,128]{1,0:T(8,128)} %bitcast.12, bf16[288,2,8,768]{3,2,1,0:T(8,128)(2,1)} %cache_ref.1), custom_call_target="tpu_custom_call" | custom-call | flops 1000000000 | bytes 2000000 | tf_op jit(solution)/shard_map/route/pallas_call | solution.py:437
  27.9 0.0 copy-start.2
  27.9 0.0 copy-start.4
  27.9 8.5 %all-to-all-start.2 = ((bf16[128,8,384]{2,1,0:T(8,128)(2,1)}), bf16[128,8,384]{2,1,0:T(8,128)(2,1)S(1)}, u32[]{:S(2)}, u32[]{:S(2)}) async-start(bf16[128,8,384]{2,1,0:T(8,128)(2,1)} %bitcast.5), calls=%async_computation.2 | async-start | bytes 1572864 | tf_op jit(solution)/shard_map/all_to_all | solution.py:459
  36.4 0.0 collective-permute-done.low_ref
  36.4 0.0 collective-permute-done.1.high_ref
  36.4 0.0 copy-done.2
  36.4 0.0 copy-done.4
  36.4 13.6 %window.1 = (bf16[512,768]{1,0:T(8,128)(2,1)S(1)}, bf16[4,784,128]{2,1,0:T(8,128)(2,1)}) custom-call(bf16[264,768]{1,0:T(8,128)(2,1)S(1)} %collective-permute-done.low_ref, bf16[512,768]{1,0:T(8,128)(2,1)S(1)} %bitcast.10, bf16[264,768]{1,0:T(8,128)(2,1)S(1)} %collective-permute-done.1.high_ref, s32[1,512]{1,0:T(1,128)S(1)} %copy-done.4, ...), custom_call_target="tpu_custom_call" | custom-call | flops 12000000000 | bytes 10000000 | tf_op jit(solution)/shard_map/window/pallas_call | solution.py:463
  50.0 0.0 copy-start.6
  50.0 0.9 copy-done.6
  50.9 1.5 %all-to-all-done.2 = bf16[128,8,384]{2,1,0:T(8,128)(2,1)S(1)} async-done(((bf16[128,8,384]{2,1,0:T(8,128)(2,1)}), bf16[128,8,384]{2,1,0:T(8,128)(2,1)S(1)}, u32[]{:S(2)}, u32[]{:S(2)}) %all-to-all-start.2) | async-done | bytes 786464 | tf_op jit(solution)/shard_map/all_to_all | solution.py:459
  52.4 4.8 %all-to-all-start.1 = ((bf16[4,784,128]{2,1,0:T(8,128)(2,1)}), bf16[4,784,128]{2,1,0:T(8,128)(2,1)S(1)}, u32[]{:S(2)}, u32[]{:S(2)}) async-start(bf16[4,784,128]{2,1,0:T(8,128)(2,1)} %get-tuple-element.23), calls=%async_computation.1 | async-start | bytes 1605632 | tf_op jit(solution)/shard_map/all_to_all | solution.py:492
  57.3 0.8 compact.1
  58.1 0.9 collective-permute-start.5
  59.0 2.5 %collective-permute-start.6 = (bf16[640,128]{1,0:T(8,128)(2,1)S(1)}, bf16[640,128]{1,0:T(8,128)(2,1)S(1)}, u32[]{:S(2)}, u32[]{:S(2)}) collective-permute-start(bf16[640,128]{1,0:T(8,128)(2,1)S(1)} %get-tuple-element.27.refs_0_), channel_id=1, source_target_pairs={{0,8},{1,9},{2,10},{3,11},{4,12},{5,13},{6,14},{7,15},{8,0},{9,1},... | collective-permute-start | bytes 491528 | tf_op jit(solution)/shard_map/ppermute | solution.py:512
  61.5 1.2 collective-permute-start.7
  62.6 0.8 collective-permute-start.2
  63.5 1.1 collective-permute-start.3
  64.6 3.7 %collective-permute-done.5.refs_1_ = bf16[640,128]{1,0:T(8,128)(2,1)S(1)} collective-permute-done((bf16[640,128]{1,0:T(8,128)(2,1)S(1)}, bf16[640,128]{1,0:T(8,128)(2,1)S(1)}, u32[]{:S(2)}, u32[]{:S(2)}) %collective-permute-start.5) | collective-permute-done | bytes 163872 | tf_op jit(solution)/shard_map/ppermute | solution.py:512
  68.2 0.0 collective-permute-start.4
  68.2 1.8 %collective-permute-done.6.refs_2_ = bf16[640,128]{1,0:T(8,128)(2,1)S(1)} collective-permute-done((bf16[640,128]{1,0:T(8,128)(2,1)S(1)}, bf16[640,128]{1,0:T(8,128)(2,1)S(1)}, u32[]{:S(2)}, u32[]{:S(2)}) %collective-permute-start.6) | collective-permute-done | bytes 163872 | tf_op jit(solution)/shard_map/ppermute | solution.py:512
  70.1 3.8 %collective-permute-done.7.refs_3_ = bf16[640,128]{1,0:T(8,128)(2,1)S(1)} collective-permute-done((bf16[640,128]{1,0:T(8,128)(2,1)S(1)}, bf16[640,128]{1,0:T(8,128)(2,1)S(1)}, u32[]{:S(2)}, u32[]{:S(2)}) %collective-permute-start.7) | collective-permute-done | bytes 163872 | tf_op jit(solution)/shard_map/ppermute | solution.py:512
  73.9 0.0 all-to-all-done.1.query_ref
  73.9 10.2 %cross.2 = (bf16[4,512,128]{2,1,0:T(8,128)(2,1)S(1)}, f32[8,2560]{1,0:T(8,128)S(1)}) custom-call(s32[3]{0:T(128)S(1)} %pad_add_fusion.where_ref, s32[1,384]{1,0:T(1,128)S(1)} %get-tuple-element.22.pos_ref, bf16[4,784,128]{2,1,0:T(8,128)(2,1)S(1)} %all-to-all-done.1.query_ref, bf16[640,128]{1,0:T(8,128)(2,1)S(1)} %get-tuple-element.27.refs_0_, ...), custom_call_target="tpu_custom_call" | custom-call | flops 10000000000 | bytes 4000000 | tf_op jit(solution)/shard_map/cross/pallas_call | solution.py:518
  84.1 0.0 collective-permute-done.2.refs_1_
  84.1 0.0 collective-permute-done.3.refs_2_
  84.1 0.0 collective-permute-done.4.refs_3_
  84.1 18.9 %cross.3 = bf16[4,784,128]{2,1,0:T(8,128)(2,1)S(1)} custom-call(s32[3]{0:T(128)S(1)} %pad_add_fusion.where_ref, s32[1,384]{1,0:T(1,128)S(1)} %get-tuple-element.22.pos_ref, bf16[4,784,128]{2,1,0:T(8,128)(2,1)S(1)} %all-to-all-done.1.query_ref, bf16[640,256]{1,0:T(8,128)(2,1)S(1)} %get-tuple-element.26.refs_0_, ...), custom_call_target="tpu_custom_call" | custom-call | flops 20000000000 | bytes 4000000 | tf_op jit(solution)/shard_map/cross/pallas_call | solution.py:518
  103.0 0.0 copy-start.5
  103.1 0.0 copy-start.7
  103.1 13.8 %all_to_all.20.got_ref.out_hbm = bf16[4,784,128]{2,1,0:T(8,128)(2,1)} all-to-all(bf16[4,784,128]{2,1,0:T(8,128)(2,1)S(1)} %cross.3), channel_id=1, replica_groups={{0,1,2,3},{4,5,6,7},{8,9,10,11},{12,13,14,15},{16,17,18,19},{20,21,22,2..., dimensions={0} | all-to-all | bytes 1605632 | tf_op jit(solution)/shard_map/all_to_all | solution.py:492
  116.8 1.3 %mass.1 = f32[1,384]{1,0:T(1,128)} custom-call(bf16[4,784,128]{2,1,0:T(8,128)(2,1)} %all_to_all.20.got_ref.out_hbm), custom_call_target="tpu_custom_call" | custom-call | flops 100000 | bytes 100000 | tf_op jit(solution)/shard_map/mass/pallas_call | solution.py:544
  118.1 2.4 %collective-permute-start.9 = (f32[1,384]{1,0:T(1,128)}, f32[1,384]{1,0:T(1,128)S(1)}, u32[]{:S(2)}, u32[]{:S(2)}) collective-permute-start(f32[1,384]{1,0:T(1,128)} %mass.1), channel_id=1, source_target_pairs={{0,4},{1,5},{2,6},{3,7},{4,8},{5,9},{6,10},{7,11},{8,12},{9,13},{1... | collective-permute-start | bytes 4616 | tf_op jit(solution)/shard_map/ppermute | solution.py:512
  120.6 1.4 %collective-permute-start.10 = (f32[1,384]{1,0:T(1,128)}, f32[1,384]{1,0:T(1,128)S(1)}, u32[]{:S(2)}, u32[]{:S(2)}) collective-permute-start(f32[1,384]{1,0:T(1,128)} %mass.1), channel_id=1, source_target_pairs={{0,12},{1,13},{2,14},{3,15},{4,0},{5,1},{6,2},{7,3},{8,4},{9,5},{1... | collective-permute-start | bytes 4616 | tf_op jit(solution)/shard_map/ppermute | solution.py:512
  122.0 1.4 %collective-permute-start.8 = (f32[1,384]{1,0:T(1,128)}, f32[1,384]{1,0:T(1,128)S(1)}, u32[]{:S(2)}, u32[]{:S(2)}) collective-permute-start(f32[1,384]{1,0:T(1,128)} %mass.1), channel_id=1, source_target_pairs={{0,8},{1,9},{2,10},{3,11},{4,12},{5,13},{6,14},{7,15},{8,0},{9,1},... | collective-permute-start | bytes 4616 | tf_op jit(solution)/shard_map/ppermute | solution.py:512
  123.4 0.0 copy-done.5
  123.4 0.0 copy-done.7
  123.4 0.0 copy-start
  123.4 1.1 copy-done
  124.5 0.0 copy-start.8
  124.5 1.9 %final.1 = bf16[512,768]{1,0:T(8,128)(2,1)} custom-call(bf16[512,768]{1,0:T(8,128)(2,1)S(1)} %copy-done.7, bf16[4,784,128]{2,1,0:T(8,128)(2,1)S(1)} %copy-done, bf16[768,768]{1,0:T(8,128)(2,1)S(1)} %copy-done.5), custom_call_target="tpu_custom_call" | custom-call | flops 1000000000 | bytes 4000000 | tf_op jit(solution)/shard_map/final/pallas_call | solution.py:558
  126.4 0.0 collective-permute-done.9
  126.4 0.0 collective-permute-done.10
  126.4 0.9 collective-permute-done.8
  127.3 0.0 copy-done.8
  127.3 0.6 slice.9
  128.5 0.6 fusion
  (1 shorter events, 0.0 us)
Async XLA Ops:
  1.9 1.1 copy-start.1
  3.1 0.7 copy-start.3
  3.8 32.6 %collective-permute-start = (bf16[264,768]{1,0:T(8,128)(2,1)S(1)}, bf16[264,768]{1,0:T(8,128)(2,1)S(1)}, u32[]{:S(2)}, u32[]{:S(2)}) collective-permute-start(bf16[264,768]{1,0:T(8,128)(2,1)S(1)} %get-tuple-element.18), channel_id=1, source_target_pairs={{0,1},{1,2},{2,3},{3,4},{4,5},{5,6},{6,7},{7,8},{8,9},{9,10},{10,1... | collective-permute-start | bytes 1216520 | tf_op jit(solution)/shard_map/ppermute | solution.py:434
  7.2 29.2 %collective-permute-start.1 = (bf16[264,768]{1,0:T(8,128)(2,1)S(1)}, bf16[264,768]{1,0:T(8,128)(2,1)S(1)}, u32[]{:S(2)}, u32[]{:S(2)}) collective-permute-start(bf16[264,768]{1,0:T(8,128)(2,1)S(1)} %get-tuple-element.19), channel_id=1, source_target_pairs={{1,0},{2,1},{3,2},{4,3},{5,4},{6,5},{7,6},{8,7},{9,8},{10,9},{11,1... | collective-permute-start | bytes 1216520 | tf_op jit(solution)/shard_map/ppermute | solution.py:435
  9.7 9.8 %all-to-all-start = ((s32[8,1,320]{2,1,0:T(1,128)}), s32[8,1,320]{2,1,0:T(1,128)S(1)}, u32[]{:S(2)}, u32[]{:S(2)}) async-start(s32[8,1,320]{2,1,0:T(1,128)} %broadcast_in_dim.12), calls=%async_computation | async-start | bytes 24576 | tf_op jit(solution)/shard_map/all_to_all | solution.py:424
  27.9 8.5 %copy-start.2 = (bf16[1,512,768]{2,1,0:T(8,128)(2,1)S(1)}, bf16[1,512,768]{2,1,0:T(8,128)(2,1)}, u32[]{:S(2)}) copy-start(bf16[1,512,768]{2,1,0:T(8,128)(2,1)} %param.10) | copy-start | bytes 2359300
  27.9 8.5 %copy-start.4 = (s32[1,512]{1,0:T(1,128)S(1)}, s32[1,512]{1,0:T(1,128)}, u32[]{:S(2)}) copy-start(s32[1,512]{1,0:T(1,128)} %tokens_ref.1) | copy-start | bytes 6148
  27.9 24.5 %all-to-all-start.2 = ((bf16[128,8,384]{2,1,0:T(8,128)(2,1)}), bf16[128,8,384]{2,1,0:T(8,128)(2,1)S(1)}, u32[]{:S(2)}, u32[]{:S(2)}) async-start(bf16[128,8,384]{2,1,0:T(8,128)(2,1)} %bitcast.5), calls=%async_computation.2 | async-start | bytes 1572864 | tf_op jit(solution)/shard_map/all_to_all | solution.py:459
  50.0 0.9 copy-start.6
  52.4 21.5 %all-to-all-start.1 = ((bf16[4,784,128]{2,1,0:T(8,128)(2,1)}), bf16[4,784,128]{2,1,0:T(8,128)(2,1)S(1)}, u32[]{:S(2)}, u32[]{:S(2)}) async-start(bf16[4,784,128]{2,1,0:T(8,128)(2,1)} %get-tuple-element.23), calls=%async_computation.1 | async-start | bytes 1605632 | tf_op jit(solution)/shard_map/all_to_all | solution.py:492
  58.1 10.1 %collective-permute-start.5 = (bf16[640,128]{1,0:T(8,128)(2,1)S(1)}, bf16[640,128]{1,0:T(8,128)(2,1)S(1)}, u32[]{:S(2)}, u32[]{:S(2)}) collective-permute-start(bf16[640,128]{1,0:T(8,128)(2,1)S(1)} %get-tuple-element.27.refs_0_), channel_id=1, source_target_pairs={{0,4},{1,5},{2,6},{3,7},{4,8},{5,9},{6,10},{7,11},{8,12},{9,13},{1... | collective-permute-start | bytes 491528 | tf_op jit(solution)/shard_map/ppermute | solution.py:512
  59.0 11.1 %collective-permute-start.6 = (bf16[640,128]{1,0:T(8,128)(2,1)S(1)}, bf16[640,128]{1,0:T(8,128)(2,1)S(1)}, u32[]{:S(2)}, u32[]{:S(2)}) collective-permute-start(bf16[640,128]{1,0:T(8,128)(2,1)S(1)} %get-tuple-element.27.refs_0_), channel_id=1, source_target_pairs={{0,8},{1,9},{2,10},{3,11},{4,12},{5,13},{6,14},{7,15},{8,0},{9,1},... | collective-permute-start | bytes 491528 | tf_op jit(solution)/shard_map/ppermute | solution.py:512
  61.5 12.4 %collective-permute-start.7 = (bf16[640,128]{1,0:T(8,128)(2,1)S(1)}, bf16[640,128]{1,0:T(8,128)(2,1)S(1)}, u32[]{:S(2)}, u32[]{:S(2)}) collective-permute-start(bf16[640,128]{1,0:T(8,128)(2,1)S(1)} %get-tuple-element.27.refs_0_), channel_id=1, source_target_pairs={{0,12},{1,13},{2,14},{3,15},{4,0},{5,1},{6,2},{7,3},{8,4},{9,5},{1... | collective-permute-start | bytes 491528 | tf_op jit(solution)/shard_map/ppermute | solution.py:512
  62.6 21.4 %collective-permute-start.2 = (bf16[640,256]{1,0:T(8,128)(2,1)S(1)}, bf16[640,256]{1,0:T(8,128)(2,1)S(1)}, u32[]{:S(2)}, u32[]{:S(2)}) collective-permute-start(bf16[640,256]{1,0:T(8,128)(2,1)S(1)} %get-tuple-element.26.refs_0_), channel_id=1, source_target_pairs={{0,4},{1,5},{2,6},{3,7},{4,8},{5,9},{6,10},{7,11},{8,12},{9,13},{1... | collective-permute-start | bytes 983048 | tf_op jit(solution)/shard_map/ppermute | solution.py:512
  63.5 20.6 %collective-permute-start.3 = (bf16[640,256]{1,0:T(8,128)(2,1)S(1)}, bf16[640,256]{1,0:T(8,128)(2,1)S(1)}, u32[]{:S(2)}, u32[]{:S(2)}) collective-permute-start(bf16[640,256]{1,0:T(8,128)(2,1)S(1)} %get-tuple-element.26.refs_0_), channel_id=1, source_target_pairs={{0,8},{1,9},{2,10},{3,11},{4,12},{5,13},{6,14},{7,15},{8,0},{9,1},... | collective-permute-start | bytes 983048 | tf_op jit(solution)/shard_map/ppermute | solution.py:512
  68.2 15.9 %collective-permute-start.4 = (bf16[640,256]{1,0:T(8,128)(2,1)S(1)}, bf16[640,256]{1,0:T(8,128)(2,1)S(1)}, u32[]{:S(2)}, u32[]{:S(2)}) collective-permute-start(bf16[640,256]{1,0:T(8,128)(2,1)S(1)} %get-tuple-element.26.refs_0_), channel_id=1, source_target_pairs={{0,12},{1,13},{2,14},{3,15},{4,0},{5,1},{6,2},{7,3},{8,4},{9,5},{1... | collective-permute-start | bytes 983048 | tf_op jit(solution)/shard_map/ppermute | solution.py:512
  103.0 20.3 %copy-start.5 = (bf16[768,768]{1,0:T(8,128)(2,1)S(1)}, bf16[768,768]{1,0:T(8,128)(2,1)}, u32[]{:S(2)}) copy-start(bf16[768,768]{1,0:T(8,128)(2,1)} %weight_ref.1) | copy-start | bytes 3538948
  103.1 20.3 %copy-start.7 = (bf16[512,768]{1,0:T(8,128)(2,1)S(1)}, bf16[512,768]{1,0:T(8,128)(2,1)}, u32[]{:S(2)}) copy-start(bf16[512,768]{1,0:T(8,128)(2,1)} %copy-done.6) | copy-start | bytes 2359300
  118.1 8.2 %collective-permute-start.9 = (f32[1,384]{1,0:T(1,128)}, f32[1,384]{1,0:T(1,128)S(1)}, u32[]{:S(2)}, u32[]{:S(2)}) collective-permute-start(f32[1,384]{1,0:T(1,128)} %mass.1), channel_id=1, source_target_pairs={{0,4},{1,5},{2,6},{3,7},{4,8},{5,9},{6,10},{7,11},{8,12},{9,13},{1... | collective-permute-start | bytes 4616 | tf_op jit(solution)/shard_map/ppermute | solution.py:512
  120.6 5.8 %collective-permute-start.10 = (f32[1,384]{1,0:T(1,128)}, f32[1,384]{1,0:T(1,128)S(1)}, u32[]{:S(2)}, u32[]{:S(2)}) collective-permute-start(f32[1,384]{1,0:T(1,128)} %mass.1), channel_id=1, source_target_pairs={{0,12},{1,13},{2,14},{3,15},{4,0},{5,1},{6,2},{7,3},{8,4},{9,5},{1... | collective-permute-start | bytes 4616 | tf_op jit(solution)/shard_map/ppermute | solution.py:512
  122.0 5.3 %collective-permute-start.8 = (f32[1,384]{1,0:T(1,128)}, f32[1,384]{1,0:T(1,128)S(1)}, u32[]{:S(2)}, u32[]{:S(2)}) collective-permute-start(f32[1,384]{1,0:T(1,128)} %mass.1), channel_id=1, source_target_pairs={{0,8},{1,9},{2,10},{3,11},{4,12},{5,13},{6,14},{7,15},{8,0},{9,1},... | collective-permute-start | bytes 4616 | tf_op jit(solution)/shard_map/ppermute | solution.py:512
  123.4 1.1 copy-start
  124.5 2.8 %copy-start.8 = (f32[1,384]{1,0:T(1,128)S(1)}, f32[1,384]{1,0:T(1,128)}, u32[]{:S(2)}) copy-start(f32[1,384]{1,0:T(1,128)} %mass.1) | copy-start | bytes 4612

commit v4 on v3

--- a/solution.py
+++ b/solution.py
@@ -57,14 +57,15 @@
 
 
 def split_table(table):
-    high = table >> 8
-    return jnp.concatenate([high, table - (high << 8)], axis=1).astype(F32).astype(BF)
+    wide = jnp.transpose(table.astype(F32))
+    high = jnp.floor(wide * (1.0 / 256.0))
+    return jnp.concatenate([high, wide - high * 256.0], axis=0).astype(BF)
 
 
 def look_up(code, table):
     n = code.shape[1]
-    picks = (iota((table.shape[0], n), 0) == (code >> 7)).astype(F32).astype(BF)
-    found = lax.dot_general(table, picks, (((0,), (0,)), ((), ())), preferred_element_type=F32)
+    picks = (iota((table.shape[1], n), 0) == (code >> 7)).astype(F32).astype(BF)
+    found = dot(table, picks)
     here = iota((LANES, n), 0) == (code & 127)
     value = jnp.where(here, found[:LANES] * 256.0 + found[LANES:], 0.0)
     return jnp.sum(value, axis=0, keepdims=True)
@@ -92,10 +93,11 @@
 ):
     docs = codes_ref.shape[0]
     n = line.shape[1]
-    fetch = pltpu.make_async_copy(table_ref, table, sem.at[0])
+    fetch = pltpu.make_async_copy(table_ref, table.at[pl.ds(0, table_ref.shape[0]), :], sem.at[0])
     fetch.start()
     upper = upper_ones(n)
     lane = iota((1, LANES), 1)
+    table[table_ref.shape[0] :, :] = jnp.zeros((table.shape[0] - table_ref.shape[0], LANES), I32)
     line[...] = jnp.full(line.shape, -1, I32)
     for d in range(docs):
         line[d : d + 1, :count] = codes_ref[d]
@@ -270,7 +272,7 @@
     kv_refs, refs = refs[:GRID], refs[GRID:]
     last = 2 in heads
     if last:
-        before_ref, earlier_ref, out_ref, keys, values, expds, total, sems = refs
+        before_ref, earlier_ref, out_ref, score_ref, keys, values, expds, total, sems = refs
     else:
         out_ref, mass_ref, keys, values, expds, total, sems = refs
     held = kv_refs[0].shape[0]
@@ -359,12 +361,7 @@
     for g in range(1, groups):
         tokens = tokens + tokens_of(g)
     score = jnp.where(iota((1, padded), 1) == count, tokens, score)
-    tail = jnp.zeros((16, LANES), F32)
-    for k, part in enumerate(thirds(score)):
-        for j in range(padded // LANES):
-            tail = jnp.where(iota(tail.shape, 0) == 3 * j + k, part[:, j * LANES : (j + 1) * LANES], tail)
-    for g in range(groups):
-        out_ref[g, tok + half :, :] = tail.astype(BF)
+    score_ref[...] = score
 
 
 def thirds(value):
@@ -373,23 +370,21 @@
     return first, second, value - first - second
 
 
-def mass_kernel(out_hbm, line_ref, tail, sem):
-    groups, size, _ = tail.shape
-    copy = pltpu.make_async_copy(out_hbm.at[:, pl.ds(out_hbm.shape[1] - size, size), :], tail, sem)
-    copy.start()
-    copy.wait()
-    total = jnp.sum(tail[...].astype(F32), axis=0)
-    for j in range(line_ref.shape[1] // LANES):
-        line_ref[:, j * LANES : (j + 1) * LANES] = jnp.sum(total[3 * j : 3 * j + 3, :], axis=0, keepdims=True)
-
-
-def final_kernel(middle_ref, got_ref, weight_ref, out_ref):
+def final_kernel(middle_ref, got_hbm, weight_hbm, out_ref, got_ref, weight_ref, sems):
     tok = middle_ref.shape[0]
+    groups = got_ref.shape[0]
+    whole = pltpu.make_async_copy(weight_hbm, weight_ref, sems.at[groups])
+    whole.start()
+    copies = [pltpu.make_async_copy(got_hbm.at[g], got_ref.at[g], sems.at[g]) for g in range(groups)]
+    for copy in copies:
+        copy.start()
+    whole.wait()
     half = tok // 2
     size = 3 * HALF
     low = iota((half, LANES), 1) < HALF
     acc = middle_ref[...].astype(F32)
-    for g in range(got_ref.shape[0]):
+    for g in range(groups):
+        copies[g].wait()
         at = g * size
         heads = [weight_ref[at + k * HALF : at + (k + 1) * HALF, :] for k in (1, 0, 2, 2)]
         packed = got_ref[g, tok : tok + half, :]
@@ -445,7 +440,7 @@
         in_specs=[smem(), vmem(), hbm(), hbm()],
         out_specs=(vmem(),) * 3,
         scratch_shapes=[
-            pltpu.VMEM(table.shape, I32),
+            pltpu.VMEM((-(-table.shape[0] // LANES) * LANES, LANES), I32),
             pltpu.VMEM((docs * GRID, 2, DESC, width), BF),
             pltpu.VMEM((docs, padded), I32),
             pltpu.VMEM((docs, LANES), I32),
@@ -538,20 +533,19 @@
         (),
         (jax.ShapeDtypeStruct((GRID, tok, LANES), BF), jax.ShapeDtypeStruct((8, GRID * held), F32)),
     )
-    out = cross((1, 2), rest, (mass, out), jax.ShapeDtypeStruct((GRID, message, LANES), BF))
+    out, score = cross(
+        (1, 2),
+        rest,
+        (mass, out),
+        (jax.ShapeDtypeStruct((GRID, message, LANES), BF), jax.ShapeDtypeStruct((1, padded), F32)),
+    )
+
+    across_x = [[(i, GRID * (i // GRID) + (i + shift) % GRID) for i in range(seq_count)] for shift in range(1, GRID)]
+    one, two, three = [lax.ppermute(score, "seq", pairs) for pairs in across_x]
+    score = (score + two) + (one + three)
+    one, two, three = turns(score)
+    sums = (score + two) + (one + three)
     out = across(out)
-
-    mass = pl.pallas_call(
-        mass_kernel,
-        name="mass",
-        out_shape=jax.ShapeDtypeStruct((1, padded), F32),
-        in_specs=[hbm()],
-        out_specs=vmem(),
-        scratch_shapes=[pltpu.VMEM((GRID, 16, LANES), BF), pltpu.SemaphoreType.DMA],
-        cost_estimate=cost(10**5, 0, 10**5),
-    )(out)
-    one, two, three = turns(mass)
-    sums = (mass + two) + (one + three)
     tokens = sums[:, count : count + 1] * (1.0 / GRID)
     cand_score = count * sums[:, :count] / (HEADS * tokens)
 
@@ -559,11 +553,16 @@
         final_kernel,
         name="final",
         out_shape=jax.ShapeDtypeStruct((tok, width), BF),
-        in_specs=[vmem()] * 3,
+        in_specs=[vmem(), hbm(), hbm()],
         out_specs=vmem(),
+        scratch_shapes=[
+            pltpu.VMEM((GRID, message, LANES), BF),
+            pltpu.VMEM((width, width), BF),
+            pltpu.SemaphoreType.DMA((GRID + 1,)),
+        ],
         compiler_params=params(16),
         cost_estimate=cost(10**9, 0, 4 * 10**6),
-    )(middle, out, x_out)
+    )(middle, out, pinned(x_out))
     return (refined[None], cand_score)
 
 

time: 131 us -> 129 us (0.985)
  blocking collectives: 13.8 us -> 0 us
  starting transfers between devices: 35.3 us -> 44.9 us
  waiting for transfers between devices: 17 us -> 19.8 us
  Pallas kernels: 55.1 us -> 56.6 us
    all_to_all x1 -> x0, blocking collectives: 13.8 us -> none  [across(): lax.all_to_all(block, 'seq', split_axis=0, concat_axis=0, axis_index_grou...]
    all_to_all x1 -> x2, starting transfers between devices: 4.83 us -> 9.75 us  [across(): lax.all_to_all(block, 'seq', split_axis=0, concat_axis=0, axis_index_grou...]
    ppermute x0 -> x3, starting transfers between devices: none -> 4.16 us  [local(): one, two, three = [lax.ppermute(score, 'seq', pairs) for pairs in across_x]]
    ppermute x9, waiting for transfers between devices: 10.2 us -> 13 us  [turns(): parts.append(lax.ppermute(block, 'seq', pairs))]
    pallas_call x1, Pallas kernels: 1.87 us -> 3.84 us  [local(): pl.pallas_call(final_kernel, name='final', out_shape=jax.ShapeDtypeStruct...]
    unnamed x18 -> x12, local copies, waits for them, and re-layouts: 3.86 us -> 2.71 us
  transfers between devices with their start and end apart: 14 -> 18, of which waited for: 6 -> 8; matrix products, arithmetic and copies ran while one was open for 0% -> 1% of each run, Pallas kernels for 27% -> 26%
where the time goes in v4:
time: 129 us; the launch traced here: 128 us
  Pallas kernels  56.6 us (44%)
  starting transfers between devices  44.9 us (35%)
  waiting for transfers between devices  19.8 us (15%)
  local copies, waits for them, and re-layouts  3.9 us (3%)
  between operations  1.65 us (1%)
  other arithmetic  1.36 us (1%)
    pallas_call x2, Pallas kernels, cross(): pl.pallas_call(functools.partial(cross_kernel, heads, count), name='cross...  29.9 us
    pallas_call x1, Pallas kernels, local(): pl.pallas_call(window_kernel, name='window', out_shape=(jax.ShapeDtypeStr...  13.6 us
    ppermute x9, waiting for transfers between devices, turns(): parts.append(lax.ppermute(block, 'seq', pairs))  13 us
    ppermute x9, starting transfers between devices, turns(): parts.append(lax.ppermute(block, 'seq', pairs))  12.2 us
    all_to_all x2, starting transfers between devices, across(): lax.all_to_all(block, 'seq', split_axis=0, concat_axis=0, axis_index_grou...  9.75 us
    all_to_all x1, starting transfers between devices, local(): lax.all_to_all(send.reshape(devices, DESC, 3 * LANES), ('doc', 'seq'), sp...  8.46 us
    pallas_call x1, Pallas kernels, local(): pl.pallas_call(functools.partial(route_kernel, count, code_dev, devices),...  8.37 us
    all_to_all x1, waiting for transfers between devices, local(): lax.all_to_all(asked, 'doc', split_axis=0, concat_axis=0, tiled=True)  5.26 us
  transfers between devices with their start and end apart: 18, of which 8 were waited for; matrix products, arithmetic and copies ran while one was open for 1% of the time, Pallas kernels for 26%

profile of v4, /device:TPU:2, one launch (start us, length us, event | category | flops | bytes accessed | tf_op | source)
XLA Modules:
  0.0 128.2 jit_solution(6301955170405823734)
XLA Ops:
  0.6 0.7 reduce
  1.3 0.6 broadcast_in_dim.12
  1.9 0.0 copy-start
  1.9 1.1 copy-done
  3.1 0.0 copy-start.2
  3.1 0.7 copy-done.2
  3.8 0.1 halo.1
  3.8 3.4 %collective-permute-start = (bf16[264,768]{1,0:T(8,128)(2,1)S(1)}, bf16[264,768]{1,0:T(8,128)(2,1)S(1)}, u32[]{:S(2)}, u32[]{:S(2)}) collective-permute-start(bf16[264,768]{1,0:T(8,128)(2,1)S(1)} %get-tuple-element.20), channel_id=1, source_target_pairs={{0,1},{1,2},{2,3},{3,4},{4,5},{5,6},{6,7},{7,8},{8,9},{9,10},{10,1... | collective-permute-start | bytes 1216520 | tf_op jit(solution)/shard_map/ppermute | solution.py:429
  7.2 2.5 %collective-permute-start.1 = (bf16[264,768]{1,0:T(8,128)(2,1)S(1)}, bf16[264,768]{1,0:T(8,128)(2,1)S(1)}, u32[]{:S(2)}, u32[]{:S(2)}) collective-permute-start(bf16[264,768]{1,0:T(8,128)(2,1)S(1)} %get-tuple-element.21), channel_id=1, source_target_pairs={{1,0},{2,1},{3,2},{4,3},{5,4},{6,5},{7,6},{8,7},{9,8},{10,9},{11,1... | collective-permute-start | bytes 1216520 | tf_op jit(solution)/shard_map/ppermute | solution.py:430
  9.7 4.5 %all-to-all-start = ((s32[8,1,320]{2,1,0:T(1,128)}), s32[8,1,320]{2,1,0:T(1,128)S(1)}, u32[]{:S(2)}, u32[]{:S(2)}) async-start(s32[8,1,320]{2,1,0:T(1,128)} %broadcast_in_dim.12), calls=%async_computation | async-start | bytes 24576 | tf_op jit(solution)/shard_map/all_to_all | solution.py:419
  14.2 0.1 pad_add_fusion.where_ref
  14.2 5.3 %all-to-all-done.codes_ref = s32[8,1,320]{2,1,0:T(1,128)S(1)} async-done(((s32[8,1,320]{2,1,0:T(1,128)}), s32[8,1,320]{2,1,0:T(1,128)S(1)}, u32[]{:S(2)}, u32[]{:S(2)}) %all-to-all-start) | async-done | bytes 10272 | tf_op jit(solution)/shard_map/all_to_all | solution.py:419
  19.5 8.4 %route.1 = (bf16[32,4,8,384]{3,2,1,0:T(8,128)(2,1)}, s32[1,1024]{1,0:T(1,128)S(1)}, s32[1,384]{1,0:T(1,128)S(1)}) custom-call(s32[3]{0:T(128)S(1)} %pad_add_fusion.where_ref, s32[8,1,320]{2,1,0:T(1,128)S(1)} %all-to-all-done.codes_ref, s32[288,128]{1,0:T(8,128)} %bitcast.12, bf16[288,2,8,768]{3,2,1,0:T(8,128)(2,1)} %cache_ref.1), custom_call_target="tpu_custom_call" | custom-call | flops 1000000000 | bytes 2000000 | tf_op jit(solution)/shard_map/route/pallas_call | solution.py:432
  27.9 0.0 copy-start.1
  27.9 0.0 copy-start.3
  27.9 8.5 %all-to-all-start.2 = ((bf16[128,8,384]{2,1,0:T(8,128)(2,1)}), bf16[128,8,384]{2,1,0:T(8,128)(2,1)S(1)}, u32[]{:S(2)}, u32[]{:S(2)}) async-start(bf16[128,8,384]{2,1,0:T(8,128)(2,1)} %bitcast.5), calls=%async_computation.2 | async-start | bytes 1572864 | tf_op jit(solution)/shard_map/all_to_all | solution.py:454
  36.4 0.0 collective-permute-done.low_ref
  36.4 0.0 collective-permute-done.1.high_ref
  36.4 0.0 copy-done.1
  36.4 0.0 copy-done.3
  36.4 13.6 %window.1 = (bf16[512,768]{1,0:T(8,128)(2,1)S(1)}, bf16[4,784,128]{2,1,0:T(8,128)(2,1)}) custom-call(bf16[264,768]{1,0:T(8,128)(2,1)S(1)} %collective-permute-done.low_ref, bf16[512,768]{1,0:T(8,128)(2,1)S(1)} %bitcast.10, bf16[264,768]{1,0:T(8,128)(2,1)S(1)} %collective-permute-done.1.high_ref, s32[1,512]{1,0:T(1,128)S(1)} %copy-done.3, ...), custom_call_target="tpu_custom_call" | custom-call | flops 12000000000 | bytes 10000000 | tf_op jit(solution)/shard_map/window/pallas_call | solution.py:458
  50.0 0.0 copy-start.4
  50.0 0.9 copy-done.4
  50.9 1.5 %all-to-all-done.2 = bf16[128,8,384]{2,1,0:T(8,128)(2,1)S(1)} async-done(((bf16[128,8,384]{2,1,0:T(8,128)(2,1)}), bf16[128,8,384]{2,1,0:T(8,128)(2,1)S(1)}, u32[]{:S(2)}, u32[]{:S(2)}) %all-to-all-start.2) | async-done | bytes 786464 | tf_op jit(solution)/shard_map/all_to_all | solution.py:454
  52.4 4.8 %all-to-all-start.1 = ((bf16[4,784,128]{2,1,0:T(8,128)(2,1)}), bf16[4,784,128]{2,1,0:T(8,128)(2,1)S(1)}, u32[]{:S(2)}, u32[]{:S(2)}) async-start(bf16[4,784,128]{2,1,0:T(8,128)(2,1)} %get-tuple-element.25), calls=%async_computation.1 | async-start | bytes 1605632 | tf_op jit(solution)/shard_map/all_to_all | solution.py:487
  57.3 0.8 compact.1
  58.1 0.9 collective-permute-start.5
  59.0 2.4 %collective-permute-start.6 = (bf16[640,128]{1,0:T(8,128)(2,1)S(1)}, bf16[640,128]{1,0:T(8,128)(2,1)S(1)}, u32[]{:S(2)}, u32[]{:S(2)}) collective-permute-start(bf16[640,128]{1,0:T(8,128)(2,1)S(1)} %get-tuple-element.29.refs_0_), channel_id=1, source_target_pairs={{0,8},{1,9},{2,10},{3,11},{4,12},{5,13},{6,14},{7,15},{8,0},{9,1},... | collective-permute-start | bytes 491528 | tf_op jit(solution)/shard_map/ppermute | solution.py:507
  61.5 1.2 collective-permute-start.7
  62.6 0.8 collective-permute-start.2
  63.5 1.1 collective-permute-start.3
  64.6 3.7 %collective-permute-done.5.refs_1_ = bf16[640,128]{1,0:T(8,128)(2,1)S(1)} collective-permute-done((bf16[640,128]{1,0:T(8,128)(2,1)S(1)}, bf16[640,128]{1,0:T(8,128)(2,1)S(1)}, u32[]{:S(2)}, u32[]{:S(2)}) %collective-permute-start.5) | collective-permute-done | bytes 163872 | tf_op jit(solution)/shard_map/ppermute | solution.py:507
  68.2 0.0 collective-permute-start.4
  68.2 1.8 %collective-permute-done.6.refs_2_ = bf16[640,128]{1,0:T(8,128)(2,1)S(1)} collective-permute-done((bf16[640,128]{1,0:T(8,128)(2,1)S(1)}, bf16[640,128]{1,0:T(8,128)(2,1)S(1)}, u32[]{:S(2)}, u32[]{:S(2)}) %collective-permute-start.6) | collective-permute-done | bytes 163872 | tf_op jit(solution)/shard_map/ppermute | solution.py:507
  70.1 3.8 %collective-permute-done.7.refs_3_ = bf16[640,128]{1,0:T(8,128)(2,1)S(1)} collective-permute-done((bf16[640,128]{1,0:T(8,128)(2,1)S(1)}, bf16[640,128]{1,0:T(8,128)(2,1)S(1)}, u32[]{:S(2)}, u32[]{:S(2)}) %collective-permute-start.7) | collective-permute-done | bytes 163872 | tf_op jit(solution)/shard_map/ppermute | solution.py:507
  73.9 0.0 all-to-all-done.1.query_ref
  73.9 10.2 %cross.2 = (bf16[4,512,128]{2,1,0:T(8,128)(2,1)S(1)}, f32[8,2560]{1,0:T(8,128)S(1)}) custom-call(s32[3]{0:T(128)S(1)} %pad_add_fusion.where_ref, s32[1,384]{1,0:T(1,128)S(1)} %get-tuple-element.24.pos_ref, bf16[4,784,128]{2,1,0:T(8,128)(2,1)S(1)} %all-to-all-done.1.query_ref, bf16[640,128]{1,0:T(8,128)(2,1)S(1)} %get-tuple-element.29.refs_0_, ...), custom_call_target="tpu_custom_call" | custom-call | flops 10000000000 | bytes 4000000 | tf_op jit(solution)/shard_map/cross/pallas_call | solution.py:513
  84.1 0.0 collective-permute-done.2.refs_1_
  84.1 0.0 collective-permute-done.3.refs_2_
  84.1 0.0 collective-permute-done.4.refs_3_
  84.1 19.7 %cross.3 = (bf16[4,784,128]{2,1,0:T(8,128)(2,1)}, f32[1,384]{1,0:T(1,128)S(1)}) custom-call(s32[3]{0:T(128)S(1)} %pad_add_fusion.where_ref, s32[1,384]{1,0:T(1,128)S(1)} %get-tuple-element.24.pos_ref, bf16[4,784,128]{2,1,0:T(8,128)(2,1)S(1)} %all-to-all-done.1.query_ref, bf16[640,256]{1,0:T(8,128)(2,1)S(1)} %get-tuple-element.28.refs_0_, ...), custom_call_target="tpu_custom_call" | custom-call | flops 20000000000 | bytes 4000000 | tf_op jit(solution)/shard_map/cross/pallas_call | solution.py:513
  103.8 0.0 copy-start.5
  103.8 1.5 %collective-permute-start.9 = (f32[1,384]{1,0:T(1,128)S(1)}, f32[1,384]{1,0:T(1,128)S(1)}, u32[]{:S(2)}, u32[]{:S(2)}) collective-permute-start(f32[1,384]{1,0:T(1,128)S(1)} %get-tuple-element.33), channel_id=1, source_target_pairs={{0,1},{1,2},{2,3},{3,0},{4,5},{5,6},{6,7},{7,4},{8,9},{9,10},{10,1... | collective-permute-start | bytes 4616 | tf_op jit(solution)/shard_map/ppermute | solution.py:544
  105.3 0.6 collective-permute-start.10
  105.9 2.1 %collective-permute-start.8 = (f32[1,384]{1,0:T(1,128)S(1)}, f32[1,384]{1,0:T(1,128)S(1)}, u32[]{:S(2)}, u32[]{:S(2)}) collective-permute-start(f32[1,384]{1,0:T(1,128)S(1)} %get-tuple-element.33), channel_id=1, source_target_pairs={{0,2},{1,3},{2,0},{3,1},{4,6},{5,7},{6,4},{7,5},{8,10},{9,11},{10,... | collective-permute-start | bytes 4616 | tf_op jit(solution)/shard_map/ppermute | solution.py:544
  108.0 4.9 %all-to-all-start.3 = ((bf16[4,784,128]{2,1,0:T(8,128)(2,1)}), bf16[4,784,128]{2,1,0:T(8,128)(2,1)S(1)}, u32[]{:S(2)}, u32[]{:S(2)}) async-start(bf16[4,784,128]{2,1,0:T(8,128)(2,1)} %get-tuple-element.32), calls=%async_computation.3 | async-start | bytes 1605632 | tf_op jit(solution)/shard_map/all_to_all | solution.py:487
  112.9 0.0 collective-permute-done.9
  112.9 0.0 collective-permute-done.10
  112.9 0.0 collective-permute-done.8
  112.9 2.5 %collective-permute-start.12 = (f32[1,384]{1,0:T(1,128)S(1)}, f32[1,384]{1,0:T(1,128)S(1)}, u32[]{:S(2)}, u32[]{:S(2)}) collective-permute-start(f32[1,384]{1,0:T(1,128)S(1)} %add_add_fusion.1), channel_id=1, source_target_pairs={{0,4},{1,5},{2,6},{3,7},{4,8},{5,9},{6,10},{7,11},{8,12},{9,13},{1... | collective-permute-start | bytes 4616 | tf_op jit(solution)/shard_map/ppermute | solution.py:507
  115.5 1.8 %collective-permute-start.13 = (f32[1,384]{1,0:T(1,128)S(1)}, f32[1,384]{1,0:T(1,128)S(1)}, u32[]{:S(2)}, u32[]{:S(2)}) collective-permute-start(f32[1,384]{1,0:T(1,128)S(1)} %add_add_fusion.1), channel_id=1, source_target_pairs={{0,12},{1,13},{2,14},{3,15},{4,0},{5,1},{6,2},{7,3},{8,4},{9,5},{1... | collective-permute-start | bytes 4616 | tf_op jit(solution)/shard_map/ppermute | solution.py:507
  117.3 1.4 %collective-permute-start.11 = (f32[1,384]{1,0:T(1,128)S(1)}, f32[1,384]{1,0:T(1,128)S(1)}, u32[]{:S(2)}, u32[]{:S(2)}) collective-permute-start(f32[1,384]{1,0:T(1,128)S(1)} %add_add_fusion.1), channel_id=1, source_target_pairs={{0,8},{1,9},{2,10},{3,11},{4,12},{5,13},{6,14},{7,15},{8,0},{9,1},... | collective-permute-start | bytes 4616 | tf_op jit(solution)/shard_map/ppermute | solution.py:507
  118.6 0.1 collective-permute-done.12
  118.7 0.3 collective-permute-done.13
  119.0 3.3 %collective-permute-done.11 = f32[1,384]{1,0:T(1,128)S(1)} collective-permute-done((f32[1,384]{1,0:T(1,128)S(1)}, f32[1,384]{1,0:T(1,128)S(1)}, u32[]{:S(2)}, u32[]{:S(2)}) %collective-permute-start.11) | collective-permute-done | bytes 1568 | tf_op jit(solution)/shard_map/ppermute | solution.py:507
  122.3 0.6 slice.9
  123.6 0.6 fusion
  124.2 0.0 all-to-all-done.3.got_hbm
  124.2 0.0 copy-done.5
  124.2 3.8 %final.1 = bf16[512,768]{1,0:T(8,128)(2,1)} custom-call(bf16[512,768]{1,0:T(8,128)(2,1)S(1)} %copy-done.5, bf16[4,784,128]{2,1,0:T(8,128)(2,1)S(1)} %all-to-all-done.3.got_hbm, bf16[768,768]{1,0:T(8,128)(2,1)} %weight_hbm.1), custom_call_target="tpu_custom_call" | custom-call | flops 1000000000 | bytes 4000000 | tf_op jit(solution)/shard_map/final/pallas_call | solution.py:552
  (2 shorter events, 0.0 us)
Async XLA Ops:
  1.9 1.1 copy-start
  3.1 0.7 copy-start.2
  3.8 32.6 %collective-permute-start = (bf16[264,768]{1,0:T(8,128)(2,1)S(1)}, bf16[264,768]{1,0:T(8,128)(2,1)S(1)}, u32[]{:S(2)}, u32[]{:S(2)}) collective-permute-start(bf16[264,768]{1,0:T(8,128)(2,1)S(1)} %get-tuple-element.20), channel_id=1, source_target_pairs={{0,1},{1,2},{2,3},{3,4},{4,5},{5,6},{6,7},{7,8},{8,9},{9,10},{10,1... | collective-permute-start | bytes 1216520 | tf_op jit(solution)/shard_map/ppermute | solution.py:429
  7.2 29.2 %collective-permute-start.1 = (bf16[264,768]{1,0:T(8,128)(2,1)S(1)}, bf16[264,768]{1,0:T(8,128)(2,1)S(1)}, u32[]{:S(2)}, u32[]{:S(2)}) collective-permute-start(bf16[264,768]{1,0:T(8,128)(2,1)S(1)} %get-tuple-element.21), channel_id=1, source_target_pairs={{1,0},{2,1},{3,2},{4,3},{5,4},{6,5},{7,6},{8,7},{9,8},{10,9},{11,1... | collective-permute-start | bytes 1216520 | tf_op jit(solution)/shard_map/ppermute | solution.py:430
  9.7 9.8 %all-to-all-start = ((s32[8,1,320]{2,1,0:T(1,128)}), s32[8,1,320]{2,1,0:T(1,128)S(1)}, u32[]{:S(2)}, u32[]{:S(2)}) async-start(s32[8,1,320]{2,1,0:T(1,128)} %broadcast_in_dim.12), calls=%async_computation | async-start | bytes 24576 | tf_op jit(solution)/shard_map/all_to_all | solution.py:419
  27.9 8.5 %copy-start.1 = (bf16[1,512,768]{2,1,0:T(8,128)(2,1)S(1)}, bf16[1,512,768]{2,1,0:T(8,128)(2,1)}, u32[]{:S(2)}) copy-start(bf16[1,512,768]{2,1,0:T(8,128)(2,1)} %param.10) | copy-start | bytes 2359300
  27.9 8.5 %copy-start.3 = (s32[1,512]{1,0:T(1,128)S(1)}, s32[1,512]{1,0:T(1,128)}, u32[]{:S(2)}) copy-start(s32[1,512]{1,0:T(1,128)} %tokens_ref.1) | copy-start | bytes 6148
  27.9 24.5 %all-to-all-start.2 = ((bf16[128,8,384]{2,1,0:T(8,128)(2,1)}), bf16[128,8,384]{2,1,0:T(8,128)(2,1)S(1)}, u32[]{:S(2)}, u32[]{:S(2)}) async-start(bf16[128,8,384]{2,1,0:T(8,128)(2,1)} %bitcast.5), calls=%async_computation.2 | async-start | bytes 1572864 | tf_op jit(solution)/shard_map/all_to_all | solution.py:454
  50.0 0.9 copy-start.4
  52.4 21.5 %all-to-all-start.1 = ((bf16[4,784,128]{2,1,0:T(8,128)(2,1)}), bf16[4,784,128]{2,1,0:T(8,128)(2,1)S(1)}, u32[]{:S(2)}, u32[]{:S(2)}) async-start(bf16[4,784,128]{2,1,0:T(8,128)(2,1)} %get-tuple-element.25), calls=%async_computation.1 | async-start | bytes 1605632 | tf_op jit(solution)/shard_map/all_to_all | solution.py:487
  58.1 10.1 %collective-permute-start.5 = (bf16[640,128]{1,0:T(8,128)(2,1)S(1)}, bf16[640,128]{1,0:T(8,128)(2,1)S(1)}, u32[]{:S(2)}, u32[]{:S(2)}) collective-permute-start(bf16[640,128]{1,0:T(8,128)(2,1)S(1)} %get-tuple-element.29.refs_0_), channel_id=1, source_target_pairs={{0,4},{1,5},{2,6},{3,7},{4,8},{5,9},{6,10},{7,11},{8,12},{9,13},{1... | collective-permute-start | bytes 491528 | tf_op jit(solution)/shard_map/ppermute | solution.py:507
  59.0 11.0 %collective-permute-start.6 = (bf16[640,128]{1,0:T(8,128)(2,1)S(1)}, bf16[640,128]{1,0:T(8,128)(2,1)S(1)}, u32[]{:S(2)}, u32[]{:S(2)}) collective-permute-start(bf16[640,128]{1,0:T(8,128)(2,1)S(1)} %get-tuple-element.29.refs_0_), channel_id=1, source_target_pairs={{0,8},{1,9},{2,10},{3,11},{4,12},{5,13},{6,14},{7,15},{8,0},{9,1},... | collective-permute-start | bytes 491528 | tf_op jit(solution)/shard_map/ppermute | solution.py:507
  61.5 12.4 %collective-permute-start.7 = (bf16[640,128]{1,0:T(8,128)(2,1)S(1)}, bf16[640,128]{1,0:T(8,128)(2,1)S(1)}, u32[]{:S(2)}, u32[]{:S(2)}) collective-permute-start(bf16[640,128]{1,0:T(8,128)(2,1)S(1)} %get-tuple-element.29.refs_0_), channel_id=1, source_target_pairs={{0,12},{1,13},{2,14},{3,15},{4,0},{5,1},{6,2},{7,3},{8,4},{9,5},{1... | collective-permute-start | bytes 491528 | tf_op jit(solution)/shard_map/ppermute | solution.py:507
  62.6 21.4 %collective-permute-start.2 = (bf16[640,256]{1,0:T(8,128)(2,1)S(1)}, bf16[640,256]{1,0:T(8,128)(2,1)S(1)}, u32[]{:S(2)}, u32[]{:S(2)}) collective-permute-start(bf16[640,256]{1,0:T(8,128)(2,1)S(1)} %get-tuple-element.28.refs_0_), channel_id=1, source_target_pairs={{0,4},{1,5},{2,6},{3,7},{4,8},{5,9},{6,10},{7,11},{8,12},{9,13},{1... | collective-permute-start | bytes 983048 | tf_op jit(solution)/shard_map/ppermute | solution.py:507
  63.5 20.6 %collective-permute-start.3 = (bf16[640,256]{1,0:T(8,128)(2,1)S(1)}, bf16[640,256]{1,0:T(8,128)(2,1)S(1)}, u32[]{:S(2)}, u32[]{:S(2)}) collective-permute-start(bf16[640,256]{1,0:T(8,128)(2,1)S(1)} %get-tuple-element.28.refs_0_), channel_id=1, source_target_pairs={{0,8},{1,9},{2,10},{3,11},{4,12},{5,13},{6,14},{7,15},{8,0},{9,1},... | collective-permute-start | bytes 983048 | tf_op jit(solution)/shard_map/ppermute | solution.py:507
  68.2 15.8 %collective-permute-start.4 = (bf16[640,256]{1,0:T(8,128)(2,1)S(1)}, bf16[640,256]{1,0:T(8,128)(2,1)S(1)}, u32[]{:S(2)}, u32[]{:S(2)}) collective-permute-start(bf16[640,256]{1,0:T(8,128)(2,1)S(1)} %get-tuple-element.28.refs_0_), channel_id=1, source_target_pairs={{0,12},{1,13},{2,14},{3,15},{4,0},{5,1},{6,2},{7,3},{8,4},{9,5},{1... | collective-permute-start | bytes 983048 | tf_op jit(solution)/shard_map/ppermute | solution.py:507
  103.8 20.4 %copy-start.5 = (bf16[512,768]{1,0:T(8,128)(2,1)S(1)}, bf16[512,768]{1,0:T(8,128)(2,1)}, u32[]{:S(2)}) copy-start(bf16[512,768]{1,0:T(8,128)(2,1)} %copy-done.4) | copy-start | bytes 2359300
  103.8 9.1 %collective-permute-start.9 = (f32[1,384]{1,0:T(1,128)S(1)}, f32[1,384]{1,0:T(1,128)S(1)}, u32[]{:S(2)}, u32[]{:S(2)}) collective-permute-start(f32[1,384]{1,0:T(1,128)S(1)} %get-tuple-element.33), channel_id=1, source_target_pairs={{0,1},{1,2},{2,3},{3,0},{4,5},{5,6},{6,7},{7,4},{8,9},{9,10},{10,1... | collective-permute-start | bytes 4616 | tf_op jit(solution)/shard_map/ppermute | solution.py:544
  105.3 7.6 %collective-permute-start.10 = (f32[1,384]{1,0:T(1,128)S(1)}, f32[1,384]{1,0:T(1,128)S(1)}, u32[]{:S(2)}, u32[]{:S(2)}) collective-permute-start(f32[1,384]{1,0:T(1,128)S(1)} %get-tuple-element.33), channel_id=1, source_target_pairs={{0,3},{1,0},{2,1},{3,2},{4,7},{5,4},{6,5},{7,6},{8,11},{9,8},{10,9... | collective-permute-start | bytes 4616 | tf_op jit(solution)/shard_map/ppermute | solution.py:544
  105.9 7.0 %collective-permute-start.8 = (f32[1,384]{1,0:T(1,128)S(1)}, f32[1,384]{1,0:T(1,128)S(1)}, u32[]{:S(2)}, u32[]{:S(2)}) collective-permute-start(f32[1,384]{1,0:T(1,128)S(1)} %get-tuple-element.33), channel_id=1, source_target_pairs={{0,2},{1,3},{2,0},{3,1},{4,6},{5,7},{6,4},{7,5},{8,10},{9,11},{10,... | collective-permute-start | bytes 4616 | tf_op jit(solution)/shard_map/ppermute | solution.py:544
  108.0 16.2 %all-to-all-start.3 = ((bf16[4,784,128]{2,1,0:T(8,128)(2,1)}), bf16[4,784,128]{2,1,0:T(8,128)(2,1)S(1)}, u32[]{:S(2)}, u32[]{:S(2)}) async-start(bf16[4,784,128]{2,1,0:T(8,128)(2,1)} %get-tuple-element.32), calls=%async_computation.3 | async-start | bytes 1605632 | tf_op jit(solution)/shard_map/all_to_all | solution.py:487
  112.9 5.8 %collective-permute-start.12 = (f32[1,384]{1,0:T(1,128)S(1)}, f32[1,384]{1,0:T(1,128)S(1)}, u32[]{:S(2)}, u32[]{:S(2)}) collective-permute-start(f32[1,384]{1,0:T(1,128)S(1)} %add_add_fusion.1), channel_id=1, source_target_pairs={{0,4},{1,5},{2,6},{3,7},{4,8},{5,9},{6,10},{7,11},{8,12},{9,13},{1... | collective-permute-start | bytes 4616 | tf_op jit(solution)/shard_map/ppermute | solution.py:507
  115.5 3.6 %collective-permute-start.13 = (f32[1,384]{1,0:T(1,128)S(1)}, f32[1,384]{1,0:T(1,128)S(1)}, u32[]{:S(2)}, u32[]{:S(2)}) collective-permute-start(f32[1,384]{1,0:T(1,128)S(1)} %add_add_fusion.1), channel_id=1, source_target_pairs={{0,12},{1,13},{2,14},{3,15},{4,0},{5,1},{6,2},{7,3},{8,4},{9,5},{1... | collective-permute-start | bytes 4616 | tf_op jit(solution)/shard_map/ppermute | solution.py:507
  117.3 5.1 %collective-permute-start.11 = (f32[1,384]{1,0:T(1,128)S(1)}, f32[1,384]{1,0:T(1,128)S(1)}, u32[]{:S(2)}, u32[]{:S(2)}) collective-permute-start(f32[1,384]{1,0:T(1,128)S(1)} %add_add_fusion.1), channel_id=1, source_target_pairs={{0,8},{1,9},{2,10},{3,11},{4,12},{5,13},{6,14},{7,15},{8,0},{9,1},... | collective-permute-start | bytes 4616 | tf_op jit(solution)/shard_map/ppermute | solution.py:507

commit v5 on v4

--- a/solution.py
+++ b/solution.py
@@ -56,10 +56,13 @@
     return pl.CostEstimate(flops=flops, transcendentals=exps, bytes_accessed=bytes_)
 
 
-def split_table(table):
-    wide = jnp.transpose(table.astype(F32))
+def planes_kernel(table_ref, planes_ref):
+    missing = planes_ref.shape[1] - table_ref.shape[0]
+    rows = jnp.concatenate([table_ref[...].astype(F32), jnp.zeros((missing, LANES), F32)], axis=0)
+    wide = jnp.transpose(rows)
     high = jnp.floor(wide * (1.0 / 256.0))
-    return jnp.concatenate([high, wide - high * 256.0], axis=0).astype(BF)
+    planes_ref[:LANES, :] = high.astype(BF)
+    planes_ref[LANES:, :] = (wide - high * 256.0).astype(BF)
 
 
 def look_up(code, table):
@@ -89,20 +92,16 @@
 
 
 def route_kernel(
-    count, code_dev, devices, where_ref, codes_ref, table_ref, cache_ref, send_ref, slot_ref, pos_ref, table, rows, line, picks, picked, sems, sem
+    count, code_dev, devices, where_ref, codes_ref, planes_ref, cache_ref, send_hbm, slot_ref, pos_ref, send_ref, rows, line, picks, picked, sems, sem
 ):
     docs = codes_ref.shape[0]
     n = line.shape[1]
-    fetch = pltpu.make_async_copy(table_ref, table.at[pl.ds(0, table_ref.shape[0]), :], sem.at[0])
-    fetch.start()
     upper = upper_ones(n)
     lane = iota((1, LANES), 1)
-    table[table_ref.shape[0] :, :] = jnp.zeros((table.shape[0] - table_ref.shape[0], LANES), I32)
     line[...] = jnp.full(line.shape, -1, I32)
     for d in range(docs):
         line[d : d + 1, :count] = codes_ref[d]
-    fetch.wait()
-    planes = split_table(table[...])
+    planes = planes_ref[...]
     doc = where_ref[2]
     owner_here = jnp.zeros((1, n), I32)
     rank_here = jnp.zeros((1, n), I32)
@@ -118,7 +117,7 @@
         picks[d : d + 1, :] = jnp.maximum(found.astype(I32) - 1, 0)
         owner_here = jnp.where(doc == d, owner, owner_here)
         rank_here = jnp.where(doc == d, rank, rank_here)
-    to_scalars = pltpu.make_async_copy(picks, picked, sem.at[1])
+    to_scalars = pltpu.make_async_copy(picks, picked, sem.at[docs])
     to_scalars.start()
     to_scalars.wait()
     copies = []
@@ -141,6 +140,7 @@
     pos_ref[...] = part * (count // GRID) + spot
 
     low = iota((GRID, DESC, LANES), 2) < HALF
+    sent = []
     for d in range(docs):
         for copy in copies[d * GRID : (d + 1) * GRID]:
             copy.wait()
@@ -163,6 +163,10 @@
                 else:
                     tile = jnp.where(low, key_low, value_high)
                 send_ref[block, group, :, pl.ds(inner * LANES, LANES)] = tile.astype(BF)
+        sent.append(pltpu.make_async_copy(send_ref.at[block], send_hbm.at[block], sem.at[d]))
+        sent[-1].start()
+    for copy in sent:
+        copy.wait()
 
 
 def compact_kernel(slot_ref, got_ref, first_ref, rest_ref):
@@ -179,14 +183,22 @@
     return centered * lax.rsqrt(spread + 1e-05)
 
 
-def halo_kernel(hidden_ref, tokens_ref, tail_ref, head_ref):
-    tok, width = hidden_ref.shape
+def halo_kernel(hidden_hbm, tokens_ref, wanted_ref, tail_ref, head_ref, asked_ref, sems):
+    tok, width = hidden_hbm.shape
     win = HALF_WIN
+    places = ((tail_ref, tok - win), (head_ref, 0))
+    copies = []
+    for k, (ref, start) in enumerate(places):
+        copies.append(pltpu.make_async_copy(hidden_hbm.at[pl.ds(start, win), :], ref.at[pl.ds(0, win), :], sems.at[k]))
+        copies[-1].start()
+    for d in range(asked_ref.shape[0]):
+        asked_ref[d] = wanted_ref[...]
     flags = (tokens_ref[...] != 0).astype(F32)
-    for ref, start in ((tail_ref, tok - win), (head_ref, 0)):
-        ref[:win, :] = hidden_ref[start : start + win, :]
+    for ref, start in places:
         row = jnp.concatenate([flags[:, start : start + win], jnp.zeros((1, width - win), F32)], axis=1)
         ref[win:, :] = jnp.broadcast_to(row, (8, width)).astype(BF)
+    for copy in copies:
+        copy.wait()
 
 
 def window_kernel(
@@ -272,20 +284,13 @@
     kv_refs, refs = refs[:GRID], refs[GRID:]
     last = 2 in heads
     if last:
-        before_ref, earlier_ref, out_ref, score_ref, keys, values, expds, total, sems = refs
+        before_ref, earlier_ref, out_ref, score_ref, keys, values, expds, total = refs
     else:
-        out_ref, mass_ref, keys, values, expds, total, sems = refs
+        out_ref, mass_ref, keys, values, expds, total = refs
     held = kv_refs[0].shape[0]
     tok = expds.shape[1]
     groups = query_ref.shape[0]
     half = tok // 2
-    copies = []
-    for k in range(len(heads)):
-        for c in range(GRID):
-            source = kv_refs[c].at[:, pl.ds(k * LANES, LANES)]
-            copy = pltpu.make_async_copy(source, keys.at[k, pl.ds(c * held, held), :], sems.at[k * GRID + c])
-            copy.start()
-            copies.append(copy)
     small = iota((tok, LANES), 1) < HALF
     low = iota((half, LANES), 1) < HALF
     if last:
@@ -295,9 +300,10 @@
     lower = iota((held, LANES), 1) < HALF
     for k, inner in enumerate(heads):
         for c in range(GRID):
-            copies[k * GRID + c].wait()
             rows = pl.ds(c * held, held)
-            scaled = keys[k, rows, :].astype(F32) * 2.0**-4
+            block = kv_refs[c][:, k * LANES : (k + 1) * LANES]
+            keys[k, rows, :] = block
+            scaled = block.astype(F32) * 2.0**-4
             values[k, rows, :] = jnp.where(lower == (inner == 1), scaled, 1.0).astype(BF)
 
     def one(g, k, slot):
@@ -370,21 +376,14 @@
     return first, second, value - first - second
 
 
-def final_kernel(middle_ref, got_hbm, weight_hbm, out_ref, got_ref, weight_ref, sems):
+def final_kernel(middle_ref, got_ref, weight_ref, out_ref):
     tok = middle_ref.shape[0]
     groups = got_ref.shape[0]
-    whole = pltpu.make_async_copy(weight_hbm, weight_ref, sems.at[groups])
-    whole.start()
-    copies = [pltpu.make_async_copy(got_hbm.at[g], got_ref.at[g], sems.at[g]) for g in range(groups)]
-    for copy in copies:
-        copy.start()
-    whole.wait()
     half = tok // 2
     size = 3 * HALF
     low = iota((half, LANES), 1) < HALF
     acc = middle_ref[...].astype(F32)
     for g in range(groups):
-        copies[g].wait()
         at = g * size
         heads = [weight_ref[at + k * HALF : at + (k + 1) * HALF, :] for k in (1, 0, 2, 2)]
         packed = got_ref[g, tok : tok + half, :]
@@ -411,21 +410,30 @@
     message = tok + tok // 2 + 16
     table = code_row.reshape(-1, LANES)
 
-    asked = jnp.broadcast_to(shortlist[None], (docs, 1, count))
-    asked, doc_hidden, token_ids = lax.optimization_barrier((asked, doc_hidden, token_ids))
-
     forward = [(i, i + 1) for i in range(seq_count - 1)]
     backward = [(t, s) for s, t in forward]
-    all_codes = lax.all_to_all(asked, "doc", split_axis=0, concat_axis=0, tiled=True)
-    tail, head = pl.pallas_call(
+    tail, head, asked = pl.pallas_call(
         halo_kernel,
         name="halo",
-        out_shape=(jax.ShapeDtypeStruct((HALF_WIN + 8, width), BF),) * 2,
-        in_specs=[vmem()] * 2,
-        out_specs=(vmem(),) * 2,
+        out_shape=(jax.ShapeDtypeStruct((HALF_WIN + 8, width), BF),) * 2
+        + (jax.ShapeDtypeStruct((docs, 1, count), I32),),
+        in_specs=[hbm(), vmem(), vmem()],
+        out_specs=(vmem(),) * 3,
+        scratch_shapes=[pltpu.SemaphoreType.DMA((2,))],
         compiler_params=params(16),
         cost_estimate=cost(10**5, 0, 16 * 10**5),
-    )(doc_hidden, token_ids)
+    )(pinned(doc_hidden), token_ids, shortlist)
+    all_codes = lax.all_to_all(asked, "doc", split_axis=0, concat_axis=0, tiled=True)
+    table, head = lax.optimization_barrier((table, head))
+    planes = pl.pallas_call(
+        planes_kernel,
+        name="planes",
+        out_shape=jax.ShapeDtypeStruct((2 * LANES, -(-table.shape[0] // LANES) * LANES), BF),
+        in_specs=[vmem()],
+        out_specs=vmem(),
+        compiler_params=params(16),
+        cost_estimate=cost(10**5, 0, 2 * 10**5),
+    )(table)
     low = lax.ppermute(tail, "seq", forward)
     high = lax.ppermute(head, "seq", backward)
 
@@ -437,20 +445,20 @@
             jax.ShapeDtypeStruct((1, devices * DESC), I32),
             jax.ShapeDtypeStruct((1, padded), I32),
         ),
-        in_specs=[smem(), vmem(), hbm(), hbm()],
-        out_specs=(vmem(),) * 3,
+        in_specs=[smem(), vmem(), vmem(), hbm()],
+        out_specs=(hbm(), vmem(), vmem()),
         scratch_shapes=[
-            pltpu.VMEM((-(-table.shape[0] // LANES) * LANES, LANES), I32),
+            pltpu.VMEM((docs * GRID, GRID, DESC, 3 * LANES), BF),
             pltpu.VMEM((docs * GRID, 2, DESC, width), BF),
             pltpu.VMEM((docs, padded), I32),
             pltpu.VMEM((docs, LANES), I32),
             pltpu.SMEM((docs, LANES), I32),
             pltpu.SemaphoreType.DMA((docs * GRID,)),
-            pltpu.SemaphoreType.DMA((2,)),
+            pltpu.SemaphoreType.DMA((docs + 1,)),
         ],
         compiler_params=params(24),
         cost_estimate=cost(10**9, 0, 2 * 10**6),
-    )(where, all_codes, pinned(table), pinned(code_cache))
+    )(where, all_codes, planes, pinned(code_cache))
     got = lax.all_to_all(
         send.reshape(devices, DESC, 3 * LANES), ("doc", "seq"), split_axis=0, concat_axis=0, tiled=True
     )
@@ -514,14 +522,13 @@
             functools.partial(cross_kernel, heads, count),
             name="cross",
             out_shape=outs,
-            in_specs=[smem()] + [vmem()] * 2 + [hbm()] * GRID + [vmem()] * len(extra),
+            in_specs=[smem()] + [vmem()] * (2 + GRID + len(extra)),
             out_specs=jax.tree.map(lambda _: vmem(), outs),
             scratch_shapes=[
                 pltpu.VMEM((len(heads), GRID * held, LANES), BF),
                 pltpu.VMEM((len(heads), GRID * held, LANES), BF),
                 pltpu.VMEM((2, tok, GRID * held), BF),
                 pltpu.VMEM((8, GRID * held), F32),
-                pltpu.SemaphoreType.DMA((len(heads) * GRID,)),
             ],
             compiler_params=params(24),
             cost_estimate=cost(len(heads) * 10**10, 5 * 10**6, 4 * 10**6),
@@ -544,25 +551,20 @@
     one, two, three = [lax.ppermute(score, "seq", pairs) for pairs in across_x]
     score = (score + two) + (one + three)
     one, two, three = turns(score)
-    sums = (score + two) + (one + three)
-    out = across(out)
-    tokens = sums[:, count : count + 1] * (1.0 / GRID)
-    cand_score = count * sums[:, :count] / (HEADS * tokens)
 
     refined = pl.pallas_call(
         final_kernel,
         name="final",
         out_shape=jax.ShapeDtypeStruct((tok, width), BF),
-        in_specs=[vmem(), hbm(), hbm()],
+        in_specs=[vmem()] * 3,
         out_specs=vmem(),
-        scratch_shapes=[
-            pltpu.VMEM((GRID, message, LANES), BF),
-            pltpu.VMEM((width, width), BF),
-            pltpu.SemaphoreType.DMA((GRID + 1,)),
-        ],
         compiler_params=params(16),
         cost_estimate=cost(10**9, 0, 4 * 10**6),
-    )(middle, out, pinned(x_out))
+    )(middle, across(out), x_out)
+    one, two, three, refined = lax.optimization_barrier((one, two, three, refined))
+    sums = (score + two) + (one + three)
+    tokens = sums[:, count : count + 1] * (1.0 / GRID)
+    cand_score = count * sums[:, :count] / (HEADS * tokens)
     return (refined[None], cand_score)
 
 

time: 129 us -> 130 us (level)
  Pallas kernels: 56.6 us -> 53.9 us
  waiting for transfers between devices: 19.8 us -> 21.8 us
  starting transfers between devices: 44.9 us -> 46.8 us
    ppermute x3, waiting for transfers between devices: 0.01 us -> 5.09 us  [local(): one, two, three = [lax.ppermute(score, 'seq', pairs) for pairs in across_x]]
    ppermute x9, waiting for transfers between devices: 13 us -> 11 us  [turns(): parts.append(lax.ppermute(block, 'seq', pairs))]
    pallas_call x1, Pallas kernels: 3.84 us -> 1.89 us  [local(): pl.pallas_call(final_kernel, name='final', out_shape=jax.ShapeDtypeStruct...]
    all_to_all x1, starting transfers between devices: 8.46 us -> 10.3 us  [local(): lax.all_to_all(send.reshape(devices, DESC, 3 * LANES), ('doc', 'seq'), sp...]
    pallas_call x1, Pallas kernels: 0.05 us -> 1.73 us  [local(): pl.pallas_call(halo_kernel, name='halo', out_shape=(jax.ShapeDtypeStruct(...]
    pallas_call x1, Pallas kernels: 8.37 us -> 6.82 us  [local(): pl.pallas_call(functools.partial(route_kernel, count, code_dev, devices),...]
    unnamed x12 -> x16, local copies, waits for them, and re-layouts: 2.71 us -> 3.16 us
  transfers between devices with their start and end apart: 18 -> 18, of which waited for: 8 -> 9; matrix products, arithmetic and copies ran while one was open for 1% -> 0% of each run, Pallas kernels for 26% -> 25%
where the time goes in v5:
time: 130 us; the launch traced here: 128 us
  Pallas kernels  53.9 us (41%)
  starting transfers between devices  46.8 us (36%)
  waiting for transfers between devices  21.8 us (17%)
  local copies, waits for them, and re-layouts  3.75 us (3%)
  between operations  1.47 us (1%)
    pallas_call x2, Pallas kernels, cross(): pl.pallas_call(functools.partial(cross_kernel, heads, count), name='cross...  28.9 us
    pallas_call x1, Pallas kernels, local(): pl.pallas_call(window_kernel, name='window', out_shape=(jax.ShapeDtypeStr...  13.6 us
    ppermute x9, starting transfers between devices, turns(): parts.append(lax.ppermute(block, 'seq', pairs))  11.7 us
    ppermute x9, waiting for transfers between devices, turns(): parts.append(lax.ppermute(block, 'seq', pairs))  11 us
    all_to_all x1, starting transfers between devices, local(): lax.all_to_all(send.reshape(devices, DESC, 3 * LANES), ('doc', 'seq'), sp...  10.3 us
    all_to_all x2, starting transfers between devices, across(): lax.all_to_all(block, 'seq', split_axis=0, concat_axis=0, axis_index_grou...  9.77 us
    pallas_call x1, Pallas kernels, local(): pl.pallas_call(functools.partial(route_kernel, count, code_dev, devices),...  6.82 us
    ppermute x3, waiting for transfers between devices, local(): one, two, three = [lax.ppermute(score, 'seq', pairs) for pairs in across_x]  5.09 us
  transfers between devices with their start and end apart: 18, of which 9 were waited for; matrix products, arithmetic and copies ran while one was open for 0% of the time, Pallas kernels for 25%

profile of v5, /device:TPU:2, one launch (start us, length us, event | category | flops | bytes accessed | tf_op | source)
XLA Modules:
  0.0 128.4 jit_solution(1256063065324595838)
XLA Ops:
  0.6 0.0 copy-start.2
  0.6 0.7 copy-done.2
  1.3 0.0 copy-start.4
  1.3 0.7 copy-done.4
  2.0 1.7 %halo.1 = (bf16[264,768]{1,0:T(8,128)(2,1)S(1)}, bf16[264,768]{1,0:T(8,128)(2,1)S(1)}, s32[8,1,320]{2,1,0:T(1,128)}) custom-call(bf16[512,768]{1,0:T(8,128)(2,1)} %bitcast.10, s32[1,512]{1,0:T(1,128)S(1)} %copy-done.2, s32[1,320]{1,0:T(1,128)S(1)} %copy-done.4), custom_call_target="tpu_custom_call" | custom-call | flops 100000 | bytes 1600000 | tf_op jit(solution)/shard_map/halo/pallas_call | solution.py:415
  3.7 2.4 %collective-permute-start.1 = (bf16[264,768]{1,0:T(8,128)(2,1)S(1)}, bf16[264,768]{1,0:T(8,128)(2,1)S(1)}, u32[]{:S(2)}, u32[]{:S(2)}) collective-permute-start(bf16[264,768]{1,0:T(8,128)(2,1)S(1)} %get-tuple-element.27), channel_id=1, source_target_pairs={{1,0},{2,1},{3,2},{4,3},{5,4},{6,5},{7,6},{8,7},{9,8},{10,9},{11,1... | collective-permute-start | bytes 1216520 | tf_op jit(solution)/shard_map/ppermute | solution.py:438
  6.1 3.5 %collective-permute-start = (bf16[264,768]{1,0:T(8,128)(2,1)S(1)}, bf16[264,768]{1,0:T(8,128)(2,1)S(1)}, u32[]{:S(2)}, u32[]{:S(2)}) collective-permute-start(bf16[264,768]{1,0:T(8,128)(2,1)S(1)} %get-tuple-element.26), channel_id=1, source_target_pairs={{0,1},{1,2},{2,3},{3,4},{4,5},{5,6},{6,7},{7,8},{8,9},{9,10},{10,1... | collective-permute-start | bytes 1216520 | tf_op jit(solution)/shard_map/ppermute | solution.py:437
  9.6 4.5 %all-to-all-start = ((s32[8,1,320]{2,1,0:T(1,128)}), s32[8,1,320]{2,1,0:T(1,128)S(1)}, u32[]{:S(2)}, u32[]{:S(2)}) async-start(s32[8,1,320]{2,1,0:T(1,128)} %get-tuple-element.22), calls=%async_computation | async-start | bytes 24576 | tf_op jit(solution)/shard_map/all_to_all | solution.py:426
  14.1 0.1 pad_add_fusion.where_ref
  14.2 0.0 copy-start.1
  14.2 0.9 copy-done.1
  15.1 0.1 planes.1.planes_ref
  15.2 4.2 %all-to-all-done.codes_ref = s32[8,1,320]{2,1,0:T(1,128)S(1)} async-done(((s32[8,1,320]{2,1,0:T(1,128)}), s32[8,1,320]{2,1,0:T(1,128)S(1)}, u32[]{:S(2)}, u32[]{:S(2)}) %all-to-all-start) | async-done | bytes 10272 | tf_op jit(solution)/shard_map/all_to_all | solution.py:426
  19.4 6.8 %route.1 = (bf16[32,4,8,384]{3,2,1,0:T(8,128)(2,1)}, s32[1,1024]{1,0:T(1,128)S(1)}, s32[1,384]{1,0:T(1,128)S(1)}) custom-call(s32[3]{0:T(128)S(1)} %pad_add_fusion.where_ref, s32[8,1,320]{2,1,0:T(1,128)S(1)} %all-to-all-done.codes_ref, bf16[256,384]{1,0:T(8,128)(2,1)S(1)} %planes.1.planes_ref, bf16[288,2,8,768]{3,2,1,0:T(8,128)(2,1)} %cache_ref.1), custom_call_target="tpu_custom_call" | custom-call | flops 1000000000 | bytes 2000000 | tf_op jit(solution)/shard_map/route/pallas_call | solution.py:440
  26.2 0.0 copy-start
  26.3 0.0 copy-start.3
  26.3 10.3 %all-to-all-start.2 = ((bf16[128,8,384]{2,1,0:T(8,128)(2,1)}), bf16[128,8,384]{2,1,0:T(8,128)(2,1)S(1)}, u32[]{:S(2)}, u32[]{:S(2)}) async-start(bf16[128,8,384]{2,1,0:T(8,128)(2,1)} %bitcast.5), calls=%async_computation.2 | async-start | bytes 1572864 | tf_op jit(solution)/shard_map/all_to_all | solution.py:462
  36.6 0.0 collective-permute-done.1.high_ref
  36.6 0.0 collective-permute-done.low_ref
  36.6 0.0 copy-done
  36.6 0.0 copy-done.3
  36.6 13.6 %window.1 = (bf16[512,768]{1,0:T(8,128)(2,1)S(1)}, bf16[4,784,128]{2,1,0:T(8,128)(2,1)}) custom-call(bf16[264,768]{1,0:T(8,128)(2,1)S(1)} %collective-permute-done.low_ref, bf16[512,768]{1,0:T(8,128)(2,1)S(1)} %bitcast.11, bf16[264,768]{1,0:T(8,128)(2,1)S(1)} %collective-permute-done.1.high_ref, s32[1,512]{1,0:T(1,128)S(1)} %copy-done.3, ...), custom_call_target="tpu_custom_call" | custom-call | flops 12000000000 | bytes 10000000 | tf_op jit(solution)/shard_map/window/pallas_call | solution.py:466
  50.2 0.0 copy-start.6
  50.2 0.9 copy-done.6
  51.1 1.5 %all-to-all-done.2 = bf16[128,8,384]{2,1,0:T(8,128)(2,1)S(1)} async-done(((bf16[128,8,384]{2,1,0:T(8,128)(2,1)}), bf16[128,8,384]{2,1,0:T(8,128)(2,1)S(1)}, u32[]{:S(2)}, u32[]{:S(2)}) %all-to-all-start.2) | async-done | bytes 786464 | tf_op jit(solution)/shard_map/all_to_all | solution.py:462
  52.6 4.8 %all-to-all-start.1 = ((bf16[4,784,128]{2,1,0:T(8,128)(2,1)}), bf16[4,784,128]{2,1,0:T(8,128)(2,1)S(1)}, u32[]{:S(2)}, u32[]{:S(2)}) async-start(bf16[4,784,128]{2,1,0:T(8,128)(2,1)} %get-tuple-element.28), calls=%async_computation.1 | async-start | bytes 1605632 | tf_op jit(solution)/shard_map/all_to_all | solution.py:495
  57.5 0.8 compact.1
  58.3 0.9 collective-permute-start.5
  59.2 2.4 %collective-permute-start.6 = (bf16[640,128]{1,0:T(8,128)(2,1)S(1)}, bf16[640,128]{1,0:T(8,128)(2,1)S(1)}, u32[]{:S(2)}, u32[]{:S(2)}) collective-permute-start(bf16[640,128]{1,0:T(8,128)(2,1)S(1)} %get-tuple-element.32.refs_0_), channel_id=1, source_target_pairs={{0,8},{1,9},{2,10},{3,11},{4,12},{5,13},{6,14},{7,15},{8,0},{9,1},... | collective-permute-start | bytes 491528 | tf_op jit(solution)/shard_map/ppermute | solution.py:515
  61.7 1.2 collective-permute-start.7
  62.9 0.8 collective-permute-start.2
  63.7 1.1 collective-permute-start.3
  64.8 3.7 %collective-permute-done.5.refs_1_ = bf16[640,128]{1,0:T(8,128)(2,1)S(1)} collective-permute-done((bf16[640,128]{1,0:T(8,128)(2,1)S(1)}, bf16[640,128]{1,0:T(8,128)(2,1)S(1)}, u32[]{:S(2)}, u32[]{:S(2)}) %collective-permute-start.5) | collective-permute-done | bytes 163872 | tf_op jit(solution)/shard_map/ppermute | solution.py:515
  68.5 0.0 collective-permute-start.4
  68.5 1.8 %collective-permute-done.6.refs_2_ = bf16[640,128]{1,0:T(8,128)(2,1)S(1)} collective-permute-done((bf16[640,128]{1,0:T(8,128)(2,1)S(1)}, bf16[640,128]{1,0:T(8,128)(2,1)S(1)}, u32[]{:S(2)}, u32[]{:S(2)}) %collective-permute-start.6) | collective-permute-done | bytes 163872 | tf_op jit(solution)/shard_map/ppermute | solution.py:515
  70.3 3.8 %collective-permute-done.7.refs_3_ = bf16[640,128]{1,0:T(8,128)(2,1)S(1)} collective-permute-done((bf16[640,128]{1,0:T(8,128)(2,1)S(1)}, bf16[640,128]{1,0:T(8,128)(2,1)S(1)}, u32[]{:S(2)}, u32[]{:S(2)}) %collective-permute-start.7) | collective-permute-done | bytes 163872 | tf_op jit(solution)/shard_map/ppermute | solution.py:515
  74.1 0.0 all-to-all-done.1.query_ref
  74.1 9.4 %cross.2 = (bf16[4,512,128]{2,1,0:T(8,128)(2,1)S(1)}, f32[8,2560]{1,0:T(8,128)S(1)}) custom-call(s32[3]{0:T(128)S(1)} %pad_add_fusion.where_ref, s32[1,384]{1,0:T(1,128)S(1)} %get-tuple-element.25.pos_ref, bf16[4,784,128]{2,1,0:T(8,128)(2,1)S(1)} %all-to-all-done.1.query_ref, bf16[640,128]{1,0:T(8,128)(2,1)S(1)} %get-tuple-element.32.refs_0_, ...), custom_call_target="tpu_custom_call" | custom-call | flops 10000000000 | bytes 4000000 | tf_op jit(solution)/shard_map/cross/pallas_call | solution.py:521
  83.5 0.0 collective-permute-done.2.refs_1_
  83.5 0.0 collective-permute-done.3.refs_2_
  83.5 0.0 collective-permute-done.4.refs_3_
  83.5 0.0 copy-start.7
  83.5 19.6 %cross.3 = (bf16[4,784,128]{2,1,0:T(8,128)(2,1)}, f32[1,384]{1,0:T(1,128)S(1)}) custom-call(s32[3]{0:T(128)S(1)} %pad_add_fusion.where_ref, s32[1,384]{1,0:T(1,128)S(1)} %get-tuple-element.25.pos_ref, bf16[4,784,128]{2,1,0:T(8,128)(2,1)S(1)} %all-to-all-done.1.query_ref, bf16[640,256]{1,0:T(8,128)(2,1)S(1)} %get-tuple-element.31.refs_0_, ...), custom_call_target="tpu_custom_call" | custom-call | flops 20000000000 | bytes 4000000 | tf_op jit(solution)/shard_map/cross/pallas_call | solution.py:521
  103.1 0.0 copy-start.5
  103.1 4.9 %all-to-all-start.3 = ((bf16[4,784,128]{2,1,0:T(8,128)(2,1)}), bf16[4,784,128]{2,1,0:T(8,128)(2,1)S(1)}, u32[]{:S(2)}, u32[]{:S(2)}) async-start(bf16[4,784,128]{2,1,0:T(8,128)(2,1)} %get-tuple-element.37), calls=%async_computation.3 | async-start | bytes 1605632 | tf_op jit(solution)/shard_map/all_to_all | solution.py:495
  108.0 0.0 collective-permute-start.10
  108.1 2.9 %collective-permute-start.8 = (f32[1,384]{1,0:T(1,128)S(1)}, f32[1,384]{1,0:T(1,128)S(1)}, u32[]{:S(2)}, u32[]{:S(2)}) collective-permute-start(f32[1,384]{1,0:T(1,128)S(1)} %get-tuple-element.35), channel_id=1, source_target_pairs={{0,2},{1,3},{2,0},{3,1},{4,6},{5,7},{6,4},{7,5},{8,10},{9,11},{10,... | collective-permute-start | bytes 4616 | tf_op jit(solution)/shard_map/ppermute | solution.py:551
  111.0 1.8 %collective-permute-start.9 = (f32[1,384]{1,0:T(1,128)S(1)}, f32[1,384]{1,0:T(1,128)S(1)}, u32[]{:S(2)}, u32[]{:S(2)}) collective-permute-start(f32[1,384]{1,0:T(1,128)S(1)} %get-tuple-element.35), channel_id=1, source_target_pairs={{0,1},{1,2},{2,3},{3,0},{4,5},{5,6},{6,7},{7,4},{8,9},{9,10},{10,1... | collective-permute-start | bytes 4616 | tf_op jit(solution)/shard_map/ppermute | solution.py:551
  112.7 2.9 %collective-permute-done.10 = f32[1,384]{1,0:T(1,128)S(1)} collective-permute-done((f32[1,384]{1,0:T(1,128)S(1)}, f32[1,384]{1,0:T(1,128)S(1)}, u32[]{:S(2)}, u32[]{:S(2)}) %collective-permute-start.10) | collective-permute-done | bytes 1568 | tf_op jit(solution)/shard_map/ppermute | solution.py:551
  115.6 2.2 %collective-permute-done.8 = f32[1,384]{1,0:T(1,128)S(1)} collective-permute-done((f32[1,384]{1,0:T(1,128)S(1)}, f32[1,384]{1,0:T(1,128)S(1)}, u32[]{:S(2)}, u32[]{:S(2)}) %collective-permute-start.8) | collective-permute-done | bytes 1568 | tf_op jit(solution)/shard_map/ppermute | solution.py:551
  117.8 0.0 collective-permute-done.9
  117.8 2.4 %collective-permute-start.11 = (f32[1,384]{1,0:T(1,128)S(1)}, f32[1,384]{1,0:T(1,128)S(1)}, u32[]{:S(2)}, u32[]{:S(2)}) collective-permute-start(f32[1,384]{1,0:T(1,128)S(1)} %add_add_fusion.1), channel_id=1, source_target_pairs={{0,4},{1,5},{2,6},{3,7},{4,8},{5,9},{6,10},{7,11},{8,12},{9,13},{1... | collective-permute-start | bytes 4616 | tf_op jit(solution)/shard_map/ppermute | solution.py:515
  120.3 2.8 %collective-permute-start.12 = (f32[1,384]{1,0:T(1,128)S(1)}, f32[1,384]{1,0:T(1,128)S(1)}, u32[]{:S(2)}, u32[]{:S(2)}) collective-permute-start(f32[1,384]{1,0:T(1,128)S(1)} %add_add_fusion.1), channel_id=1, source_target_pairs={{0,8},{1,9},{2,10},{3,11},{4,12},{5,13},{6,14},{7,15},{8,0},{9,1},... | collective-permute-start | bytes 4616 | tf_op jit(solution)/shard_map/ppermute | solution.py:515
  123.0 0.0 collective-permute-start.13
  123.1 0.0 all-to-all-done.3.got_ref
  123.1 0.0 copy-done.7
  123.1 0.0 copy-done.5
  123.1 1.9 %final.1 = bf16[512,768]{1,0:T(8,128)(2,1)} custom-call(bf16[512,768]{1,0:T(8,128)(2,1)S(1)} %copy-done.7, bf16[4,784,128]{2,1,0:T(8,128)(2,1)S(1)} %all-to-all-done.3.got_ref, bf16[768,768]{1,0:T(8,128)(2,1)S(1)} %copy-done.5), custom_call_target="tpu_custom_call" | custom-call | flops 1000000000 | bytes 4000000 | tf_op jit(solution)/shard_map/final/pallas_call | solution.py:555
  125.0 0.0 collective-permute-done.11
  125.0 0.4 collective-permute-done.12
  125.3 1.3 %collective-permute-done.13 = f32[1,384]{1,0:T(1,128)S(1)} collective-permute-done((f32[1,384]{1,0:T(1,128)S(1)}, f32[1,384]{1,0:T(1,128)S(1)}, u32[]{:S(2)}, u32[]{:S(2)}) %collective-permute-start.13) | collective-permute-done | bytes 1568 | tf_op jit(solution)/shard_map/ppermute | solution.py:515
  126.6 0.6 slice.9
  127.9 0.6 fusion
  (2 shorter events, 0.0 us)
Async XLA Ops:
  0.6 0.7 copy-start.2
  1.3 0.7 copy-start.4
  3.7 32.9 %collective-permute-start.1 = (bf16[264,768]{1,0:T(8,128)(2,1)S(1)}, bf16[264,768]{1,0:T(8,128)(2,1)S(1)}, u32[]{:S(2)}, u32[]{:S(2)}) collective-permute-start(bf16[264,768]{1,0:T(8,128)(2,1)S(1)} %get-tuple-element.27), channel_id=1, source_target_pairs={{1,0},{2,1},{3,2},{4,3},{5,4},{6,5},{7,6},{8,7},{9,8},{10,9},{11,1... | collective-permute-start | bytes 1216520 | tf_op jit(solution)/shard_map/ppermute | solution.py:438
  6.1 30.5 %collective-permute-start = (bf16[264,768]{1,0:T(8,128)(2,1)S(1)}, bf16[264,768]{1,0:T(8,128)(2,1)S(1)}, u32[]{:S(2)}, u32[]{:S(2)}) collective-permute-start(bf16[264,768]{1,0:T(8,128)(2,1)S(1)} %get-tuple-element.26), channel_id=1, source_target_pairs={{0,1},{1,2},{2,3},{3,4},{4,5},{5,6},{6,7},{7,8},{8,9},{9,10},{10,1... | collective-permute-start | bytes 1216520 | tf_op jit(solution)/shard_map/ppermute | solution.py:437
  9.6 9.8 %all-to-all-start = ((s32[8,1,320]{2,1,0:T(1,128)}), s32[8,1,320]{2,1,0:T(1,128)S(1)}, u32[]{:S(2)}, u32[]{:S(2)}) async-start(s32[8,1,320]{2,1,0:T(1,128)} %get-tuple-element.22), calls=%async_computation | async-start | bytes 24576 | tf_op jit(solution)/shard_map/all_to_all | solution.py:426
  14.2 0.9 copy-start.1
  26.2 10.4 %copy-start = (bf16[1,512,768]{2,1,0:T(8,128)(2,1)S(1)}, bf16[1,512,768]{2,1,0:T(8,128)(2,1)}, u32[]{:S(2)}) copy-start(bf16[1,512,768]{2,1,0:T(8,128)(2,1)} %param.10) | copy-start | bytes 2359300
  26.3 10.4 %copy-start.3 = (s32[1,512]{1,0:T(1,128)S(1)}, s32[1,512]{1,0:T(1,128)}, u32[]{:S(2)}) copy-start(s32[1,512]{1,0:T(1,128)} %tokens_ref.3) | copy-start | bytes 6148
  26.3 26.4 %all-to-all-start.2 = ((bf16[128,8,384]{2,1,0:T(8,128)(2,1)}), bf16[128,8,384]{2,1,0:T(8,128)(2,1)S(1)}, u32[]{:S(2)}, u32[]{:S(2)}) async-start(bf16[128,8,384]{2,1,0:T(8,128)(2,1)} %bitcast.5), calls=%async_computation.2 | async-start | bytes 1572864 | tf_op jit(solution)/shard_map/all_to_all | solution.py:462
  50.2 0.9 copy-start.6
  52.6 21.4 %all-to-all-start.1 = ((bf16[4,784,128]{2,1,0:T(8,128)(2,1)}), bf16[4,784,128]{2,1,0:T(8,128)(2,1)S(1)}, u32[]{:S(2)}, u32[]{:S(2)}) async-start(bf16[4,784,128]{2,1,0:T(8,128)(2,1)} %get-tuple-element.28), calls=%async_computation.1 | async-start | bytes 1605632 | tf_op jit(solution)/shard_map/all_to_all | solution.py:495
  58.3 10.2 %collective-permute-start.5 = (bf16[640,128]{1,0:T(8,128)(2,1)S(1)}, bf16[640,128]{1,0:T(8,128)(2,1)S(1)}, u32[]{:S(2)}, u32[]{:S(2)}) collective-permute-start(bf16[640,128]{1,0:T(8,128)(2,1)S(1)} %get-tuple-element.32.refs_0_), channel_id=1, source_target_pairs={{0,4},{1,5},{2,6},{3,7},{4,8},{5,9},{6,10},{7,11},{8,12},{9,13},{1... | collective-permute-start | bytes 491528 | tf_op jit(solution)/shard_map/ppermute | solution.py:515
  59.2 11.0 %collective-permute-start.6 = (bf16[640,128]{1,0:T(8,128)(2,1)S(1)}, bf16[640,128]{1,0:T(8,128)(2,1)S(1)}, u32[]{:S(2)}, u32[]{:S(2)}) collective-permute-start(bf16[640,128]{1,0:T(8,128)(2,1)S(1)} %get-tuple-element.32.refs_0_), channel_id=1, source_target_pairs={{0,8},{1,9},{2,10},{3,11},{4,12},{5,13},{6,14},{7,15},{8,0},{9,1},... | collective-permute-start | bytes 491528 | tf_op jit(solution)/shard_map/ppermute | solution.py:515
  61.7 12.4 %collective-permute-start.7 = (bf16[640,128]{1,0:T(8,128)(2,1)S(1)}, bf16[640,128]{1,0:T(8,128)(2,1)S(1)}, u32[]{:S(2)}, u32[]{:S(2)}) collective-permute-start(bf16[640,128]{1,0:T(8,128)(2,1)S(1)} %get-tuple-element.32.refs_0_), channel_id=1, source_target_pairs={{0,12},{1,13},{2,14},{3,15},{4,0},{5,1},{6,2},{7,3},{8,4},{9,5},{1... | collective-permute-start | bytes 491528 | tf_op jit(solution)/shard_map/ppermute | solution.py:515
  62.9 20.6 %collective-permute-start.2 = (bf16[640,256]{1,0:T(8,128)(2,1)S(1)}, bf16[640,256]{1,0:T(8,128)(2,1)S(1)}, u32[]{:S(2)}, u32[]{:S(2)}) collective-permute-start(bf16[640,256]{1,0:T(8,128)(2,1)S(1)} %get-tuple-element.31.refs_0_), channel_id=1, source_target_pairs={{0,4},{1,5},{2,6},{3,7},{4,8},{5,9},{6,10},{7,11},{8,12},{9,13},{1... | collective-permute-start | bytes 983048 | tf_op jit(solution)/shard_map/ppermute | solution.py:515
  63.7 19.8 %collective-permute-start.3 = (bf16[640,256]{1,0:T(8,128)(2,1)S(1)}, bf16[640,256]{1,0:T(8,128)(2,1)S(1)}, u32[]{:S(2)}, u32[]{:S(2)}) collective-permute-start(bf16[640,256]{1,0:T(8,128)(2,1)S(1)} %get-tuple-element.31.refs_0_), channel_id=1, source_target_pairs={{0,8},{1,9},{2,10},{3,11},{4,12},{5,13},{6,14},{7,15},{8,0},{9,1},... | collective-permute-start | bytes 983048 | tf_op jit(solution)/shard_map/ppermute | solution.py:515
  68.5 15.0 %collective-permute-start.4 = (bf16[640,256]{1,0:T(8,128)(2,1)S(1)}, bf16[640,256]{1,0:T(8,128)(2,1)S(1)}, u32[]{:S(2)}, u32[]{:S(2)}) collective-permute-start(bf16[640,256]{1,0:T(8,128)(2,1)S(1)} %get-tuple-element.31.refs_0_), channel_id=1, source_target_pairs={{0,12},{1,13},{2,14},{3,15},{4,0},{5,1},{6,2},{7,3},{8,4},{9,5},{1... | collective-permute-start | bytes 983048 | tf_op jit(solution)/shard_map/ppermute | solution.py:515
  83.5 39.6 %copy-start.7 = (bf16[512,768]{1,0:T(8,128)(2,1)S(1)}, bf16[512,768]{1,0:T(8,128)(2,1)}, u32[]{:S(2)}) copy-start(bf16[512,768]{1,0:T(8,128)(2,1)} %copy-done.6) | copy-start | bytes 2359300
  103.1 20.0 %copy-start.5 = (bf16[768,768]{1,0:T(8,128)(2,1)S(1)}, bf16[768,768]{1,0:T(8,128)(2,1)}, u32[]{:S(2)}) copy-start(bf16[768,768]{1,0:T(8,128)(2,1)} %weight_ref.1) | copy-start | bytes 3538948
  103.1 20.0 %all-to-all-start.3 = ((bf16[4,784,128]{2,1,0:T(8,128)(2,1)}), bf16[4,784,128]{2,1,0:T(8,128)(2,1)S(1)}, u32[]{:S(2)}, u32[]{:S(2)}) async-start(bf16[4,784,128]{2,1,0:T(8,128)(2,1)} %get-tuple-element.37), calls=%async_computation.3 | async-start | bytes 1605632 | tf_op jit(solution)/shard_map/all_to_all | solution.py:495
  108.0 7.6 %collective-permute-start.10 = (f32[1,384]{1,0:T(1,128)S(1)}, f32[1,384]{1,0:T(1,128)S(1)}, u32[]{:S(2)}, u32[]{:S(2)}) collective-permute-start(f32[1,384]{1,0:T(1,128)S(1)} %get-tuple-element.35), channel_id=1, source_target_pairs={{0,3},{1,0},{2,1},{3,2},{4,7},{5,4},{6,5},{7,6},{8,11},{9,8},{10,9... | collective-permute-start | bytes 4616 | tf_op jit(solution)/shard_map/ppermute | solution.py:551
  108.1 9.8 %collective-permute-start.8 = (f32[1,384]{1,0:T(1,128)S(1)}, f32[1,384]{1,0:T(1,128)S(1)}, u32[]{:S(2)}, u32[]{:S(2)}) collective-permute-start(f32[1,384]{1,0:T(1,128)S(1)} %get-tuple-element.35), channel_id=1, source_target_pairs={{0,2},{1,3},{2,0},{3,1},{4,6},{5,7},{6,4},{7,5},{8,10},{9,11},{10,... | collective-permute-start | bytes 4616 | tf_op jit(solution)/shard_map/ppermute | solution.py:551
  111.0 6.9 %collective-permute-start.9 = (f32[1,384]{1,0:T(1,128)S(1)}, f32[1,384]{1,0:T(1,128)S(1)}, u32[]{:S(2)}, u32[]{:S(2)}) collective-permute-start(f32[1,384]{1,0:T(1,128)S(1)} %get-tuple-element.35), channel_id=1, source_target_pairs={{0,1},{1,2},{2,3},{3,0},{4,5},{5,6},{6,7},{7,4},{8,9},{9,10},{10,1... | collective-permute-start | bytes 4616 | tf_op jit(solution)/shard_map/ppermute | solution.py:551
  117.8 7.1 %collective-permute-start.11 = (f32[1,384]{1,0:T(1,128)S(1)}, f32[1,384]{1,0:T(1,128)S(1)}, u32[]{:S(2)}, u32[]{:S(2)}) collective-permute-start(f32[1,384]{1,0:T(1,128)S(1)} %add_add_fusion.1), channel_id=1, source_target_pairs={{0,4},{1,5},{2,6},{3,7},{4,8},{5,9},{6,10},{7,11},{8,12},{9,13},{1... | collective-permute-start | bytes 4616 | tf_op jit(solution)/shard_map/ppermute | solution.py:515
  120.3 5.1 %collective-permute-start.12 = (f32[1,384]{1,0:T(1,128)S(1)}, f32[1,384]{1,0:T(1,128)S(1)}, u32[]{:S(2)}, u32[]{:S(2)}) collective-permute-start(f32[1,384]{1,0:T(1,128)S(1)} %add_add_fusion.1), channel_id=1, source_target_pairs={{0,8},{1,9},{2,10},{3,11},{4,12},{5,13},{6,14},{7,15},{8,0},{9,1},... | collective-permute-start | bytes 4616 | tf_op jit(solution)/shard_map/ppermute | solution.py:515
  123.0 3.6 %collective-permute-start.13 = (f32[1,384]{1,0:T(1,128)S(1)}, f32[1,384]{1,0:T(1,128)S(1)}, u32[]{:S(2)}, u32[]{:S(2)}) collective-permute-start(f32[1,384]{1,0:T(1,128)S(1)} %add_add_fusion.1), channel_id=1, source_target_pairs={{0,12},{1,13},{2,14},{3,15},{4,0},{5,1},{6,2},{7,3},{8,4},{9,5},{1... | collective-permute-start | bytes 4616 | tf_op jit(solution)/shard_map/ppermute | solution.py:515

commit v6 on v5

--- a/solution.py
+++ b/solution.py
@@ -183,7 +183,7 @@
     return centered * lax.rsqrt(spread + 1e-05)
 
 
-def halo_kernel(hidden_hbm, tokens_ref, wanted_ref, tail_ref, head_ref, asked_ref, sems):
+def halo_kernel(hidden_hbm, tokens_hbm, wanted_hbm, tail_ref, head_ref, asked_ref, tokens_ref, wanted_ref, sems):
     tok, width = hidden_hbm.shape
     win = HALF_WIN
     places = ((tail_ref, tok - win), (head_ref, 0))
@@ -191,8 +191,16 @@
     for k, (ref, start) in enumerate(places):
         copies.append(pltpu.make_async_copy(hidden_hbm.at[pl.ds(start, win), :], ref.at[pl.ds(0, win), :], sems.at[k]))
         copies[-1].start()
+    small = [
+        pltpu.make_async_copy(wanted_hbm, wanted_ref, sems.at[2]),
+        pltpu.make_async_copy(tokens_hbm, tokens_ref, sems.at[3]),
+    ]
+    for copy in small:
+        copy.start()
+    small[0].wait()
     for d in range(asked_ref.shape[0]):
         asked_ref[d] = wanted_ref[...]
+    small[1].wait()
     flags = (tokens_ref[...] != 0).astype(F32)
     for ref, start in places:
         row = jnp.concatenate([flags[:, start : start + win], jnp.zeros((1, width - win), F32)], axis=1)
@@ -417,12 +425,12 @@
         name="halo",
         out_shape=(jax.ShapeDtypeStruct((HALF_WIN + 8, width), BF),) * 2
         + (jax.ShapeDtypeStruct((docs, 1, count), I32),),
-        in_specs=[hbm(), vmem(), vmem()],
+        in_specs=[hbm()] * 3,
         out_specs=(vmem(),) * 3,
-        scratch_shapes=[pltpu.SemaphoreType.DMA((2,))],
+        scratch_shapes=[pltpu.VMEM((1, tok), I32), pltpu.VMEM((1, count), I32), pltpu.SemaphoreType.DMA((4,))],
         compiler_params=params(16),
         cost_estimate=cost(10**5, 0, 16 * 10**5),
-    )(pinned(doc_hidden), token_ids, shortlist)
+    )(*map(pinned, (doc_hidden, token_ids, shortlist)))
     all_codes = lax.all_to_all(asked, "doc", split_axis=0, concat_axis=0, tiled=True)
     table, head = lax.optimization_barrier((table, head))
     planes = pl.pallas_call(
@@ -485,7 +493,7 @@
             pltpu.VMEM((tok // HALF_WIN, HALF_WIN, 3 * HALF_WIN), F32),
             pltpu.SemaphoreType.DMA((4,)),
         ],
-        compiler_params=params(32),
+        compiler_params=params(26),
         cost_estimate=cost(12 * 10**9, 5 * 10**6, 10**7),
     )(low, doc_hidden, high, token_ids, *map(pinned, (w_keyval, w_query, w_out, x_query)))
 
@@ -515,7 +523,9 @@
             parts.append(lax.ppermute(block, "seq", pairs))
         return parts
 
-    first, rest = [[block] + turns(block) for block in blocks]
+    block, rest_block = blocks
+    *arrived, rest_block = lax.optimization_barrier((*turns(block), rest_block))
+    first, rest = [block] + arrived, [rest_block] + turns(rest_block)
 
     def cross(heads, parts, extra, outs):
         return pl.pallas_call(
@@ -530,7 +540,7 @@
                 pltpu.VMEM((2, tok, GRID * held), BF),
                 pltpu.VMEM((8, GRID * held), F32),
             ],
-            compiler_params=params(24),
+            compiler_params=params(18),
             cost_estimate=cost(len(heads) * 10**10, 5 * 10**6, 4 * 10**6),
         )(where, pos, queries, *parts, *extra)
 
@@ -551,6 +561,10 @@
     one, two, three = [lax.ppermute(score, "seq", pairs) for pairs in across_x]
     score = (score + two) + (one + three)
     one, two, three = turns(score)
+    sums = (score + two) + (one + three)
+    tokens = sums[:, count : count + 1] * (1.0 / GRID)
+    cand_score = count * sums[:, :count] / (HEADS * tokens)
+    out = across(out)
 
     refined = pl.pallas_call(
         final_kernel,
@@ -560,11 +574,7 @@
         out_specs=vmem(),
         compiler_params=params(16),
         cost_estimate=cost(10**9, 0, 4 * 10**6),
-    )(middle, across(out), x_out)
-    one, two, three, refined = lax.optimization_barrier((one, two, three, refined))
-    sums = (score + two) + (one + three)
-    tokens = sums[:, count : count + 1] * (1.0 / GRID)
-    cand_score = count * sums[:, :count] / (HEADS * tokens)
+    )(middle, out, x_out)
     return (refined[None], cand_score)
 
 

time: 130 us -> 126 us (0.969); the launches traced: 128 us -> 126 us
  local copies, waits for them, and re-layouts: 3.75 us -> 2.39 us
    ppermute x3, waiting for transfers between devices: 5.09 us -> 0.01 us  [local(): one, two, three = [lax.ppermute(score, 'seq', pairs) for pairs in across_x]]
    ppermute x9, waiting for transfers between devices: 11 us -> 15.8 us  [turns(): parts.append(lax.ppermute(block, 'seq', pairs))]
    all_to_all x1, starting transfers between devices: 10.3 us -> 8.9 us  [local(): lax.all_to_all(send.reshape(devices, DESC, 3 * LANES), ('doc', 'seq'), sp...]
    unnamed x16 -> x12, local copies, waits for them, and re-layouts: 3.16 us -> 1.81 us
  transfers between devices with their start and end apart: 18 -> 18, of which waited for: 9 -> 8; matrix products, arithmetic and copies ran while one was open for 0% -> 1% of each run, Pallas kernels for 25% -> 24%
where the time goes in v6:
time: 126 us
  Pallas kernels  54 us (43%)
  starting transfers between devices  45.7 us (36%)
  waiting for transfers between devices  21.6 us (17%)
  local copies, waits for them, and re-layouts  2.39 us (2%)
  between operations  1.44 us (1%)
    pallas_call x2, Pallas kernels, cross(): pl.pallas_call(functools.partial(cross_kernel, heads, count), name='cross...  29 us
    ppermute x9, waiting for transfers between devices, turns(): parts.append(lax.ppermute(block, 'seq', pairs))  15.8 us
    pallas_call x1, Pallas kernels, local(): pl.pallas_call(window_kernel, name='window', out_shape=(jax.ShapeDtypeStr...  13.6 us
    ppermute x9, starting transfers between devices, turns(): parts.append(lax.ppermute(block, 'seq', pairs))  12.6 us
    all_to_all x2, starting transfers between devices, across(): lax.all_to_all(block, 'seq', split_axis=0, concat_axis=0, axis_index_grou...  9.75 us
    all_to_all x1, starting transfers between devices, local(): lax.all_to_all(send.reshape(devices, DESC, 3 * LANES), ('doc', 'seq'), sp...  8.9 us
    pallas_call x1, Pallas kernels, local(): pl.pallas_call(functools.partial(route_kernel, count, code_dev, devices),...  6.81 us
    all_to_all x1, starting transfers between devices, local(): lax.all_to_all(asked, 'doc', split_axis=0, concat_axis=0, tiled=True)  4.48 us
  transfers between devices with their start and end apart: 18, of which 8 were waited for; matrix products, arithmetic and copies ran while one was open for 1% of the time, Pallas kernels for 24%

profile of v6, /device:TPU:2, one launch (start us, length us, event | category | flops | bytes accessed | tf_op | source)
XLA Modules:
  0.0 125.8 jit_solution(12655561977847797788)
XLA Ops:
  0.6 1.8 %halo.1 = (bf16[264,768]{1,0:T(8,128)(2,1)S(1)}, bf16[264,768]{1,0:T(8,128)(2,1)S(1)}, s32[8,1,320]{2,1,0:T(1,128)}) custom-call(bf16[512,768]{1,0:T(8,128)(2,1)} %bitcast.10, s32[1,512]{1,0:T(1,128)} %tokens_ref.1, s32[1,320]{1,0:T(1,128)} %wanted_hbm.1), custom_call_target="tpu_custom_call" | custom-call | flops 100000 | bytes 1600000 | tf_op jit(solution)/shard_map/halo/pallas_call | solution.py:423
  2.4 3.4 %collective-permute-start = (bf16[264,768]{1,0:T(8,128)(2,1)S(1)}, bf16[264,768]{1,0:T(8,128)(2,1)S(1)}, u32[]{:S(2)}, u32[]{:S(2)}) collective-permute-start(bf16[264,768]{1,0:T(8,128)(2,1)S(1)} %get-tuple-element.22), channel_id=1, source_target_pairs={{0,1},{1,2},{2,3},{3,4},{4,5},{5,6},{6,7},{7,8},{8,9},{9,10},{10,1... | collective-permute-start | bytes 1216520 | tf_op jit(solution)/shard_map/ppermute | solution.py:445
  5.8 2.5 %collective-permute-start.1 = (bf16[264,768]{1,0:T(8,128)(2,1)S(1)}, bf16[264,768]{1,0:T(8,128)(2,1)S(1)}, u32[]{:S(2)}, u32[]{:S(2)}) collective-permute-start(bf16[264,768]{1,0:T(8,128)(2,1)S(1)} %get-tuple-element.24), channel_id=1, source_target_pairs={{1,0},{2,1},{3,2},{4,3},{5,4},{6,5},{7,6},{8,7},{9,8},{10,9},{11,1... | collective-permute-start | bytes 1216520 | tf_op jit(solution)/shard_map/ppermute | solution.py:446
  8.3 4.5 %all-to-all-start = ((s32[8,1,320]{2,1,0:T(1,128)}), s32[8,1,320]{2,1,0:T(1,128)S(1)}, u32[]{:S(2)}, u32[]{:S(2)}) async-start(s32[8,1,320]{2,1,0:T(1,128)} %get-tuple-element.26), calls=%async_computation | async-start | bytes 24576 | tf_op jit(solution)/shard_map/all_to_all | solution.py:434
  12.8 0.1 pad_add_fusion.where_ref
  12.8 0.0 copy-start.1
  12.8 0.9 copy-done.1
  13.7 0.1 planes.1.planes_ref
  13.9 4.2 %all-to-all-done.codes_ref = s32[8,1,320]{2,1,0:T(1,128)S(1)} async-done(((s32[8,1,320]{2,1,0:T(1,128)}), s32[8,1,320]{2,1,0:T(1,128)S(1)}, u32[]{:S(2)}, u32[]{:S(2)}) %all-to-all-start) | async-done | bytes 10272 | tf_op jit(solution)/shard_map/all_to_all | solution.py:434
  18.1 6.8 %route.1 = (bf16[32,4,8,384]{3,2,1,0:T(8,128)(2,1)}, s32[1,1024]{1,0:T(1,128)S(1)}, s32[1,384]{1,0:T(1,128)S(1)}) custom-call(s32[3]{0:T(128)S(1)} %pad_add_fusion.where_ref, s32[8,1,320]{2,1,0:T(1,128)S(1)} %all-to-all-done.codes_ref, bf16[256,384]{1,0:T(8,128)(2,1)S(1)} %planes.1.planes_ref, bf16[288,2,8,768]{3,2,1,0:T(8,128)(2,1)} %cache_ref.1), custom_call_target="tpu_custom_call" | custom-call | flops 1000000000 | bytes 2000000 | tf_op jit(solution)/shard_map/route/pallas_call | solution.py:448
  24.9 0.0 copy-start
  24.9 0.0 copy-start.2
  24.9 8.9 %all-to-all-start.2 = ((bf16[128,8,384]{2,1,0:T(8,128)(2,1)}), bf16[128,8,384]{2,1,0:T(8,128)(2,1)S(1)}, u32[]{:S(2)}, u32[]{:S(2)}) async-start(bf16[128,8,384]{2,1,0:T(8,128)(2,1)} %bitcast.5), calls=%async_computation.2 | async-start | bytes 1572864 | tf_op jit(solution)/shard_map/all_to_all | solution.py:470
  33.8 0.0 collective-permute-done.low_ref
  33.9 0.0 collective-permute-done.1.high_ref
  33.9 0.0 copy-done
  33.9 0.0 copy-done.2
  33.9 13.6 %window.1 = (bf16[512,768]{1,0:T(8,128)(2,1)S(1)}, bf16[4,784,128]{2,1,0:T(8,128)(2,1)}) custom-call(bf16[264,768]{1,0:T(8,128)(2,1)S(1)} %collective-permute-done.low_ref, bf16[512,768]{1,0:T(8,128)(2,1)S(1)} %bitcast.11, bf16[264,768]{1,0:T(8,128)(2,1)S(1)} %collective-permute-done.1.high_ref, s32[1,512]{1,0:T(1,128)S(1)} %copy-done.2, ...), custom_call_target="tpu_custom_call" | custom-call | flops 12000000000 | bytes 10000000 | tf_op jit(solution)/shard_map/window/pallas_call | solution.py:474
  47.5 0.0 copy-start.4
  47.5 0.9 copy-done.4
  48.4 1.5 %all-to-all-done.2 = bf16[128,8,384]{2,1,0:T(8,128)(2,1)S(1)} async-done(((bf16[128,8,384]{2,1,0:T(8,128)(2,1)}), bf16[128,8,384]{2,1,0:T(8,128)(2,1)S(1)}, u32[]{:S(2)}, u32[]{:S(2)}) %all-to-all-start.2) | async-done | bytes 786464 | tf_op jit(solution)/shard_map/all_to_all | solution.py:470
  49.9 4.8 %all-to-all-start.1 = ((bf16[4,784,128]{2,1,0:T(8,128)(2,1)}), bf16[4,784,128]{2,1,0:T(8,128)(2,1)S(1)}, u32[]{:S(2)}, u32[]{:S(2)}) async-start(bf16[4,784,128]{2,1,0:T(8,128)(2,1)} %get-tuple-element.29), calls=%async_computation.1 | async-start | bytes 1605632 | tf_op jit(solution)/shard_map/all_to_all | solution.py:503
  54.7 0.8 compact.1
  55.6 0.9 collective-permute-start.2
  56.5 2.4 %collective-permute-start.3 = (bf16[640,128]{1,0:T(8,128)(2,1)S(1)}, bf16[640,128]{1,0:T(8,128)(2,1)S(1)}, u32[]{:S(2)}, u32[]{:S(2)}) collective-permute-start(bf16[640,128]{1,0:T(8,128)(2,1)S(1)} %get-tuple-element.32.refs_0_), channel_id=1, source_target_pairs={{0,8},{1,9},{2,10},{3,11},{4,12},{5,13},{6,14},{7,15},{8,0},{9,1},... | collective-permute-start | bytes 491528 | tf_op jit(solution)/shard_map/ppermute | solution.py:523
  58.9 1.2 collective-permute-start.4
  60.1 3.8 %collective-permute-done.2.refs_1_ = bf16[640,128]{1,0:T(8,128)(2,1)S(1)} collective-permute-done((bf16[640,128]{1,0:T(8,128)(2,1)S(1)}, bf16[640,128]{1,0:T(8,128)(2,1)S(1)}, u32[]{:S(2)}, u32[]{:S(2)}) %collective-permute-start.2) | collective-permute-done | bytes 163872 | tf_op jit(solution)/shard_map/ppermute | solution.py:523
  63.9 2.2 %collective-permute-done.3.refs_2_ = bf16[640,128]{1,0:T(8,128)(2,1)S(1)} collective-permute-done((bf16[640,128]{1,0:T(8,128)(2,1)S(1)}, bf16[640,128]{1,0:T(8,128)(2,1)S(1)}, u32[]{:S(2)}, u32[]{:S(2)}) %collective-permute-start.3) | collective-permute-done | bytes 163872 | tf_op jit(solution)/shard_map/ppermute | solution.py:523
  66.1 0.5 collective-permute-done.4.refs_3_
  66.6 1.2 collective-permute-start.5
  67.9 2.9 %collective-permute-start.6 = (bf16[640,256]{1,0:T(8,128)(2,1)S(1)}, bf16[640,256]{1,0:T(8,128)(2,1)S(1)}, u32[]{:S(2)}, u32[]{:S(2)}) collective-permute-start(bf16[640,256]{1,0:T(8,128)(2,1)S(1)} %get-tuple-element.34.refs_0_), channel_id=1, source_target_pairs={{0,8},{1,9},{2,10},{3,11},{4,12},{5,13},{6,14},{7,15},{8,0},{9,1},... | collective-permute-start | bytes 983048 | tf_op jit(solution)/shard_map/ppermute | solution.py:523
  70.8 0.3 collective-permute-start.7
  71.1 0.0 all-to-all-done.1.query_ref
  71.1 9.4 %cross.2 = (bf16[4,512,128]{2,1,0:T(8,128)(2,1)S(1)}, f32[8,2560]{1,0:T(8,128)S(1)}) custom-call(s32[3]{0:T(128)S(1)} %pad_add_fusion.where_ref, s32[1,384]{1,0:T(1,128)S(1)} %get-tuple-element.28.pos_ref, bf16[4,784,128]{2,1,0:T(8,128)(2,1)S(1)} %all-to-all-done.1.query_ref, bf16[640,128]{1,0:T(8,128)(2,1)S(1)} %get-tuple-element.32.refs_0_, ...), custom_call_target="tpu_custom_call" | custom-call | flops 10000000000 | bytes 4000000 | tf_op jit(solution)/shard_map/cross/pallas_call | solution.py:531
  80.5 0.0 collective-permute-done.5.refs_1_
  80.5 4.5 %collective-permute-done.6.refs_2_ = bf16[640,256]{1,0:T(8,128)(2,1)S(1)} collective-permute-done((bf16[640,256]{1,0:T(8,128)(2,1)S(1)}, bf16[640,256]{1,0:T(8,128)(2,1)S(1)}, u32[]{:S(2)}, u32[]{:S(2)}) %collective-permute-start.6) | collective-permute-done | bytes 327712 | tf_op jit(solution)/shard_map/ppermute | solution.py:523
  85.0 0.0 collective-permute-done.7.refs_3_
  85.0 0.0 copy-start.5
  85.0 19.6 %cross.3 = (bf16[4,784,128]{2,1,0:T(8,128)(2,1)}, f32[1,384]{1,0:T(1,128)S(1)}) custom-call(s32[3]{0:T(128)S(1)} %pad_add_fusion.where_ref, s32[1,384]{1,0:T(1,128)S(1)} %get-tuple-element.28.pos_ref, bf16[4,784,128]{2,1,0:T(8,128)(2,1)S(1)} %all-to-all-done.1.query_ref, bf16[640,256]{1,0:T(8,128)(2,1)S(1)} %get-tuple-element.34.refs_0_, ...), custom_call_target="tpu_custom_call" | custom-call | flops 20000000000 | bytes 4000000 | tf_op jit(solution)/shard_map/cross/pallas_call | solution.py:531
  104.6 0.0 copy-start.3
  104.6 1.5 %collective-permute-start.9 = (f32[1,384]{1,0:T(1,128)S(1)}, f32[1,384]{1,0:T(1,128)S(1)}, u32[]{:S(2)}, u32[]{:S(2)}) collective-permute-start(f32[1,384]{1,0:T(1,128)S(1)} %get-tuple-element.41), channel_id=1, source_target_pairs={{0,1},{1,2},{2,3},{3,0},{4,5},{5,6},{6,7},{7,4},{8,9},{9,10},{10,1... | collective-permute-start | bytes 4616 | tf_op jit(solution)/shard_map/ppermute | solution.py:561
  106.1 0.6 collective-permute-start.10
  106.6 2.1 %collective-permute-start.8 = (f32[1,384]{1,0:T(1,128)S(1)}, f32[1,384]{1,0:T(1,128)S(1)}, u32[]{:S(2)}, u32[]{:S(2)}) collective-permute-start(f32[1,384]{1,0:T(1,128)S(1)} %get-tuple-element.41), channel_id=1, source_target_pairs={{0,2},{1,3},{2,0},{3,1},{4,6},{5,7},{6,4},{7,5},{8,10},{9,11},{10,... | collective-permute-start | bytes 4616 | tf_op jit(solution)/shard_map/ppermute | solution.py:561
  108.7 4.9 %all-to-all-start.3 = ((bf16[4,784,128]{2,1,0:T(8,128)(2,1)}), bf16[4,784,128]{2,1,0:T(8,128)(2,1)S(1)}, u32[]{:S(2)}, u32[]{:S(2)}) async-start(bf16[4,784,128]{2,1,0:T(8,128)(2,1)} %get-tuple-element.40), calls=%async_computation.3 | async-start | bytes 1605632 | tf_op jit(solution)/shard_map/all_to_all | solution.py:503
  113.6 0.0 collective-permute-done.9
  113.6 0.0 collective-permute-done.10
  113.7 0.0 collective-permute-done.8
  113.7 0.8 collective-permute-start.12
  114.5 2.5 %collective-permute-start.13 = (f32[1,384]{1,0:T(1,128)S(1)}, f32[1,384]{1,0:T(1,128)S(1)}, u32[]{:S(2)}, u32[]{:S(2)}) collective-permute-start(f32[1,384]{1,0:T(1,128)S(1)} %add_add_fusion.1), channel_id=1, source_target_pairs={{0,12},{1,13},{2,14},{3,15},{4,0},{5,1},{6,2},{7,3},{8,4},{9,5},{1... | collective-permute-start | bytes 4616 | tf_op jit(solution)/shard_map/ppermute | solution.py:523
  117.0 0.3 collective-permute-start.11
  117.3 1.3 %collective-permute-done.12 = f32[1,384]{1,0:T(1,128)S(1)} collective-permute-done((f32[1,384]{1,0:T(1,128)S(1)}, f32[1,384]{1,0:T(1,128)S(1)}, u32[]{:S(2)}, u32[]{:S(2)}) %collective-permute-start.12) | collective-permute-done | bytes 1568 | tf_op jit(solution)/shard_map/ppermute | solution.py:523
  118.5 0.0 collective-permute-done.13
  118.5 3.5 %collective-permute-done.11 = f32[1,384]{1,0:T(1,128)S(1)} collective-permute-done((f32[1,384]{1,0:T(1,128)S(1)}, f32[1,384]{1,0:T(1,128)S(1)}, u32[]{:S(2)}, u32[]{:S(2)}) %collective-permute-start.11) | collective-permute-done | bytes 1568 | tf_op jit(solution)/shard_map/ppermute | solution.py:523
  122.1 0.6 slice.9
  123.3 0.6 fusion
  123.9 0.0 all-to-all-done.3.got_ref
  123.9 0.0 copy-done.5
  123.9 0.0 copy-done.3
  123.9 1.9 %final.1 = bf16[512,768]{1,0:T(8,128)(2,1)} custom-call(bf16[512,768]{1,0:T(8,128)(2,1)S(1)} %copy-done.5, bf16[4,784,128]{2,1,0:T(8,128)(2,1)S(1)} %all-to-all-done.3.got_ref, bf16[768,768]{1,0:T(8,128)(2,1)S(1)} %copy-done.3), custom_call_target="tpu_custom_call" | custom-call | flops 1000000000 | bytes 4000000 | tf_op jit(solution)/shard_map/final/pallas_call | solution.py:569
  (2 shorter events, 0.0 us)
Async XLA Ops:
  2.4 31.5 %collective-permute-start = (bf16[264,768]{1,0:T(8,128)(2,1)S(1)}, bf16[264,768]{1,0:T(8,128)(2,1)S(1)}, u32[]{:S(2)}, u32[]{:S(2)}) collective-permute-start(bf16[264,768]{1,0:T(8,128)(2,1)S(1)} %get-tuple-element.22), channel_id=1, source_target_pairs={{0,1},{1,2},{2,3},{3,4},{4,5},{5,6},{6,7},{7,8},{8,9},{9,10},{10,1... | collective-permute-start | bytes 1216520 | tf_op jit(solution)/shard_map/ppermute | solution.py:445
  5.8 28.1 %collective-permute-start.1 = (bf16[264,768]{1,0:T(8,128)(2,1)S(1)}, bf16[264,768]{1,0:T(8,128)(2,1)S(1)}, u32[]{:S(2)}, u32[]{:S(2)}) collective-permute-start(bf16[264,768]{1,0:T(8,128)(2,1)S(1)} %get-tuple-element.24), channel_id=1, source_target_pairs={{1,0},{2,1},{3,2},{4,3},{5,4},{6,5},{7,6},{8,7},{9,8},{10,9},{11,1... | collective-permute-start | bytes 1216520 | tf_op jit(solution)/shard_map/ppermute | solution.py:446
  8.3 9.8 %all-to-all-start = ((s32[8,1,320]{2,1,0:T(1,128)}), s32[8,1,320]{2,1,0:T(1,128)S(1)}, u32[]{:S(2)}, u32[]{:S(2)}) async-start(s32[8,1,320]{2,1,0:T(1,128)} %get-tuple-element.26), calls=%async_computation | async-start | bytes 24576 | tf_op jit(solution)/shard_map/all_to_all | solution.py:434
  12.8 0.9 copy-start.1
  24.9 9.0 %copy-start = (bf16[1,512,768]{2,1,0:T(8,128)(2,1)S(1)}, bf16[1,512,768]{2,1,0:T(8,128)(2,1)}, u32[]{:S(2)}) copy-start(bf16[1,512,768]{2,1,0:T(8,128)(2,1)} %param.10) | copy-start | bytes 2359300
  24.9 9.0 %copy-start.2 = (s32[1,512]{1,0:T(1,128)S(1)}, s32[1,512]{1,0:T(1,128)}, u32[]{:S(2)}) copy-start(s32[1,512]{1,0:T(1,128)} %tokens_ref.1) | copy-start | bytes 6148
  24.9 25.0 %all-to-all-start.2 = ((bf16[128,8,384]{2,1,0:T(8,128)(2,1)}), bf16[128,8,384]{2,1,0:T(8,128)(2,1)S(1)}, u32[]{:S(2)}, u32[]{:S(2)}) async-start(bf16[128,8,384]{2,1,0:T(8,128)(2,1)} %bitcast.5), calls=%async_computation.2 | async-start | bytes 1572864 | tf_op jit(solution)/shard_map/all_to_all | solution.py:470
  47.5 0.9 copy-start.4
  49.9 21.2 %all-to-all-start.1 = ((bf16[4,784,128]{2,1,0:T(8,128)(2,1)}), bf16[4,784,128]{2,1,0:T(8,128)(2,1)S(1)}, u32[]{:S(2)}, u32[]{:S(2)}) async-start(bf16[4,784,128]{2,1,0:T(8,128)(2,1)} %get-tuple-element.29), calls=%async_computation.1 | async-start | bytes 1605632 | tf_op jit(solution)/shard_map/all_to_all | solution.py:503
  55.6 8.4 %collective-permute-start.2 = (bf16[640,128]{1,0:T(8,128)(2,1)S(1)}, bf16[640,128]{1,0:T(8,128)(2,1)S(1)}, u32[]{:S(2)}, u32[]{:S(2)}) collective-permute-start(bf16[640,128]{1,0:T(8,128)(2,1)S(1)} %get-tuple-element.32.refs_0_), channel_id=1, source_target_pairs={{0,4},{1,5},{2,6},{3,7},{4,8},{5,9},{6,10},{7,11},{8,12},{9,13},{1... | collective-permute-start | bytes 491528 | tf_op jit(solution)/shard_map/ppermute | solution.py:523
  56.5 9.6 %collective-permute-start.3 = (bf16[640,128]{1,0:T(8,128)(2,1)S(1)}, bf16[640,128]{1,0:T(8,128)(2,1)S(1)}, u32[]{:S(2)}, u32[]{:S(2)}) collective-permute-start(bf16[640,128]{1,0:T(8,128)(2,1)S(1)} %get-tuple-element.32.refs_0_), channel_id=1, source_target_pairs={{0,8},{1,9},{2,10},{3,11},{4,12},{5,13},{6,14},{7,15},{8,0},{9,1},... | collective-permute-start | bytes 491528 | tf_op jit(solution)/shard_map/ppermute | solution.py:523
  58.9 7.7 %collective-permute-start.4 = (bf16[640,128]{1,0:T(8,128)(2,1)S(1)}, bf16[640,128]{1,0:T(8,128)(2,1)S(1)}, u32[]{:S(2)}, u32[]{:S(2)}) collective-permute-start(bf16[640,128]{1,0:T(8,128)(2,1)S(1)} %get-tuple-element.32.refs_0_), channel_id=1, source_target_pairs={{0,12},{1,13},{2,14},{3,15},{4,0},{5,1},{6,2},{7,3},{8,4},{9,5},{1... | collective-permute-start | bytes 491528 | tf_op jit(solution)/shard_map/ppermute | solution.py:523
  66.6 13.8 %collective-permute-start.5 = (bf16[640,256]{1,0:T(8,128)(2,1)S(1)}, bf16[640,256]{1,0:T(8,128)(2,1)S(1)}, u32[]{:S(2)}, u32[]{:S(2)}) collective-permute-start(bf16[640,256]{1,0:T(8,128)(2,1)S(1)} %get-tuple-element.34.refs_0_), channel_id=1, source_target_pairs={{0,4},{1,5},{2,6},{3,7},{4,8},{5,9},{6,10},{7,11},{8,12},{9,13},{1... | collective-permute-start | bytes 983048 | tf_op jit(solution)/shard_map/ppermute | solution.py:523
  67.9 17.1 %collective-permute-start.6 = (bf16[640,256]{1,0:T(8,128)(2,1)S(1)}, bf16[640,256]{1,0:T(8,128)(2,1)S(1)}, u32[]{:S(2)}, u32[]{:S(2)}) collective-permute-start(bf16[640,256]{1,0:T(8,128)(2,1)S(1)} %get-tuple-element.34.refs_0_), channel_id=1, source_target_pairs={{0,8},{1,9},{2,10},{3,11},{4,12},{5,13},{6,14},{7,15},{8,0},{9,1},... | collective-permute-start | bytes 983048 | tf_op jit(solution)/shard_map/ppermute | solution.py:523
  70.8 14.2 %collective-permute-start.7 = (bf16[640,256]{1,0:T(8,128)(2,1)S(1)}, bf16[640,256]{1,0:T(8,128)(2,1)S(1)}, u32[]{:S(2)}, u32[]{:S(2)}) collective-permute-start(bf16[640,256]{1,0:T(8,128)(2,1)S(1)} %get-tuple-element.34.refs_0_), channel_id=1, source_target_pairs={{0,12},{1,13},{2,14},{3,15},{4,0},{5,1},{6,2},{7,3},{8,4},{9,5},{1... | collective-permute-start | bytes 983048 | tf_op jit(solution)/shard_map/ppermute | solution.py:523
  85.0 38.9 %copy-start.5 = (bf16[512,768]{1,0:T(8,128)(2,1)S(1)}, bf16[512,768]{1,0:T(8,128)(2,1)}, u32[]{:S(2)}) copy-start(bf16[512,768]{1,0:T(8,128)(2,1)} %copy-done.4) | copy-start | bytes 2359300
  104.6 19.3 %copy-start.3 = (bf16[768,768]{1,0:T(8,128)(2,1)S(1)}, bf16[768,768]{1,0:T(8,128)(2,1)}, u32[]{:S(2)}) copy-start(bf16[768,768]{1,0:T(8,128)(2,1)} %weight_ref.1) | copy-start | bytes 3538948
  104.6 9.0 %collective-permute-start.9 = (f32[1,384]{1,0:T(1,128)S(1)}, f32[1,384]{1,0:T(1,128)S(1)}, u32[]{:S(2)}, u32[]{:S(2)}) collective-permute-start(f32[1,384]{1,0:T(1,128)S(1)} %get-tuple-element.41), channel_id=1, source_target_pairs={{0,1},{1,2},{2,3},{3,0},{4,5},{5,6},{6,7},{7,4},{8,9},{9,10},{10,1... | collective-permute-start | bytes 4616 | tf_op jit(solution)/shard_map/ppermute | solution.py:561
  106.1 7.6 %collective-permute-start.10 = (f32[1,384]{1,0:T(1,128)S(1)}, f32[1,384]{1,0:T(1,128)S(1)}, u32[]{:S(2)}, u32[]{:S(2)}) collective-permute-start(f32[1,384]{1,0:T(1,128)S(1)} %get-tuple-element.41), channel_id=1, source_target_pairs={{0,3},{1,0},{2,1},{3,2},{4,7},{5,4},{6,5},{7,6},{8,11},{9,8},{10,9... | collective-permute-start | bytes 4616 | tf_op jit(solution)/shard_map/ppermute | solution.py:561
  106.6 7.0 %collective-permute-start.8 = (f32[1,384]{1,0:T(1,128)S(1)}, f32[1,384]{1,0:T(1,128)S(1)}, u32[]{:S(2)}, u32[]{:S(2)}) collective-permute-start(f32[1,384]{1,0:T(1,128)S(1)} %get-tuple-element.41), channel_id=1, source_target_pairs={{0,2},{1,3},{2,0},{3,1},{4,6},{5,7},{6,4},{7,5},{8,10},{9,11},{10,... | collective-permute-start | bytes 4616 | tf_op jit(solution)/shard_map/ppermute | solution.py:561
  108.7 15.2 %all-to-all-start.3 = ((bf16[4,784,128]{2,1,0:T(8,128)(2,1)}), bf16[4,784,128]{2,1,0:T(8,128)(2,1)S(1)}, u32[]{:S(2)}, u32[]{:S(2)}) async-start(bf16[4,784,128]{2,1,0:T(8,128)(2,1)} %get-tuple-element.40), calls=%async_computation.3 | async-start | bytes 1605632 | tf_op jit(solution)/shard_map/all_to_all | solution.py:503
  113.7 4.9 %collective-permute-start.12 = (f32[1,384]{1,0:T(1,128)S(1)}, f32[1,384]{1,0:T(1,128)S(1)}, u32[]{:S(2)}, u32[]{:S(2)}) collective-permute-start(f32[1,384]{1,0:T(1,128)S(1)} %add_add_fusion.1), channel_id=1, source_target_pairs={{0,4},{1,5},{2,6},{3,7},{4,8},{5,9},{6,10},{7,11},{8,12},{9,13},{1... | collective-permute-start | bytes 4616 | tf_op jit(solution)/shard_map/ppermute | solution.py:523
  114.5 4.0 %collective-permute-start.13 = (f32[1,384]{1,0:T(1,128)S(1)}, f32[1,384]{1,0:T(1,128)S(1)}, u32[]{:S(2)}, u32[]{:S(2)}) collective-permute-start(f32[1,384]{1,0:T(1,128)S(1)} %add_add_fusion.1), channel_id=1, source_target_pairs={{0,12},{1,13},{2,14},{3,15},{4,0},{5,1},{6,2},{7,3},{8,4},{9,5},{1... | collective-permute-start | bytes 4616 | tf_op jit(solution)/shard_map/ppermute | solution.py:523
  117.0 5.1 %collective-permute-start.11 = (f32[1,384]{1,0:T(1,128)S(1)}, f32[1,384]{1,0:T(1,128)S(1)}, u32[]{:S(2)}, u32[]{:S(2)}) collective-permute-start(f32[1,384]{1,0:T(1,128)S(1)} %add_add_fusion.1), channel_id=1, source_target_pairs={{0,8},{1,9},{2,10},{3,11},{4,12},{5,13},{6,14},{7,15},{8,0},{9,1},... | collective-permute-start | bytes 4616 | tf_op jit(solution)/shard_map/ppermute | solution.py:523

commit v7 on v6

--- a/solution.py
+++ b/solution.py
@@ -289,16 +289,29 @@
 
 
 def cross_kernel(heads, count, where_ref, pos_ref, query_ref, *refs):
-    kv_refs, refs = refs[:GRID], refs[GRID:]
     last = 2 in heads
+    pieces = 1 if last else GRID
+    kv_refs, refs = refs[:pieces], refs[pieces:]
     if last:
-        before_ref, earlier_ref, out_ref, score_ref, keys, values, expds, total = refs
+        before_ref, earlier_hbm, out_ref, score_ref, keys, values, expds, total, earlier_ref, sems = refs
     else:
         out_ref, mass_ref, keys, values, expds, total = refs
-    held = kv_refs[0].shape[0]
+    held = keys.shape[1] // GRID
     tok = expds.shape[1]
     groups = query_ref.shape[0]
     half = tok // 2
+    copies = []
+    if last:
+        for k in range(len(heads)):
+            for c in range(GRID):
+                origin = (where_ref[1] + GRID - c) & (GRID - 1)
+                rows = pl.ds(pl.multiple_of(origin * held, held), held)
+                source = kv_refs[0].at[rows, pl.ds(k * LANES, LANES)]
+                target = keys.at[k, pl.ds(c * held, held), :]
+                copies.append(pltpu.make_async_copy(source, target, sems.at[k * GRID + c]))
+        copies.append(pltpu.make_async_copy(earlier_hbm, earlier_ref, sems.at[len(copies)]))
+    for copy in copies:
+        copy.start()
     small = iota((tok, LANES), 1) < HALF
     low = iota((half, LANES), 1) < HALF
     if last:
@@ -309,8 +322,12 @@
     for k, inner in enumerate(heads):
         for c in range(GRID):
             rows = pl.ds(c * held, held)
-            block = kv_refs[c][:, k * LANES : (k + 1) * LANES]
-            keys[k, rows, :] = block
+            if last:
+                copies[k * GRID + c].wait()
+                block = keys[k, rows, :]
+            else:
+                block = kv_refs[c][...]
+                keys[k, rows, :] = block
             scaled = block.astype(F32) * 2.0**-4
             values[k, rows, :] = jnp.where(lower == (inner == 1), scaled, 1.0).astype(BF)
 
@@ -352,6 +369,8 @@
         lax.fori_loop(0, groups // 2, body, 0)
         mass_ref[...] = total[...]
         return
+
+    copies[-1].wait()
 
     def body(g, carry):
         out_ref[g, :tok, :] = jnp.where(small, one(g, 0, 0), earlier_ref[g].astype(F32)).astype(BF)
@@ -504,8 +523,6 @@
             block, "seq", split_axis=0, concat_axis=0, axis_index_groups=lines, tiled=True
         )
 
-    queries = across(queries)
-
     blocks = pl.pallas_call(
         compact_kernel,
         name="compact",
@@ -523,23 +540,32 @@
             parts.append(lax.ppermute(block, "seq", pairs))
         return parts
 
+    *blocks, queries = lax.optimization_barrier((*blocks, queries))
     block, rest_block = blocks
-    *arrived, rest_block = lax.optimization_barrier((*turns(block), rest_block))
-    first, rest = [block] + arrived, [rest_block] + turns(rest_block)
+    queries = across(queries)
+    first = [block] + turns(block)
+    columns = [[GRID * z + x for z in range(GRID)] for x in range(GRID)]
+    rest = lax.all_gather(rest_block, "seq", axis=0, axis_index_groups=columns, tiled=True)
 
     def cross(heads, parts, extra, outs):
+        last = 2 in heads
+        scratch = [
+            pltpu.VMEM((len(heads), GRID * held, LANES), BF),
+            pltpu.VMEM((len(heads), GRID * held, LANES), BF),
+            pltpu.VMEM((2, tok, GRID * held), BF),
+            pltpu.VMEM((8, GRID * held), F32),
+        ]
+        kv_specs = [vmem()] * len(parts)
+        if last:
+            scratch += [pltpu.VMEM((GRID, tok, LANES), BF), pltpu.SemaphoreType.DMA((len(heads) * GRID + 1,))]
+            kv_specs = [hbm(), vmem(), hbm()]
         return pl.pallas_call(
             functools.partial(cross_kernel, heads, count),
             name="cross",
             out_shape=outs,
-            in_specs=[smem()] + [vmem()] * (2 + GRID + len(extra)),
+            in_specs=[smem(), vmem(), vmem(), *kv_specs],
             out_specs=jax.tree.map(lambda _: vmem(), outs),
-            scratch_shapes=[
-                pltpu.VMEM((len(heads), GRID * held, LANES), BF),
-                pltpu.VMEM((len(heads), GRID * held, LANES), BF),
-                pltpu.VMEM((2, tok, GRID * held), BF),
-                pltpu.VMEM((8, GRID * held), F32),
-            ],
+            scratch_shapes=scratch,
             compiler_params=params(18),
             cost_estimate=cost(len(heads) * 10**10, 5 * 10**6, 4 * 10**6),
         )(where, pos, queries, *parts, *extra)
@@ -552,8 +578,8 @@
     )
     out, score = cross(
         (1, 2),
-        rest,
-        (mass, out),
+        [pinned(rest)],
+        (mass, pinned(out)),
         (jax.ShapeDtypeStruct((GRID, message, LANES), BF), jax.ShapeDtypeStruct((1, padded), F32)),
     )
 

time: 126 us -> 139 us (1.10)
  between operations: 1.44 us -> 14.8 us
  starting transfers between devices: 45.7 us -> 42.9 us
  Pallas kernels: 54 us -> 55.7 us
    ppermute x9 -> x6, starting transfers between devices: 12.6 us -> 7.87 us  [turns(): parts.append(lax.ppermute(block, 'seq', pairs))]
    all_to_all x1, starting transfers between devices: 8.9 us -> 10.6 us  [local(): lax.all_to_all(send.reshape(devices, DESC, 3 * LANES), ('doc', 'seq'), sp...]
    ppermute x9 -> x6, waiting for transfers between devices: 15.8 us -> 14.9 us  [turns(): parts.append(lax.ppermute(block, 'seq', pairs))]
  transfers between devices with their start and end apart: 18 -> 16, of which waited for: 8 -> 7; matrix products, arithmetic and copies ran while one was open for 1% -> 1% of each run, Pallas kernels for 24% -> 22%
where the time goes in v7:
time: 139 us; the launch traced here: 138 us
  Pallas kernels  55.7 us (40%)
  starting transfers between devices  42.9 us (31%)
  waiting for transfers between devices  20.5 us (15%)
  between operations  14.8 us (11%)
  local copies, waits for them, and re-layouts  3.2 us (2%)
    pallas_call x2, Pallas kernels, cross(): pl.pallas_call(functools.partial(cross_kernel, heads, count), name='cross...  30 us
    ppermute x6, waiting for transfers between devices, turns(): parts.append(lax.ppermute(block, 'seq', pairs))  14.9 us
    pallas_call x1, Pallas kernels, local(): pl.pallas_call(window_kernel, name='window', out_shape=(jax.ShapeDtypeStr...  13.6 us
    all_to_all x1, starting transfers between devices, local(): lax.all_to_all(send.reshape(devices, DESC, 3 * LANES), ('doc', 'seq'), sp...  10.6 us
    all_to_all x2, starting transfers between devices, across(): lax.all_to_all(block, 'seq', split_axis=0, concat_axis=0, axis_index_grou...  8.56 us
    ppermute x6, starting transfers between devices, turns(): parts.append(lax.ppermute(block, 'seq', pairs))  7.87 us
    pallas_call x1, Pallas kernels, local(): pl.pallas_call(functools.partial(route_kernel, count, code_dev, devices),...  6.8 us
    ppermute x3, starting transfers between devices, local(): one, two, three = [lax.ppermute(score, 'seq', pairs) for pairs in across_x]  5.37 us
  transfers between devices with their start and end apart: 16, of which 7 were waited for; matrix products, arithmetic and copies ran while one was open for 1% of the time, Pallas kernels for 22%

profile of v7, /device:TPU:2, one launch (start us, length us, event | category | flops | bytes accessed | tf_op | source)
XLA Modules:
  0.0 137.8 jit_solution(8711196310556906469)
XLA Ops:
  7.2 1.8 %halo.1 = (bf16[264,768]{1,0:T(8,128)(2,1)S(1)}, bf16[264,768]{1,0:T(8,128)(2,1)S(1)}, s32[8,1,320]{2,1,0:T(1,128)}) custom-call(bf16[512,768]{1,0:T(8,128)(2,1)} %bitcast.10, s32[1,512]{1,0:T(1,128)} %tokens_ref.1, s32[1,320]{1,0:T(1,128)} %wanted_hbm.1), custom_call_target="tpu_custom_call" | custom-call | flops 100000 | bytes 1600000 | tf_op jit(solution)/shard_map/halo/pallas_call | solution.py:442
  8.9 2.4 %collective-permute-start.1 = (bf16[264,768]{1,0:T(8,128)(2,1)S(1)}, bf16[264,768]{1,0:T(8,128)(2,1)S(1)}, u32[]{:S(2)}, u32[]{:S(2)}) collective-permute-start(bf16[264,768]{1,0:T(8,128)(2,1)S(1)} %get-tuple-element.23), channel_id=1, source_target_pairs={{1,0},{2,1},{3,2},{4,3},{5,4},{6,5},{7,6},{8,7},{9,8},{10,9},{11,1... | collective-permute-start | bytes 1216520 | tf_op jit(solution)/shard_map/ppermute | solution.py:465
  11.3 3.5 %collective-permute-start = (bf16[264,768]{1,0:T(8,128)(2,1)S(1)}, bf16[264,768]{1,0:T(8,128)(2,1)S(1)}, u32[]{:S(2)}, u32[]{:S(2)}) collective-permute-start(bf16[264,768]{1,0:T(8,128)(2,1)S(1)} %get-tuple-element.21), channel_id=1, source_target_pairs={{0,1},{1,2},{2,3},{3,4},{4,5},{5,6},{6,7},{7,8},{8,9},{9,10},{10,1... | collective-permute-start | bytes 1216520 | tf_op jit(solution)/shard_map/ppermute | solution.py:464
  14.8 4.5 %all-to-all-start = ((s32[8,1,320]{2,1,0:T(1,128)}), s32[8,1,320]{2,1,0:T(1,128)S(1)}, u32[]{:S(2)}, u32[]{:S(2)}) async-start(s32[8,1,320]{2,1,0:T(1,128)} %get-tuple-element.25), calls=%async_computation | async-start | bytes 24576 | tf_op jit(solution)/shard_map/all_to_all | solution.py:453
  19.3 0.1 pad_add_fusion.where_ref
  19.3 0.0 copy-start.1
  19.3 0.9 copy-done.1
  20.3 0.1 planes.1.planes_ref
  20.4 4.2 %all-to-all-done.codes_ref = s32[8,1,320]{2,1,0:T(1,128)S(1)} async-done(((s32[8,1,320]{2,1,0:T(1,128)}), s32[8,1,320]{2,1,0:T(1,128)S(1)}, u32[]{:S(2)}, u32[]{:S(2)}) %all-to-all-start) | async-done | bytes 10272 | tf_op jit(solution)/shard_map/all_to_all | solution.py:453
  24.6 6.8 %route.1 = (bf16[32,4,8,384]{3,2,1,0:T(8,128)(2,1)}, s32[1,1024]{1,0:T(1,128)S(1)}, s32[1,384]{1,0:T(1,128)S(1)}) custom-call(s32[3]{0:T(128)S(1)} %pad_add_fusion.where_ref, s32[8,1,320]{2,1,0:T(1,128)S(1)} %all-to-all-done.codes_ref, bf16[256,384]{1,0:T(8,128)(2,1)S(1)} %planes.1.planes_ref, bf16[288,2,8,768]{3,2,1,0:T(8,128)(2,1)} %cache_ref.1), custom_call_target="tpu_custom_call" | custom-call | flops 1000000000 | bytes 2000000 | tf_op jit(solution)/shard_map/route/pallas_call | solution.py:467
  31.4 0.0 copy-start
  31.4 0.0 copy-start.2
  31.4 10.6 %all-to-all-start.1 = ((bf16[128,8,384]{2,1,0:T(8,128)(2,1)}), bf16[128,8,384]{2,1,0:T(8,128)(2,1)S(1)}, u32[]{:S(2)}, u32[]{:S(2)}) async-start(bf16[128,8,384]{2,1,0:T(8,128)(2,1)} %bitcast.5), calls=%async_computation.1 | async-start | bytes 1572864 | tf_op jit(solution)/shard_map/all_to_all | solution.py:489
  42.0 0.2 all-gather.2.cloned.1.call-start
  42.3 0.0 collective-permute-done.1.high_ref
  42.3 0.0 collective-permute-done.low_ref
  42.3 0.0 copy-done
  42.3 0.0 copy-done.2
  42.3 13.6 %window.1 = (bf16[512,768]{1,0:T(8,128)(2,1)S(1)}, bf16[4,784,128]{2,1,0:T(8,128)(2,1)}) custom-call(bf16[264,768]{1,0:T(8,128)(2,1)S(1)} %collective-permute-done.low_ref, bf16[512,768]{1,0:T(8,128)(2,1)S(1)} %bitcast.11, bf16[264,768]{1,0:T(8,128)(2,1)S(1)} %collective-permute-done.1.high_ref, s32[1,512]{1,0:T(1,128)S(1)} %copy-done.2, ...), custom_call_target="tpu_custom_call" | custom-call | flops 12000000000 | bytes 10000000 | tf_op jit(solution)/shard_map/window/pallas_call | solution.py:493
  55.9 0.0 copy-start.4
  55.9 0.9 copy-done.4
  56.8 1.3 all-to-all-done.1
  58.1 1.6 %compact.1 = (bf16[640,128]{1,0:T(8,128)(2,1)S(1)}, bf16[640,256]{1,0:T(8,128)(2,1)}) custom-call(s32[1,1024]{1,0:T(1,128)S(1)} %get-tuple-element.28.slot_ref, bf16[1024,384]{1,0:T(8,128)(2,1)S(1)} %bitcast.9), custom_call_target="tpu_custom_call" | custom-call | flops 1000000000 | bytes 2000000 | tf_op jit(solution)/shard_map/compact/pallas_call | solution.py:526
  59.7 0.0 all-gather.2.cloned.1.call-update
  59.7 4.8 %all-to-all-start.2 = ((bf16[4,784,128]{2,1,0:T(8,128)(2,1)}), bf16[4,784,128]{2,1,0:T(8,128)(2,1)S(1)}, u32[]{:S(2)}, u32[]{:S(2)}) async-start(bf16[4,784,128]{2,1,0:T(8,128)(2,1)} %get-tuple-element.33), calls=%async_computation.2 | async-start | bytes 1605632 | tf_op jit(solution)/shard_map/all_to_all | solution.py:522
  64.5 2.0 %collective-permute-start.4 = (bf16[640,128]{1,0:T(8,128)(2,1)S(1)}, bf16[640,128]{1,0:T(8,128)(2,1)S(1)}, u32[]{:S(2)}, u32[]{:S(2)}) collective-permute-start(bf16[640,128]{1,0:T(8,128)(2,1)S(1)} %get-tuple-element.35.refs_0_), channel_id=1, source_target_pairs={{0,12},{1,13},{2,14},{3,15},{4,0},{5,1},{6,2},{7,3},{8,4},{9,5},{1... | collective-permute-start | bytes 491528 | tf_op jit(solution)/shard_map/ppermute | solution.py:540
  66.5 0.9 collective-permute-start.3
  67.4 0.6 collective-permute-start.2
  68.0 5.4 %collective-permute-done.4.refs_3_ = bf16[640,128]{1,0:T(8,128)(2,1)S(1)} collective-permute-done((bf16[640,128]{1,0:T(8,128)(2,1)S(1)}, bf16[640,128]{1,0:T(8,128)(2,1)S(1)}, u32[]{:S(2)}, u32[]{:S(2)}) %collective-permute-start.4) | collective-permute-done | bytes 163872 | tf_op jit(solution)/shard_map/ppermute | solution.py:540
  73.4 2.8 %collective-permute-done.3.refs_2_ = bf16[640,128]{1,0:T(8,128)(2,1)S(1)} collective-permute-done((bf16[640,128]{1,0:T(8,128)(2,1)S(1)}, bf16[640,128]{1,0:T(8,128)(2,1)S(1)}, u32[]{:S(2)}, u32[]{:S(2)}) %collective-permute-start.3) | collective-permute-done | bytes 163872 | tf_op jit(solution)/shard_map/ppermute | solution.py:540
  76.3 3.1 %collective-permute-done.2.refs_1_ = bf16[640,128]{1,0:T(8,128)(2,1)S(1)} collective-permute-done((bf16[640,128]{1,0:T(8,128)(2,1)S(1)}, bf16[640,128]{1,0:T(8,128)(2,1)S(1)}, u32[]{:S(2)}, u32[]{:S(2)}) %collective-permute-start.2) | collective-permute-done | bytes 163872 | tf_op jit(solution)/shard_map/ppermute | solution.py:540
  79.4 0.0 all-to-all-done.2.query_ref
  79.4 9.4 %cross.2 = (bf16[4,512,128]{2,1,0:T(8,128)(2,1)S(1)}, f32[8,2560]{1,0:T(8,128)S(1)}) custom-call(s32[3]{0:T(128)S(1)} %pad_add_fusion.where_ref, s32[1,384]{1,0:T(1,128)S(1)} %get-tuple-element.27.pos_ref, bf16[4,784,128]{2,1,0:T(8,128)(2,1)S(1)} %all-to-all-done.2.query_ref, bf16[640,128]{1,0:T(8,128)(2,1)S(1)} %get-tuple-element.35.refs_0_, ...), custom_call_target="tpu_custom_call" | custom-call | flops 10000000000 | bytes 4000000 | tf_op jit(solution)/shard_map/cross/pallas_call | solution.py:562
  88.7 0.0 copy-start.6
  88.7 0.8 copy-done.6
  89.6 0.0 all-gather.2.cloned.1.call-done.refs_0_
  89.6 0.0 copy-start.5
  89.6 20.6 %cross.3 = (bf16[4,784,128]{2,1,0:T(8,128)(2,1)}, f32[1,384]{1,0:T(1,128)S(1)}) custom-call(s32[3]{0:T(128)S(1)} %pad_add_fusion.where_ref, s32[1,384]{1,0:T(1,128)S(1)} %get-tuple-element.27.pos_ref, bf16[4,784,128]{2,1,0:T(8,128)(2,1)S(1)} %all-to-all-done.2.query_ref, bf16[2560,256]{1,0:T(8,128)(2,1)} %all-gather.2.cloned.1.call-done.refs_0_, ...), custom_call_target="tpu_custom_call" | custom-call | flops 20000000000 | bytes 4000000 | tf_op jit(solution)/shard_map/cross/pallas_call | solution.py:562
  110.2 0.0 copy-start.3
  110.2 0.2 collective-permute-start.7
  110.4 1.9 %collective-permute-start.6 = (f32[1,384]{1,0:T(1,128)S(1)}, f32[1,384]{1,0:T(1,128)S(1)}, u32[]{:S(2)}, u32[]{:S(2)}) collective-permute-start(f32[1,384]{1,0:T(1,128)S(1)} %get-tuple-element.39), channel_id=1, source_target_pairs={{0,1},{1,2},{2,3},{3,0},{4,5},{5,6},{6,7},{7,4},{8,9},{9,10},{10,1... | collective-permute-start | bytes 4616 | tf_op jit(solution)/shard_map/ppermute | solution.py:587
  112.3 3.3 %collective-permute-start.5 = (f32[1,384]{1,0:T(1,128)S(1)}, f32[1,384]{1,0:T(1,128)S(1)}, u32[]{:S(2)}, u32[]{:S(2)}) collective-permute-start(f32[1,384]{1,0:T(1,128)S(1)} %get-tuple-element.39), channel_id=1, source_target_pairs={{0,2},{1,3},{2,0},{3,1},{4,6},{5,7},{6,4},{7,5},{8,10},{9,11},{10,... | collective-permute-start | bytes 4616 | tf_op jit(solution)/shard_map/ppermute | solution.py:587
  115.6 3.7 %all-to-all-start.3 = ((bf16[4,784,128]{2,1,0:T(8,128)(2,1)}), bf16[4,784,128]{2,1,0:T(8,128)(2,1)S(1)}, u32[]{:S(2)}, u32[]{:S(2)}) async-start(bf16[4,784,128]{2,1,0:T(8,128)(2,1)} %get-tuple-element.38), calls=%async_computation.3 | async-start | bytes 1605632 | tf_op jit(solution)/shard_map/all_to_all | solution.py:522
  119.3 0.0 collective-permute-done.7
  119.3 0.0 collective-permute-done.6
  119.3 0.0 collective-permute-done.5
  119.3 2.9 %collective-permute-start.10 = (f32[1,384]{1,0:T(1,128)S(1)}, f32[1,384]{1,0:T(1,128)S(1)}, u32[]{:S(2)}, u32[]{:S(2)}) collective-permute-start(f32[1,384]{1,0:T(1,128)S(1)} %add_add_fusion.1), channel_id=1, source_target_pairs={{0,12},{1,13},{2,14},{3,15},{4,0},{5,1},{6,2},{7,3},{8,4},{9,5},{1... | collective-permute-start | bytes 4616 | tf_op jit(solution)/shard_map/ppermute | solution.py:540
  122.2 0.0 collective-permute-start.9
  122.2 1.5 %collective-permute-start.8 = (f32[1,384]{1,0:T(1,128)S(1)}, f32[1,384]{1,0:T(1,128)S(1)}, u32[]{:S(2)}, u32[]{:S(2)}) collective-permute-start(f32[1,384]{1,0:T(1,128)S(1)} %add_add_fusion.1), channel_id=1, source_target_pairs={{0,8},{1,9},{2,10},{3,11},{4,12},{5,13},{6,14},{7,15},{8,0},{9,1},... | collective-permute-start | bytes 4616 | tf_op jit(solution)/shard_map/ppermute | solution.py:540
  123.7 0.0 collective-permute-done.10
  123.7 3.2 %collective-permute-done.9 = f32[1,384]{1,0:T(1,128)S(1)} collective-permute-done((f32[1,384]{1,0:T(1,128)S(1)}, f32[1,384]{1,0:T(1,128)S(1)}, u32[]{:S(2)}, u32[]{:S(2)}) %collective-permute-start.9) | collective-permute-done | bytes 1568 | tf_op jit(solution)/shard_map/ppermute | solution.py:540
  127.0 0.3 collective-permute-done.8
  127.3 0.6 slice.9
  128.5 0.6 fusion
  129.1 0.0 all-to-all-done.3.got_ref
  129.1 0.0 copy-done.5
  129.1 0.0 copy-done.3
  129.1 1.9 %final.1 = bf16[512,768]{1,0:T(8,128)(2,1)} custom-call(bf16[512,768]{1,0:T(8,128)(2,1)S(1)} %copy-done.5, bf16[4,784,128]{2,1,0:T(8,128)(2,1)S(1)} %all-to-all-done.3.got_ref, bf16[768,768]{1,0:T(8,128)(2,1)S(1)} %copy-done.3), custom_call_target="tpu_custom_call" | custom-call | flops 1000000000 | bytes 4000000 | tf_op jit(solution)/shard_map/final/pallas_call | solution.py:595
  (2 shorter events, 0.0 us)
Async XLA Ops:
  8.9 33.4 %collective-permute-start.1 = (bf16[264,768]{1,0:T(8,128)(2,1)S(1)}, bf16[264,768]{1,0:T(8,128)(2,1)S(1)}, u32[]{:S(2)}, u32[]{:S(2)}) collective-permute-start(bf16[264,768]{1,0:T(8,128)(2,1)S(1)} %get-tuple-element.23), channel_id=1, source_target_pairs={{1,0},{2,1},{3,2},{4,3},{5,4},{6,5},{7,6},{8,7},{9,8},{10,9},{11,1... | collective-permute-start | bytes 1216520 | tf_op jit(solution)/shard_map/ppermute | solution.py:465
  11.3 31.0 %collective-permute-start = (bf16[264,768]{1,0:T(8,128)(2,1)S(1)}, bf16[264,768]{1,0:T(8,128)(2,1)S(1)}, u32[]{:S(2)}, u32[]{:S(2)}) collective-permute-start(bf16[264,768]{1,0:T(8,128)(2,1)S(1)} %get-tuple-element.21), channel_id=1, source_target_pairs={{0,1},{1,2},{2,3},{3,4},{4,5},{5,6},{6,7},{7,8},{8,9},{9,10},{10,1... | collective-permute-start | bytes 1216520 | tf_op jit(solution)/shard_map/ppermute | solution.py:464
  14.8 9.8 %all-to-all-start = ((s32[8,1,320]{2,1,0:T(1,128)}), s32[8,1,320]{2,1,0:T(1,128)S(1)}, u32[]{:S(2)}, u32[]{:S(2)}) async-start(s32[8,1,320]{2,1,0:T(1,128)} %get-tuple-element.25), calls=%async_computation | async-start | bytes 24576 | tf_op jit(solution)/shard_map/all_to_all | solution.py:453
  19.3 0.9 copy-start.1
  31.4 10.9 %copy-start = (bf16[1,512,768]{2,1,0:T(8,128)(2,1)S(1)}, bf16[1,512,768]{2,1,0:T(8,128)(2,1)}, u32[]{:S(2)}) copy-start(bf16[1,512,768]{2,1,0:T(8,128)(2,1)} %param.10) | copy-start | bytes 2359300
  31.4 10.9 %copy-start.2 = (s32[1,512]{1,0:T(1,128)S(1)}, s32[1,512]{1,0:T(1,128)}, u32[]{:S(2)}) copy-start(s32[1,512]{1,0:T(1,128)} %tokens_ref.1) | copy-start | bytes 6148
  31.4 26.7 %all-to-all-start.1 = ((bf16[128,8,384]{2,1,0:T(8,128)(2,1)}), bf16[128,8,384]{2,1,0:T(8,128)(2,1)S(1)}, u32[]{:S(2)}, u32[]{:S(2)}) async-start(bf16[128,8,384]{2,1,0:T(8,128)(2,1)} %bitcast.5), calls=%async_computation.1 | async-start | bytes 1572864 | tf_op jit(solution)/shard_map/all_to_all | solution.py:489
  42.0 47.5 %all-gather.2.cloned.1.call-start = ((), (), s32[]{:S(2)}) async-start(), calls=%async_computation.4 | async-start | bytes 1638400 | tf_op jit(solution)/shard_map/all_gather | solution.py:548
  55.9 0.9 copy-start.4
  59.7 19.7 %all-to-all-start.2 = ((bf16[4,784,128]{2,1,0:T(8,128)(2,1)}), bf16[4,784,128]{2,1,0:T(8,128)(2,1)S(1)}, u32[]{:S(2)}, u32[]{:S(2)}) async-start(bf16[4,784,128]{2,1,0:T(8,128)(2,1)} %get-tuple-element.33), calls=%async_computation.2 | async-start | bytes 1605632 | tf_op jit(solution)/shard_map/all_to_all | solution.py:522
  64.5 8.9 %collective-permute-start.4 = (bf16[640,128]{1,0:T(8,128)(2,1)S(1)}, bf16[640,128]{1,0:T(8,128)(2,1)S(1)}, u32[]{:S(2)}, u32[]{:S(2)}) collective-permute-start(bf16[640,128]{1,0:T(8,128)(2,1)S(1)} %get-tuple-element.35.refs_0_), channel_id=1, source_target_pairs={{0,12},{1,13},{2,14},{3,15},{4,0},{5,1},{6,2},{7,3},{8,4},{9,5},{1... | collective-permute-start | bytes 491528 | tf_op jit(solution)/shard_map/ppermute | solution.py:540
  66.5 9.7 %collective-permute-start.3 = (bf16[640,128]{1,0:T(8,128)(2,1)S(1)}, bf16[640,128]{1,0:T(8,128)(2,1)S(1)}, u32[]{:S(2)}, u32[]{:S(2)}) collective-permute-start(bf16[640,128]{1,0:T(8,128)(2,1)S(1)} %get-tuple-element.35.refs_0_), channel_id=1, source_target_pairs={{0,8},{1,9},{2,10},{3,11},{4,12},{5,13},{6,14},{7,15},{8,0},{9,1},... | collective-permute-start | bytes 491528 | tf_op jit(solution)/shard_map/ppermute | solution.py:540
  67.4 11.9 %collective-permute-start.2 = (bf16[640,128]{1,0:T(8,128)(2,1)S(1)}, bf16[640,128]{1,0:T(8,128)(2,1)S(1)}, u32[]{:S(2)}, u32[]{:S(2)}) collective-permute-start(bf16[640,128]{1,0:T(8,128)(2,1)S(1)} %get-tuple-element.35.refs_0_), channel_id=1, source_target_pairs={{0,4},{1,5},{2,6},{3,7},{4,8},{5,9},{6,10},{7,11},{8,12},{9,13},{1... | collective-permute-start | bytes 491528 | tf_op jit(solution)/shard_map/ppermute | solution.py:540
  88.7 0.8 copy-start.6
  89.6 39.6 %copy-start.5 = (bf16[512,768]{1,0:T(8,128)(2,1)S(1)}, bf16[512,768]{1,0:T(8,128)(2,1)}, u32[]{:S(2)}) copy-start(bf16[512,768]{1,0:T(8,128)(2,1)} %copy-done.4) | copy-start | bytes 2359300
  110.2 18.9 %copy-start.3 = (bf16[768,768]{1,0:T(8,128)(2,1)S(1)}, bf16[768,768]{1,0:T(8,128)(2,1)}, u32[]{:S(2)}) copy-start(bf16[768,768]{1,0:T(8,128)(2,1)} %weight_ref.1) | copy-start | bytes 3538948
  110.2 9.1 %collective-permute-start.7 = (f32[1,384]{1,0:T(1,128)S(1)}, f32[1,384]{1,0:T(1,128)S(1)}, u32[]{:S(2)}, u32[]{:S(2)}) collective-permute-start(f32[1,384]{1,0:T(1,128)S(1)} %get-tuple-element.39), channel_id=1, source_target_pairs={{0,3},{1,0},{2,1},{3,2},{4,7},{5,4},{6,5},{7,6},{8,11},{9,8},{10,9... | collective-permute-start | bytes 4616 | tf_op jit(solution)/shard_map/ppermute | solution.py:587
  110.4 8.9 %collective-permute-start.6 = (f32[1,384]{1,0:T(1,128)S(1)}, f32[1,384]{1,0:T(1,128)S(1)}, u32[]{:S(2)}, u32[]{:S(2)}) collective-permute-start(f32[1,384]{1,0:T(1,128)S(1)} %get-tuple-element.39), channel_id=1, source_target_pairs={{0,1},{1,2},{2,3},{3,0},{4,5},{5,6},{6,7},{7,4},{8,9},{9,10},{10,1... | collective-permute-start | bytes 4616 | tf_op jit(solution)/shard_map/ppermute | solution.py:587
  112.3 7.0 %collective-permute-start.5 = (f32[1,384]{1,0:T(1,128)S(1)}, f32[1,384]{1,0:T(1,128)S(1)}, u32[]{:S(2)}, u32[]{:S(2)}) collective-permute-start(f32[1,384]{1,0:T(1,128)S(1)} %get-tuple-element.39), channel_id=1, source_target_pairs={{0,2},{1,3},{2,0},{3,1},{4,6},{5,7},{6,4},{7,5},{8,10},{9,11},{10,... | collective-permute-start | bytes 4616 | tf_op jit(solution)/shard_map/ppermute | solution.py:587
  115.6 13.5 %all-to-all-start.3 = ((bf16[4,784,128]{2,1,0:T(8,128)(2,1)}), bf16[4,784,128]{2,1,0:T(8,128)(2,1)S(1)}, u32[]{:S(2)}, u32[]{:S(2)}) async-start(bf16[4,784,128]{2,1,0:T(8,128)(2,1)} %get-tuple-element.38), calls=%async_computation.3 | async-start | bytes 1605632 | tf_op jit(solution)/shard_map/all_to_all | solution.py:522
  119.3 4.4 %collective-permute-start.10 = (f32[1,384]{1,0:T(1,128)S(1)}, f32[1,384]{1,0:T(1,128)S(1)}, u32[]{:S(2)}, u32[]{:S(2)}) collective-permute-start(f32[1,384]{1,0:T(1,128)S(1)} %add_add_fusion.1), channel_id=1, source_target_pairs={{0,12},{1,13},{2,14},{3,15},{4,0},{5,1},{6,2},{7,3},{8,4},{9,5},{1... | collective-permute-start | bytes 4616 | tf_op jit(solution)/shard_map/ppermute | solution.py:540
  122.2 4.8 %collective-permute-start.9 = (f32[1,384]{1,0:T(1,128)S(1)}, f32[1,384]{1,0:T(1,128)S(1)}, u32[]{:S(2)}, u32[]{:S(2)}) collective-permute-start(f32[1,384]{1,0:T(1,128)S(1)} %add_add_fusion.1), channel_id=1, source_target_pairs={{0,4},{1,5},{2,6},{3,7},{4,8},{5,9},{6,10},{7,11},{8,12},{9,13},{1... | collective-permute-start | bytes 4616 | tf_op jit(solution)/shard_map/ppermute | solution.py:540
  122.2 5.1 %collective-permute-start.8 = (f32[1,384]{1,0:T(1,128)S(1)}, f32[1,384]{1,0:T(1,128)S(1)}, u32[]{:S(2)}, u32[]{:S(2)}) collective-permute-start(f32[1,384]{1,0:T(1,128)S(1)} %add_add_fusion.1), channel_id=1, source_target_pairs={{0,8},{1,9},{2,10},{3,11},{4,12},{5,13},{6,14},{7,15},{8,0},{9,1},... | collective-permute-start | bytes 4616 | tf_op jit(solution)/shard_map/ppermute | solution.py:540
Sparse Core Ops, SparseCore 0:
  59.8 28.0 all-gather.1

commit v8 on v6

--- a/solution.py
+++ b/solution.py
@@ -516,16 +516,17 @@
         cost_estimate=cost(10**9, 0, 2 * 10**6),
     )(slots, got.reshape(devices * DESC, 3 * LANES))
 
-    def turns(block):
-        parts = []
-        for shift in range(1, GRID):
-            pairs = [(i, (i + GRID * shift) % seq_count) for i in range(seq_count)]
-            parts.append(lax.ppermute(block, "seq", pairs))
-        return parts
+    def turn(block, shift):
+        pairs = [(i, (i + GRID * shift) % seq_count) for i in range(seq_count)]
+        return lax.ppermute(block, "seq", pairs)
 
     block, rest_block = blocks
-    *arrived, rest_block = lax.optimization_barrier((*turns(block), rest_block))
-    first, rest = [block] + arrived, [rest_block] + turns(rest_block)
+    up, down = turn(block, 1), turn(block, 3)
+    rest_up, rest_down = turn(rest_block, 1), turn(rest_block, 3)
+    far = turn(down, 3)
+    up, down, far, rest_up = lax.optimization_barrier((up, down, far, rest_up))
+    rest_far = turn(rest_up, 1)
+    first, rest = [block, up, far, down], [rest_block, rest_up, rest_far, rest_down]
 
     def cross(heads, parts, extra, outs):
         return pl.pallas_call(
@@ -560,7 +561,7 @@
     across_x = [[(i, GRID * (i // GRID) + (i + shift) % GRID) for i in range(seq_count)] for shift in range(1, GRID)]
     one, two, three = [lax.ppermute(score, "seq", pairs) for pairs in across_x]
     score = (score + two) + (one + three)
-    one, two, three = turns(score)
+    one, two, three = [turn(score, shift) for shift in (1, 2, 3)]
     sums = (score + two) + (one + three)
     tokens = sums[:, count : count + 1] * (1.0 / GRID)
     cand_score = count * sums[:, :count] / (HEADS * tokens)

time: 126 us -> 122 us (0.968)
  waiting for transfers between devices: 21.6 us -> 18.6 us
  starting transfers between devices: 45.7 us -> 43.8 us
    ppermute x9, waiting for transfers between devices: 15.8 us -> 12.9 us  [turn(): return lax.ppermute(block, 'seq', pairs)]
    ppermute x9, starting transfers between devices: 12.6 us -> 11.1 us  [turn(): return lax.ppermute(block, 'seq', pairs)]
  transfers between devices with their start and end apart: 18 -> 18, of which waited for: 8 -> 5; matrix products, arithmetic and copies ran while one was open for 1% -> 1% of each run, Pallas kernels for 24% -> 26%
where the time goes in v8:
time: 122 us; the launch traced here: 121 us
  Pallas kernels  54.4 us (45%)
  starting transfers between devices  43.8 us (36%)
  waiting for transfers between devices  18.6 us (15%)
  local copies, waits for them, and re-layouts  2.39 us (2%)
  between operations  1.47 us (1%)
    pallas_call x2, Pallas kernels, cross(): pl.pallas_call(functools.partial(cross_kernel, heads, count), name='cross...  29 us
    pallas_call x1, Pallas kernels, local(): pl.pallas_call(window_kernel, name='window', out_shape=(jax.ShapeDtypeStr...  13.6 us
    ppermute x9, waiting for transfers between devices, turn(): return lax.ppermute(block, 'seq', pairs)  12.9 us
    ppermute x9, starting transfers between devices, turn(): return lax.ppermute(block, 'seq', pairs)  11.1 us
    all_to_all x2, starting transfers between devices, across(): lax.all_to_all(block, 'seq', split_axis=0, concat_axis=0, axis_index_grou...  9.75 us
    all_to_all x1, starting transfers between devices, local(): lax.all_to_all(send.reshape(devices, DESC, 3 * LANES), ('doc', 'seq'), sp...  8.49 us
    pallas_call x1, Pallas kernels, local(): pl.pallas_call(functools.partial(route_kernel, count, code_dev, devices),...  7.22 us
    all_to_all x1, starting transfers between devices, local(): lax.all_to_all(asked, 'doc', split_axis=0, concat_axis=0, tiled=True)  4.48 us
  transfers between devices with their start and end apart: 18, of which 5 were waited for; matrix products, arithmetic and copies ran while one was open for 1% of the time, Pallas kernels for 26%

profile of v8, /device:TPU:2, one launch (start us, length us, event | category | flops | bytes accessed | tf_op | source)
XLA Modules:
  0.0 121.3 jit_solution(6152826865793125832)
XLA Ops:
  0.6 1.8 %halo.1 = (bf16[264,768]{1,0:T(8,128)(2,1)S(1)}, bf16[264,768]{1,0:T(8,128)(2,1)S(1)}, s32[8,1,320]{2,1,0:T(1,128)}) custom-call(bf16[512,768]{1,0:T(8,128)(2,1)} %bitcast.10, s32[1,512]{1,0:T(1,128)} %tokens_ref.1, s32[1,320]{1,0:T(1,128)} %wanted_hbm.1), custom_call_target="tpu_custom_call" | custom-call | flops 100000 | bytes 1600000 | tf_op jit(solution)/shard_map/halo/pallas_call | solution.py:423
  2.4 3.4 %collective-permute-start = (bf16[264,768]{1,0:T(8,128)(2,1)S(1)}, bf16[264,768]{1,0:T(8,128)(2,1)S(1)}, u32[]{:S(2)}, u32[]{:S(2)}) collective-permute-start(bf16[264,768]{1,0:T(8,128)(2,1)S(1)} %get-tuple-element.22), channel_id=1, source_target_pairs={{0,1},{1,2},{2,3},{3,4},{4,5},{5,6},{6,7},{7,8},{8,9},{9,10},{10,1... | collective-permute-start | bytes 1216520 | tf_op jit(solution)/shard_map/ppermute | solution.py:445
  5.8 2.5 %collective-permute-start.1 = (bf16[264,768]{1,0:T(8,128)(2,1)S(1)}, bf16[264,768]{1,0:T(8,128)(2,1)S(1)}, u32[]{:S(2)}, u32[]{:S(2)}) collective-permute-start(bf16[264,768]{1,0:T(8,128)(2,1)S(1)} %get-tuple-element.24), channel_id=1, source_target_pairs={{1,0},{2,1},{3,2},{4,3},{5,4},{6,5},{7,6},{8,7},{9,8},{10,9},{11,1... | collective-permute-start | bytes 1216520 | tf_op jit(solution)/shard_map/ppermute | solution.py:446
  8.3 4.5 %all-to-all-start = ((s32[8,1,320]{2,1,0:T(1,128)}), s32[8,1,320]{2,1,0:T(1,128)S(1)}, u32[]{:S(2)}, u32[]{:S(2)}) async-start(s32[8,1,320]{2,1,0:T(1,128)} %get-tuple-element.26), calls=%async_computation | async-start | bytes 24576 | tf_op jit(solution)/shard_map/all_to_all | solution.py:434
  12.8 0.1 pad_add_fusion.where_ref
  12.8 0.0 copy-start.1
  12.8 0.9 copy-done.1
  13.7 0.1 planes.1.planes_ref
  13.9 4.2 %all-to-all-done.codes_ref = s32[8,1,320]{2,1,0:T(1,128)S(1)} async-done(((s32[8,1,320]{2,1,0:T(1,128)}), s32[8,1,320]{2,1,0:T(1,128)S(1)}, u32[]{:S(2)}, u32[]{:S(2)}) %all-to-all-start) | async-done | bytes 10272 | tf_op jit(solution)/shard_map/all_to_all | solution.py:434
  18.1 7.2 %route.1 = (bf16[32,4,8,384]{3,2,1,0:T(8,128)(2,1)}, s32[1,1024]{1,0:T(1,128)S(1)}, s32[1,384]{1,0:T(1,128)S(1)}) custom-call(s32[3]{0:T(128)S(1)} %pad_add_fusion.where_ref, s32[8,1,320]{2,1,0:T(1,128)S(1)} %all-to-all-done.codes_ref, bf16[256,384]{1,0:T(8,128)(2,1)S(1)} %planes.1.planes_ref, bf16[288,2,8,768]{3,2,1,0:T(8,128)(2,1)} %cache_ref.1), custom_call_target="tpu_custom_call" | custom-call | flops 1000000000 | bytes 2000000 | tf_op jit(solution)/shard_map/route/pallas_call | solution.py:448
  25.3 0.0 copy-start
  25.3 0.0 copy-start.2
  25.3 8.5 %all-to-all-start.2 = ((bf16[128,8,384]{2,1,0:T(8,128)(2,1)}), bf16[128,8,384]{2,1,0:T(8,128)(2,1)S(1)}, u32[]{:S(2)}, u32[]{:S(2)}) async-start(bf16[128,8,384]{2,1,0:T(8,128)(2,1)} %bitcast.5), calls=%async_computation.2 | async-start | bytes 1572864 | tf_op jit(solution)/shard_map/all_to_all | solution.py:470
  33.8 0.0 collective-permute-done.low_ref
  33.9 0.0 collective-permute-done.1.high_ref
  33.9 0.0 copy-done
  33.9 0.0 copy-done.2
  33.9 13.6 %window.1 = (bf16[512,768]{1,0:T(8,128)(2,1)S(1)}, bf16[4,784,128]{2,1,0:T(8,128)(2,1)}) custom-call(bf16[264,768]{1,0:T(8,128)(2,1)S(1)} %collective-permute-done.low_ref, bf16[512,768]{1,0:T(8,128)(2,1)S(1)} %bitcast.11, bf16[264,768]{1,0:T(8,128)(2,1)S(1)} %collective-permute-done.1.high_ref, s32[1,512]{1,0:T(1,128)S(1)} %copy-done.2, ...), custom_call_target="tpu_custom_call" | custom-call | flops 12000000000 | bytes 10000000 | tf_op jit(solution)/shard_map/window/pallas_call | solution.py:474
  47.5 0.0 copy-start.4
  47.5 0.9 copy-done.4
  48.4 1.5 %all-to-all-done.2 = bf16[128,8,384]{2,1,0:T(8,128)(2,1)S(1)} async-done(((bf16[128,8,384]{2,1,0:T(8,128)(2,1)}), bf16[128,8,384]{2,1,0:T(8,128)(2,1)S(1)}, u32[]{:S(2)}, u32[]{:S(2)}) %all-to-all-start.2) | async-done | bytes 786464 | tf_op jit(solution)/shard_map/all_to_all | solution.py:470
  49.9 4.8 %all-to-all-start.1 = ((bf16[4,784,128]{2,1,0:T(8,128)(2,1)}), bf16[4,784,128]{2,1,0:T(8,128)(2,1)S(1)}, u32[]{:S(2)}, u32[]{:S(2)}) async-start(bf16[4,784,128]{2,1,0:T(8,128)(2,1)} %get-tuple-element.29), calls=%async_computation.1 | async-start | bytes 1605632 | tf_op jit(solution)/shard_map/all_to_all | solution.py:503
  54.7 0.8 compact.1
  55.6 1.9 %collective-permute-start.3 = (bf16[640,128]{1,0:T(8,128)(2,1)S(1)}, bf16[640,128]{1,0:T(8,128)(2,1)S(1)}, u32[]{:S(2)}, u32[]{:S(2)}) collective-permute-start(bf16[640,128]{1,0:T(8,128)(2,1)S(1)} %get-tuple-element.33.refs_0_), channel_id=1, source_target_pairs={{0,12},{1,13},{2,14},{3,15},{4,0},{5,1},{6,2},{7,3},{8,4},{9,5},{1... | collective-permute-start | bytes 491528 | tf_op jit(solution)/shard_map/ppermute | solution.py:521
  57.5 0.2 collective-permute-start.5
  57.7 0.8 collective-permute-start.2
  58.5 2.8 %collective-permute-done.3.refs_3_ = bf16[640,128]{1,0:T(8,128)(2,1)S(1)} collective-permute-done((bf16[640,128]{1,0:T(8,128)(2,1)S(1)}, bf16[640,128]{1,0:T(8,128)(2,1)S(1)}, u32[]{:S(2)}, u32[]{:S(2)}) %collective-permute-start.3) | collective-permute-done | bytes 163872 | tf_op jit(solution)/shard_map/ppermute | solution.py:521
  61.3 3.0 %collective-permute-start.4 = (bf16[640,128]{1,0:T(8,128)(2,1)S(1)}, bf16[640,128]{1,0:T(8,128)(2,1)S(1)}, u32[]{:S(2)}, u32[]{:S(2)}) collective-permute-start(bf16[640,128]{1,0:T(8,128)(2,1)S(1)} %collective-permute-done.3.refs_3_), channel_id=1, source_target_pairs={{0,12},{1,13},{2,14},{3,15},{4,0},{5,1},{6,2},{7,3},{8,4},{9,5},{1... | collective-permute-start | bytes 491528 | tf_op jit(solution)/shard_map/ppermute | solution.py:521
  64.4 0.0 collective-permute-start.7
  64.4 6.7 %collective-permute-done.2.refs_1_ = bf16[640,128]{1,0:T(8,128)(2,1)S(1)} collective-permute-done((bf16[640,128]{1,0:T(8,128)(2,1)S(1)}, bf16[640,128]{1,0:T(8,128)(2,1)S(1)}, u32[]{:S(2)}, u32[]{:S(2)}) %collective-permute-start.2) | collective-permute-done | bytes 163872 | tf_op jit(solution)/shard_map/ppermute | solution.py:521
  71.1 0.0 collective-permute-done.4.refs_2_
  71.1 0.0 collective-permute-done.5.refs_1_
  71.1 0.0 collective-permute-start.6
  71.1 0.0 all-to-all-done.1.query_ref
  71.1 9.4 %cross.2 = (bf16[4,512,128]{2,1,0:T(8,128)(2,1)S(1)}, f32[8,2560]{1,0:T(8,128)S(1)}) custom-call(s32[3]{0:T(128)S(1)} %pad_add_fusion.where_ref, s32[1,384]{1,0:T(1,128)S(1)} %get-tuple-element.28.pos_ref, bf16[4,784,128]{2,1,0:T(8,128)(2,1)S(1)} %all-to-all-done.1.query_ref, bf16[640,128]{1,0:T(8,128)(2,1)S(1)} %get-tuple-element.33.refs_0_, ...), custom_call_target="tpu_custom_call" | custom-call | flops 10000000000 | bytes 4000000 | tf_op jit(solution)/shard_map/cross/pallas_call | solution.py:532
  80.5 0.0 collective-permute-done.7.refs_3_
  80.5 0.0 collective-permute-done.6.refs_2_
  80.5 0.0 copy-start.5
  80.5 19.6 %cross.3 = (bf16[4,784,128]{2,1,0:T(8,128)(2,1)}, f32[1,384]{1,0:T(1,128)S(1)}) custom-call(s32[3]{0:T(128)S(1)} %pad_add_fusion.where_ref, s32[1,384]{1,0:T(1,128)S(1)} %get-tuple-element.28.pos_ref, bf16[4,784,128]{2,1,0:T(8,128)(2,1)S(1)} %all-to-all-done.1.query_ref, bf16[640,256]{1,0:T(8,128)(2,1)S(1)} %get-tuple-element.32.refs_0_, ...), custom_call_target="tpu_custom_call" | custom-call | flops 20000000000 | bytes 4000000 | tf_op jit(solution)/shard_map/cross/pallas_call | solution.py:532
  100.1 0.0 copy-start.3
  100.1 1.5 %collective-permute-start.9 = (f32[1,384]{1,0:T(1,128)S(1)}, f32[1,384]{1,0:T(1,128)S(1)}, u32[]{:S(2)}, u32[]{:S(2)}) collective-permute-start(f32[1,384]{1,0:T(1,128)S(1)} %get-tuple-element.41), channel_id=1, source_target_pairs={{0,1},{1,2},{2,3},{3,0},{4,5},{5,6},{6,7},{7,4},{8,9},{9,10},{10,1... | collective-permute-start | bytes 4616 | tf_op jit(solution)/shard_map/ppermute | solution.py:562
  101.6 0.6 collective-permute-start.10
  102.2 2.1 %collective-permute-start.8 = (f32[1,384]{1,0:T(1,128)S(1)}, f32[1,384]{1,0:T(1,128)S(1)}, u32[]{:S(2)}, u32[]{:S(2)}) collective-permute-start(f32[1,384]{1,0:T(1,128)S(1)} %get-tuple-element.41), channel_id=1, source_target_pairs={{0,2},{1,3},{2,0},{3,1},{4,6},{5,7},{6,4},{7,5},{8,10},{9,11},{10,... | collective-permute-start | bytes 4616 | tf_op jit(solution)/shard_map/ppermute | solution.py:562
  104.2 4.9 %all-to-all-start.3 = ((bf16[4,784,128]{2,1,0:T(8,128)(2,1)}), bf16[4,784,128]{2,1,0:T(8,128)(2,1)S(1)}, u32[]{:S(2)}, u32[]{:S(2)}) async-start(bf16[4,784,128]{2,1,0:T(8,128)(2,1)} %get-tuple-element.40), calls=%async_computation.3 | async-start | bytes 1605632 | tf_op jit(solution)/shard_map/all_to_all | solution.py:503
  109.1 0.0 collective-permute-done.9
  109.2 0.0 collective-permute-done.10
  109.2 0.0 collective-permute-done.8
  109.2 0.1 collective-permute-start.12
  109.3 3.3 %collective-permute-start.13 = (f32[1,384]{1,0:T(1,128)S(1)}, f32[1,384]{1,0:T(1,128)S(1)}, u32[]{:S(2)}, u32[]{:S(2)}) collective-permute-start(f32[1,384]{1,0:T(1,128)S(1)} %add_add_fusion.1), channel_id=1, source_target_pairs={{0,12},{1,13},{2,14},{3,15},{4,0},{5,1},{6,2},{7,3},{8,4},{9,5},{1... | collective-permute-start | bytes 4616 | tf_op jit(solution)/shard_map/ppermute | solution.py:521
  112.5 1.8 %collective-permute-start.11 = (f32[1,384]{1,0:T(1,128)S(1)}, f32[1,384]{1,0:T(1,128)S(1)}, u32[]{:S(2)}, u32[]{:S(2)}) collective-permute-start(f32[1,384]{1,0:T(1,128)S(1)} %add_add_fusion.1), channel_id=1, source_target_pairs={{0,8},{1,9},{2,10},{3,11},{4,12},{5,13},{6,14},{7,15},{8,0},{9,1},... | collective-permute-start | bytes 4616 | tf_op jit(solution)/shard_map/ppermute | solution.py:521
  114.3 0.0 collective-permute-done.12
  114.3 0.0 collective-permute-done.13
  114.3 3.3 %collective-permute-done.11 = f32[1,384]{1,0:T(1,128)S(1)} collective-permute-done((f32[1,384]{1,0:T(1,128)S(1)}, f32[1,384]{1,0:T(1,128)S(1)}, u32[]{:S(2)}, u32[]{:S(2)}) %collective-permute-start.11) | collective-permute-done | bytes 1568 | tf_op jit(solution)/shard_map/ppermute | solution.py:521
  117.6 0.6 slice.9
  118.9 0.6 fusion
  119.4 0.0 all-to-all-done.3.got_ref
  119.4 0.0 copy-done.5
  119.4 0.0 copy-done.3
  119.5 1.9 %final.1 = bf16[512,768]{1,0:T(8,128)(2,1)} custom-call(bf16[512,768]{1,0:T(8,128)(2,1)S(1)} %copy-done.5, bf16[4,784,128]{2,1,0:T(8,128)(2,1)S(1)} %all-to-all-done.3.got_ref, bf16[768,768]{1,0:T(8,128)(2,1)S(1)} %copy-done.3), custom_call_target="tpu_custom_call" | custom-call | flops 1000000000 | bytes 4000000 | tf_op jit(solution)/shard_map/final/pallas_call | solution.py:570
  (2 shorter events, 0.0 us)
Async XLA Ops:
  2.4 31.5 %collective-permute-start = (bf16[264,768]{1,0:T(8,128)(2,1)S(1)}, bf16[264,768]{1,0:T(8,128)(2,1)S(1)}, u32[]{:S(2)}, u32[]{:S(2)}) collective-permute-start(bf16[264,768]{1,0:T(8,128)(2,1)S(1)} %get-tuple-element.22), channel_id=1, source_target_pairs={{0,1},{1,2},{2,3},{3,4},{4,5},{5,6},{6,7},{7,8},{8,9},{9,10},{10,1... | collective-permute-start | bytes 1216520 | tf_op jit(solution)/shard_map/ppermute | solution.py:445
  5.8 28.1 %collective-permute-start.1 = (bf16[264,768]{1,0:T(8,128)(2,1)S(1)}, bf16[264,768]{1,0:T(8,128)(2,1)S(1)}, u32[]{:S(2)}, u32[]{:S(2)}) collective-permute-start(bf16[264,768]{1,0:T(8,128)(2,1)S(1)} %get-tuple-element.24), channel_id=1, source_target_pairs={{1,0},{2,1},{3,2},{4,3},{5,4},{6,5},{7,6},{8,7},{9,8},{10,9},{11,1... | collective-permute-start | bytes 1216520 | tf_op jit(solution)/shard_map/ppermute | solution.py:446
  8.3 9.8 %all-to-all-start = ((s32[8,1,320]{2,1,0:T(1,128)}), s32[8,1,320]{2,1,0:T(1,128)S(1)}, u32[]{:S(2)}, u32[]{:S(2)}) async-start(s32[8,1,320]{2,1,0:T(1,128)} %get-tuple-element.26), calls=%async_computation | async-start | bytes 24576 | tf_op jit(solution)/shard_map/all_to_all | solution.py:434
  12.8 0.9 copy-start.1
  25.3 8.5 %copy-start = (bf16[1,512,768]{2,1,0:T(8,128)(2,1)S(1)}, bf16[1,512,768]{2,1,0:T(8,128)(2,1)}, u32[]{:S(2)}) copy-start(bf16[1,512,768]{2,1,0:T(8,128)(2,1)} %param.10) | copy-start | bytes 2359300
  25.3 8.5 %copy-start.2 = (s32[1,512]{1,0:T(1,128)S(1)}, s32[1,512]{1,0:T(1,128)}, u32[]{:S(2)}) copy-start(s32[1,512]{1,0:T(1,128)} %tokens_ref.1) | copy-start | bytes 6148
  25.3 24.5 %all-to-all-start.2 = ((bf16[128,8,384]{2,1,0:T(8,128)(2,1)}), bf16[128,8,384]{2,1,0:T(8,128)(2,1)S(1)}, u32[]{:S(2)}, u32[]{:S(2)}) async-start(bf16[128,8,384]{2,1,0:T(8,128)(2,1)} %bitcast.5), calls=%async_computation.2 | async-start | bytes 1572864 | tf_op jit(solution)/shard_map/all_to_all | solution.py:470
  47.5 0.9 copy-start.4
  49.9 21.2 %all-to-all-start.1 = ((bf16[4,784,128]{2,1,0:T(8,128)(2,1)}), bf16[4,784,128]{2,1,0:T(8,128)(2,1)S(1)}, u32[]{:S(2)}, u32[]{:S(2)}) async-start(bf16[4,784,128]{2,1,0:T(8,128)(2,1)} %get-tuple-element.29), calls=%async_computation.1 | async-start | bytes 1605632 | tf_op jit(solution)/shard_map/all_to_all | solution.py:503
  55.6 5.8 %collective-permute-start.3 = (bf16[640,128]{1,0:T(8,128)(2,1)S(1)}, bf16[640,128]{1,0:T(8,128)(2,1)S(1)}, u32[]{:S(2)}, u32[]{:S(2)}) collective-permute-start(bf16[640,128]{1,0:T(8,128)(2,1)S(1)} %get-tuple-element.33.refs_0_), channel_id=1, source_target_pairs={{0,12},{1,13},{2,14},{3,15},{4,0},{5,1},{6,2},{7,3},{8,4},{9,5},{1... | collective-permute-start | bytes 491528 | tf_op jit(solution)/shard_map/ppermute | solution.py:521
  57.5 13.7 %collective-permute-start.5 = (bf16[640,256]{1,0:T(8,128)(2,1)S(1)}, bf16[640,256]{1,0:T(8,128)(2,1)S(1)}, u32[]{:S(2)}, u32[]{:S(2)}) collective-permute-start(bf16[640,256]{1,0:T(8,128)(2,1)S(1)} %get-tuple-element.32.refs_0_), channel_id=1, source_target_pairs={{0,4},{1,5},{2,6},{3,7},{4,8},{5,9},{6,10},{7,11},{8,12},{9,13},{1... | collective-permute-start | bytes 983048 | tf_op jit(solution)/shard_map/ppermute | solution.py:521
  57.7 13.4 %collective-permute-start.2 = (bf16[640,128]{1,0:T(8,128)(2,1)S(1)}, bf16[640,128]{1,0:T(8,128)(2,1)S(1)}, u32[]{:S(2)}, u32[]{:S(2)}) collective-permute-start(bf16[640,128]{1,0:T(8,128)(2,1)S(1)} %get-tuple-element.33.refs_0_), channel_id=1, source_target_pairs={{0,4},{1,5},{2,6},{3,7},{4,8},{5,9},{6,10},{7,11},{8,12},{9,13},{1... | collective-permute-start | bytes 491528 | tf_op jit(solution)/shard_map/ppermute | solution.py:521
  61.3 9.8 %collective-permute-start.4 = (bf16[640,128]{1,0:T(8,128)(2,1)S(1)}, bf16[640,128]{1,0:T(8,128)(2,1)S(1)}, u32[]{:S(2)}, u32[]{:S(2)}) collective-permute-start(bf16[640,128]{1,0:T(8,128)(2,1)S(1)} %collective-permute-done.3.refs_3_), channel_id=1, source_target_pairs={{0,12},{1,13},{2,14},{3,15},{4,0},{5,1},{6,2},{7,3},{8,4},{9,5},{1... | collective-permute-start | bytes 491528 | tf_op jit(solution)/shard_map/ppermute | solution.py:521
  64.4 16.1 %collective-permute-start.7 = (bf16[640,256]{1,0:T(8,128)(2,1)S(1)}, bf16[640,256]{1,0:T(8,128)(2,1)S(1)}, u32[]{:S(2)}, u32[]{:S(2)}) collective-permute-start(bf16[640,256]{1,0:T(8,128)(2,1)S(1)} %get-tuple-element.32.refs_0_), channel_id=1, source_target_pairs={{0,12},{1,13},{2,14},{3,15},{4,0},{5,1},{6,2},{7,3},{8,4},{9,5},{1... | collective-permute-start | bytes 983048 | tf_op jit(solution)/shard_map/ppermute | solution.py:521
  71.1 9.4 %collective-permute-start.6 = (bf16[640,256]{1,0:T(8,128)(2,1)S(1)}, bf16[640,256]{1,0:T(8,128)(2,1)S(1)}, u32[]{:S(2)}, u32[]{:S(2)}) collective-permute-start(bf16[640,256]{1,0:T(8,128)(2,1)S(1)} %collective-permute-done.5.refs_1_), channel_id=1, source_target_pairs={{0,4},{1,5},{2,6},{3,7},{4,8},{5,9},{6,10},{7,11},{8,12},{9,13},{1... | collective-permute-start | bytes 983048 | tf_op jit(solution)/shard_map/ppermute | solution.py:521
  80.5 38.9 %copy-start.5 = (bf16[512,768]{1,0:T(8,128)(2,1)S(1)}, bf16[512,768]{1,0:T(8,128)(2,1)}, u32[]{:S(2)}) copy-start(bf16[512,768]{1,0:T(8,128)(2,1)} %copy-done.4) | copy-start | bytes 2359300
  100.1 19.3 %copy-start.3 = (bf16[768,768]{1,0:T(8,128)(2,1)S(1)}, bf16[768,768]{1,0:T(8,128)(2,1)}, u32[]{:S(2)}) copy-start(bf16[768,768]{1,0:T(8,128)(2,1)} %weight_ref.1) | copy-start | bytes 3538948
  100.1 9.0 %collective-permute-start.9 = (f32[1,384]{1,0:T(1,128)S(1)}, f32[1,384]{1,0:T(1,128)S(1)}, u32[]{:S(2)}, u32[]{:S(2)}) collective-permute-start(f32[1,384]{1,0:T(1,128)S(1)} %get-tuple-element.41), channel_id=1, source_target_pairs={{0,1},{1,2},{2,3},{3,0},{4,5},{5,6},{6,7},{7,4},{8,9},{9,10},{10,1... | collective-permute-start | bytes 4616 | tf_op jit(solution)/shard_map/ppermute | solution.py:562
  101.6 7.6 %collective-permute-start.10 = (f32[1,384]{1,0:T(1,128)S(1)}, f32[1,384]{1,0:T(1,128)S(1)}, u32[]{:S(2)}, u32[]{:S(2)}) collective-permute-start(f32[1,384]{1,0:T(1,128)S(1)} %get-tuple-element.41), channel_id=1, source_target_pairs={{0,3},{1,0},{2,1},{3,2},{4,7},{5,4},{6,5},{7,6},{8,11},{9,8},{10,9... | collective-permute-start | bytes 4616 | tf_op jit(solution)/shard_map/ppermute | solution.py:562
  102.2 7.0 %collective-permute-start.8 = (f32[1,384]{1,0:T(1,128)S(1)}, f32[1,384]{1,0:T(1,128)S(1)}, u32[]{:S(2)}, u32[]{:S(2)}) collective-permute-start(f32[1,384]{1,0:T(1,128)S(1)} %get-tuple-element.41), channel_id=1, source_target_pairs={{0,2},{1,3},{2,0},{3,1},{4,6},{5,7},{6,4},{7,5},{8,10},{9,11},{10,... | collective-permute-start | bytes 4616 | tf_op jit(solution)/shard_map/ppermute | solution.py:562
  104.2 15.2 %all-to-all-start.3 = ((bf16[4,784,128]{2,1,0:T(8,128)(2,1)}), bf16[4,784,128]{2,1,0:T(8,128)(2,1)S(1)}, u32[]{:S(2)}, u32[]{:S(2)}) async-start(bf16[4,784,128]{2,1,0:T(8,128)(2,1)} %get-tuple-element.40), calls=%async_computation.3 | async-start | bytes 1605632 | tf_op jit(solution)/shard_map/all_to_all | solution.py:503
  109.2 5.1 %collective-permute-start.12 = (f32[1,384]{1,0:T(1,128)S(1)}, f32[1,384]{1,0:T(1,128)S(1)}, u32[]{:S(2)}, u32[]{:S(2)}) collective-permute-start(f32[1,384]{1,0:T(1,128)S(1)} %add_add_fusion.1), channel_id=1, source_target_pairs={{0,4},{1,5},{2,6},{3,7},{4,8},{5,9},{6,10},{7,11},{8,12},{9,13},{1... | collective-permute-start | bytes 4616 | tf_op jit(solution)/shard_map/ppermute | solution.py:521
  109.3 5.1 %collective-permute-start.13 = (f32[1,384]{1,0:T(1,128)S(1)}, f32[1,384]{1,0:T(1,128)S(1)}, u32[]{:S(2)}, u32[]{:S(2)}) collective-permute-start(f32[1,384]{1,0:T(1,128)S(1)} %add_add_fusion.1), channel_id=1, source_target_pairs={{0,12},{1,13},{2,14},{3,15},{4,0},{5,1},{6,2},{7,3},{8,4},{9,5},{1... | collective-permute-start | bytes 4616 | tf_op jit(solution)/shard_map/ppermute | solution.py:521
  112.5 5.1 %collective-permute-start.11 = (f32[1,384]{1,0:T(1,128)S(1)}, f32[1,384]{1,0:T(1,128)S(1)}, u32[]{:S(2)}, u32[]{:S(2)}) collective-permute-start(f32[1,384]{1,0:T(1,128)S(1)} %add_add_fusion.1), channel_id=1, source_target_pairs={{0,8},{1,9},{2,10},{3,11},{4,12},{5,13},{6,14},{7,15},{8,0},{9,1},... | collective-permute-start | bytes 4616 | tf_op jit(solution)/shard_map/ppermute | solution.py:521

commit v9 on v8

--- a/solution.py
+++ b/solution.py
@@ -210,7 +210,7 @@
 
 
 def window_kernel(
-    low_ref, hidden_ref, high_ref, tokens_ref, wkv_hbm, wq_hbm, wo_hbm, xq_hbm, middle_ref, query_ref, wkv_ref, wq_ref, wo_ref, xq_ref, normed, keys, values, queries, context, bias, sems
+    low_ref, hidden_ref, high_ref, tokens_ref, wkv_hbm, wq_hbm, wo_hbm, xq_hbm, middle_hbm, query_ref, middle_ref, wkv_ref, wq_ref, wo_ref, xq_ref, normed, keys, values, queries, context, bias, sems
 ):
     tok, width = hidden_ref.shape
     win = HALF_WIN
@@ -263,11 +263,14 @@
     copies[2].wait()
     copies[3].wait()
     thirds_of = [[] for _ in range(GRID)]
+    kept = []
     for b in range(tok // win):
         rows = slice(b * win, (b + 1) * win)
         mixed = hidden_ref[rows, :].astype(F32) + dot(context[rows, :], wo_ref[...])
         mixed = mixed.astype(BF)
         middle_ref[rows, :] = mixed
+        kept.append(pltpu.make_async_copy(middle_ref.at[rows, :], middle_hbm.at[rows, :], sems.at[4 + b]))
+        kept[-1].start()
         cross = dot(layer_norm(mixed.astype(F32)).astype(BF), xq_ref[...]) * SCALE
         tiles = [cross[:, p * LANES : (p + 1) * LANES] for p in range(pairs)]
         turned = [pltpu.roll(t, HALF, 1) for t in tiles]
@@ -286,6 +289,8 @@
     for g in range(GRID):
         query_ref[g, tok : tok + win, :] = jnp.where(low, thirds_of[g][0], thirds_of[g][1]).astype(BF)
         query_ref[g, tok + win :, :] = marks.astype(BF)
+    for copy in kept:
+        copy.wait()
 
 
 def cross_kernel(heads, count, where_ref, pos_ref, query_ref, *refs):
@@ -475,12 +480,13 @@
         window_kernel,
         name="window",
         out_shape=(
-            jax.ShapeDtypeStruct((tok, width), BF),
+            pltpu.HBM((tok, width), BF),
             jax.ShapeDtypeStruct((GRID, message, LANES), BF),
         ),
         in_specs=[vmem()] * 4 + [hbm()] * 4,
-        out_specs=(vmem(), vmem()),
+        out_specs=(hbm(), vmem()),
         scratch_shapes=[
+            pltpu.VMEM((tok, width), BF),
             pltpu.VMEM((width, 2 * width), BF),
             pltpu.VMEM((width, width), BF),
             pltpu.VMEM((width, width), BF),
@@ -491,7 +497,7 @@
             pltpu.VMEM((tok, width), BF),
             pltpu.VMEM((tok, width), BF),
             pltpu.VMEM((tok // HALF_WIN, HALF_WIN, 3 * HALF_WIN), F32),
-            pltpu.SemaphoreType.DMA((4,)),
+            pltpu.SemaphoreType.DMA((4 + tok // HALF_WIN,)),
         ],
         compiler_params=params(26),
         cost_estimate=cost(12 * 10**9, 5 * 10**6, 10**7),

time: 122 us -> 121 us (level)
  no operation moved by 1% of the time
where the time goes in v9:
time: 121 us
  Pallas kernels  54.2 us (45%)
  starting transfers between devices  43.2 us (36%)
  waiting for transfers between devices  19.5 us (16%)
  local copies, waits for them, and re-layouts  1.52 us (1%)
  between operations  1.46 us (1%)
    pallas_call x2, Pallas kernels, cross(): pl.pallas_call(functools.partial(cross_kernel, heads, count), name='cross...  29 us
    pallas_call x1, Pallas kernels, local(): pl.pallas_call(window_kernel, name='window', out_shape=(pltpu.HBM((tok, w...  13.6 us
    ppermute x9, waiting for transfers between devices, turn(): return lax.ppermute(block, 'seq', pairs)  12.9 us
    ppermute x9, starting transfers between devices, turn(): return lax.ppermute(block, 'seq', pairs)  10.3 us
    all_to_all x2, starting transfers between devices, across(): lax.all_to_all(block, 'seq', split_axis=0, concat_axis=0, axis_index_grou...  9.75 us
    all_to_all x1, starting transfers between devices, local(): lax.all_to_all(send.reshape(devices, DESC, 3 * LANES), ('doc', 'seq'), sp...  8.72 us
    pallas_call x1, Pallas kernels, local(): pl.pallas_call(functools.partial(route_kernel, count, code_dev, devices),...  6.99 us
    all_to_all x1, starting transfers between devices, local(): lax.all_to_all(asked, 'doc', split_axis=0, concat_axis=0, tiled=True)  4.48 us
  transfers between devices with their start and end apart: 18, of which 5 were waited for; matrix products, arithmetic and copies ran while one was open for 1% of the time, Pallas kernels for 26%

profile of v9, /device:TPU:2, one launch (start us, length us, event | category | flops | bytes accessed | tf_op | source)
XLA Modules:
  0.0 120.5 jit_solution(9060247731194271841)
XLA Ops:
  0.6 1.8 %halo.1 = (bf16[264,768]{1,0:T(8,128)(2,1)S(1)}, bf16[264,768]{1,0:T(8,128)(2,1)S(1)}, s32[8,1,320]{2,1,0:T(1,128)}) custom-call(bf16[512,768]{1,0:T(8,128)(2,1)} %bitcast.10, s32[1,512]{1,0:T(1,128)} %tokens_ref.1, s32[1,320]{1,0:T(1,128)} %wanted_hbm.1), custom_call_target="tpu_custom_call" | custom-call | flops 100000 | bytes 1600000 | tf_op jit(solution)/shard_map/halo/pallas_call | solution.py:428
  2.4 3.4 %collective-permute-start = (bf16[264,768]{1,0:T(8,128)(2,1)S(1)}, bf16[264,768]{1,0:T(8,128)(2,1)S(1)}, u32[]{:S(2)}, u32[]{:S(2)}) collective-permute-start(bf16[264,768]{1,0:T(8,128)(2,1)S(1)} %get-tuple-element.22), channel_id=1, source_target_pairs={{0,1},{1,2},{2,3},{3,4},{4,5},{5,6},{6,7},{7,8},{8,9},{9,10},{10,1... | collective-permute-start | bytes 1216520 | tf_op jit(solution)/shard_map/ppermute | solution.py:450
  5.8 2.5 %collective-permute-start.1 = (bf16[264,768]{1,0:T(8,128)(2,1)S(1)}, bf16[264,768]{1,0:T(8,128)(2,1)S(1)}, u32[]{:S(2)}, u32[]{:S(2)}) collective-permute-start(bf16[264,768]{1,0:T(8,128)(2,1)S(1)} %get-tuple-element.24), channel_id=1, source_target_pairs={{1,0},{2,1},{3,2},{4,3},{5,4},{6,5},{7,6},{8,7},{9,8},{10,9},{11,1... | collective-permute-start | bytes 1216520 | tf_op jit(solution)/shard_map/ppermute | solution.py:451
  8.3 4.5 %all-to-all-start = ((s32[8,1,320]{2,1,0:T(1,128)}), s32[8,1,320]{2,1,0:T(1,128)S(1)}, u32[]{:S(2)}, u32[]{:S(2)}) async-start(s32[8,1,320]{2,1,0:T(1,128)} %get-tuple-element.26), calls=%async_computation | async-start | bytes 24576 | tf_op jit(solution)/shard_map/all_to_all | solution.py:439
  12.8 0.1 pad_add_fusion.where_ref
  12.8 0.0 copy-start.1
  12.8 0.9 copy-done.1
  13.7 0.1 planes.1.planes_ref
  13.9 4.2 %all-to-all-done.codes_ref = s32[8,1,320]{2,1,0:T(1,128)S(1)} async-done(((s32[8,1,320]{2,1,0:T(1,128)}), s32[8,1,320]{2,1,0:T(1,128)S(1)}, u32[]{:S(2)}, u32[]{:S(2)}) %all-to-all-start) | async-done | bytes 10272 | tf_op jit(solution)/shard_map/all_to_all | solution.py:439
  18.1 7.0 %route.1 = (bf16[32,4,8,384]{3,2,1,0:T(8,128)(2,1)}, s32[1,1024]{1,0:T(1,128)S(1)}, s32[1,384]{1,0:T(1,128)S(1)}) custom-call(s32[3]{0:T(128)S(1)} %pad_add_fusion.where_ref, s32[8,1,320]{2,1,0:T(1,128)S(1)} %all-to-all-done.codes_ref, bf16[256,384]{1,0:T(8,128)(2,1)S(1)} %planes.1.planes_ref, bf16[288,2,8,768]{3,2,1,0:T(8,128)(2,1)} %cache_ref.1), custom_call_target="tpu_custom_call" | custom-call | flops 1000000000 | bytes 2000000 | tf_op jit(solution)/shard_map/route/pallas_call | solution.py:453
  25.1 0.0 copy-start
  25.1 0.0 copy-start.2
  25.1 8.7 %all-to-all-start.2 = ((bf16[128,8,384]{2,1,0:T(8,128)(2,1)}), bf16[128,8,384]{2,1,0:T(8,128)(2,1)S(1)}, u32[]{:S(2)}, u32[]{:S(2)}) async-start(bf16[128,8,384]{2,1,0:T(8,128)(2,1)} %bitcast.5), calls=%async_computation.2 | async-start | bytes 1572864 | tf_op jit(solution)/shard_map/all_to_all | solution.py:475
  33.8 0.0 collective-permute-done.low_ref
  33.9 0.0 collective-permute-done.1.high_ref
  33.9 0.0 copy-done
  33.9 0.0 copy-done.2
  33.9 13.6 %window.1 = (bf16[512,768]{1,0:T(8,128)(2,1)}, bf16[4,784,128]{2,1,0:T(8,128)(2,1)}) custom-call(bf16[264,768]{1,0:T(8,128)(2,1)S(1)} %collective-permute-done.low_ref, bf16[512,768]{1,0:T(8,128)(2,1)S(1)} %bitcast.11, bf16[264,768]{1,0:T(8,128)(2,1)S(1)} %collective-permute-done.1.high_ref, s32[1,512]{1,0:T(1,128)S(1)} %copy-done.2, ...), custom_call_target="tpu_custom_call" | custom-call | flops 12000000000 | bytes 10000000 | tf_op jit(solution)/shard_map/window/pallas_call | solution.py:479
  47.5 2.4 %all-to-all-done.2 = bf16[128,8,384]{2,1,0:T(8,128)(2,1)S(1)} async-done(((bf16[128,8,384]{2,1,0:T(8,128)(2,1)}), bf16[128,8,384]{2,1,0:T(8,128)(2,1)S(1)}, u32[]{:S(2)}, u32[]{:S(2)}) %all-to-all-start.2) | async-done | bytes 786464 | tf_op jit(solution)/shard_map/all_to_all | solution.py:475
  49.9 4.8 %all-to-all-start.1 = ((bf16[4,784,128]{2,1,0:T(8,128)(2,1)}), bf16[4,784,128]{2,1,0:T(8,128)(2,1)S(1)}, u32[]{:S(2)}, u32[]{:S(2)}) async-start(bf16[4,784,128]{2,1,0:T(8,128)(2,1)} %get-tuple-element.29), calls=%async_computation.1 | async-start | bytes 1605632 | tf_op jit(solution)/shard_map/all_to_all | solution.py:509
  54.7 0.8 compact.1
  55.6 1.1 collective-permute-start.3
  56.6 1.0 collective-permute-start.5
  57.7 0.8 collective-permute-start.2
  58.5 2.8 %collective-permute-done.3.refs_3_ = bf16[640,128]{1,0:T(8,128)(2,1)S(1)} collective-permute-done((bf16[640,128]{1,0:T(8,128)(2,1)S(1)}, bf16[640,128]{1,0:T(8,128)(2,1)S(1)}, u32[]{:S(2)}, u32[]{:S(2)}) %collective-permute-start.3) | collective-permute-done | bytes 163872 | tf_op jit(solution)/shard_map/ppermute | solution.py:527
  61.3 2.2 %collective-permute-start.4 = (bf16[640,128]{1,0:T(8,128)(2,1)S(1)}, bf16[640,128]{1,0:T(8,128)(2,1)S(1)}, u32[]{:S(2)}, u32[]{:S(2)}) collective-permute-start(bf16[640,128]{1,0:T(8,128)(2,1)S(1)} %collective-permute-done.3.refs_3_), channel_id=1, source_target_pairs={{0,12},{1,13},{2,14},{3,15},{4,0},{5,1},{6,2},{7,3},{8,4},{9,5},{1... | collective-permute-start | bytes 491528 | tf_op jit(solution)/shard_map/ppermute | solution.py:527
  63.5 0.0 collective-permute-start.7
  63.6 6.7 %collective-permute-done.2.refs_1_ = bf16[640,128]{1,0:T(8,128)(2,1)S(1)} collective-permute-done((bf16[640,128]{1,0:T(8,128)(2,1)S(1)}, bf16[640,128]{1,0:T(8,128)(2,1)S(1)}, u32[]{:S(2)}, u32[]{:S(2)}) %collective-permute-start.2) | collective-permute-done | bytes 163872 | tf_op jit(solution)/shard_map/ppermute | solution.py:527
  70.3 0.0 collective-permute-done.4.refs_2_
  70.3 0.0 collective-permute-done.5.refs_1_
  70.3 0.0 collective-permute-start.6
  70.3 0.0 all-to-all-done.1.query_ref
  70.3 9.4 %cross.2 = (bf16[4,512,128]{2,1,0:T(8,128)(2,1)S(1)}, f32[8,2560]{1,0:T(8,128)S(1)}) custom-call(s32[3]{0:T(128)S(1)} %pad_add_fusion.where_ref, s32[1,384]{1,0:T(1,128)S(1)} %get-tuple-element.28.pos_ref, bf16[4,784,128]{2,1,0:T(8,128)(2,1)S(1)} %all-to-all-done.1.query_ref, bf16[640,128]{1,0:T(8,128)(2,1)S(1)} %get-tuple-element.33.refs_0_, ...), custom_call_target="tpu_custom_call" | custom-call | flops 10000000000 | bytes 4000000 | tf_op jit(solution)/shard_map/cross/pallas_call | solution.py:538
  79.7 0.0 collective-permute-done.7.refs_3_
  79.7 0.0 collective-permute-done.6.refs_2_
  79.7 0.0 copy-start.4
  79.7 19.6 %cross.3 = (bf16[4,784,128]{2,1,0:T(8,128)(2,1)}, f32[1,384]{1,0:T(1,128)S(1)}) custom-call(s32[3]{0:T(128)S(1)} %pad_add_fusion.where_ref, s32[1,384]{1,0:T(1,128)S(1)} %get-tuple-element.28.pos_ref, bf16[4,784,128]{2,1,0:T(8,128)(2,1)S(1)} %all-to-all-done.1.query_ref, bf16[640,256]{1,0:T(8,128)(2,1)S(1)} %get-tuple-element.32.refs_0_, ...), custom_call_target="tpu_custom_call" | custom-call | flops 20000000000 | bytes 4000000 | tf_op jit(solution)/shard_map/cross/pallas_call | solution.py:538
  99.3 0.0 copy-start.3
  99.3 1.5 %collective-permute-start.9 = (f32[1,384]{1,0:T(1,128)S(1)}, f32[1,384]{1,0:T(1,128)S(1)}, u32[]{:S(2)}, u32[]{:S(2)}) collective-permute-start(f32[1,384]{1,0:T(1,128)S(1)} %get-tuple-element.41), channel_id=1, source_target_pairs={{0,1},{1,2},{2,3},{3,0},{4,5},{5,6},{6,7},{7,4},{8,9},{9,10},{10,1... | collective-permute-start | bytes 4616 | tf_op jit(solution)/shard_map/ppermute | solution.py:568
  100.8 0.6 collective-permute-start.10
  101.3 2.1 %collective-permute-start.8 = (f32[1,384]{1,0:T(1,128)S(1)}, f32[1,384]{1,0:T(1,128)S(1)}, u32[]{:S(2)}, u32[]{:S(2)}) collective-permute-start(f32[1,384]{1,0:T(1,128)S(1)} %get-tuple-element.41), channel_id=1, source_target_pairs={{0,2},{1,3},{2,0},{3,1},{4,6},{5,7},{6,4},{7,5},{8,10},{9,11},{10,... | collective-permute-start | bytes 4616 | tf_op jit(solution)/shard_map/ppermute | solution.py:568
  103.4 4.9 %all-to-all-start.3 = ((bf16[4,784,128]{2,1,0:T(8,128)(2,1)}), bf16[4,784,128]{2,1,0:T(8,128)(2,1)S(1)}, u32[]{:S(2)}, u32[]{:S(2)}) async-start(bf16[4,784,128]{2,1,0:T(8,128)(2,1)} %get-tuple-element.40), calls=%async_computation.3 | async-start | bytes 1605632 | tf_op jit(solution)/shard_map/all_to_all | solution.py:509
  108.3 0.0 collective-permute-done.9
  108.3 0.0 collective-permute-done.10
  108.3 0.0 collective-permute-done.8
  108.3 0.2 collective-permute-start.12
  108.5 3.2 %collective-permute-start.13 = (f32[1,384]{1,0:T(1,128)S(1)}, f32[1,384]{1,0:T(1,128)S(1)}, u32[]{:S(2)}, u32[]{:S(2)}) collective-permute-start(f32[1,384]{1,0:T(1,128)S(1)} %add_add_fusion.1), channel_id=1, source_target_pairs={{0,12},{1,13},{2,14},{3,15},{4,0},{5,1},{6,2},{7,3},{8,4},{9,5},{1... | collective-permute-start | bytes 4616 | tf_op jit(solution)/shard_map/ppermute | solution.py:527
  111.7 1.8 %collective-permute-start.11 = (f32[1,384]{1,0:T(1,128)S(1)}, f32[1,384]{1,0:T(1,128)S(1)}, u32[]{:S(2)}, u32[]{:S(2)}) collective-permute-start(f32[1,384]{1,0:T(1,128)S(1)} %add_add_fusion.1), channel_id=1, source_target_pairs={{0,8},{1,9},{2,10},{3,11},{4,12},{5,13},{6,14},{7,15},{8,0},{9,1},... | collective-permute-start | bytes 4616 | tf_op jit(solution)/shard_map/ppermute | solution.py:527
  113.5 0.0 collective-permute-done.12
  113.5 0.0 collective-permute-done.13
  113.5 3.3 %collective-permute-done.11 = f32[1,384]{1,0:T(1,128)S(1)} collective-permute-done((f32[1,384]{1,0:T(1,128)S(1)}, f32[1,384]{1,0:T(1,128)S(1)}, u32[]{:S(2)}, u32[]{:S(2)}) %collective-permute-start.11) | collective-permute-done | bytes 1568 | tf_op jit(solution)/shard_map/ppermute | solution.py:527
  116.8 0.6 slice.9
  118.0 0.6 fusion
  118.6 0.0 all-to-all-done.3.got_ref
  118.6 0.0 copy-done.4
  118.6 0.0 copy-done.3
  118.6 1.9 %final.1 = bf16[512,768]{1,0:T(8,128)(2,1)} custom-call(bf16[512,768]{1,0:T(8,128)(2,1)S(1)} %copy-done.4, bf16[4,784,128]{2,1,0:T(8,128)(2,1)S(1)} %all-to-all-done.3.got_ref, bf16[768,768]{1,0:T(8,128)(2,1)S(1)} %copy-done.3), custom_call_target="tpu_custom_call" | custom-call | flops 1000000000 | bytes 4000000 | tf_op jit(solution)/shard_map/final/pallas_call | solution.py:576
  (2 shorter events, 0.0 us)
Async XLA Ops:
  2.4 31.5 %collective-permute-start = (bf16[264,768]{1,0:T(8,128)(2,1)S(1)}, bf16[264,768]{1,0:T(8,128)(2,1)S(1)}, u32[]{:S(2)}, u32[]{:S(2)}) collective-permute-start(bf16[264,768]{1,0:T(8,128)(2,1)S(1)} %get-tuple-element.22), channel_id=1, source_target_pairs={{0,1},{1,2},{2,3},{3,4},{4,5},{5,6},{6,7},{7,8},{8,9},{9,10},{10,1... | collective-permute-start | bytes 1216520 | tf_op jit(solution)/shard_map/ppermute | solution.py:450
  5.8 28.1 %collective-permute-start.1 = (bf16[264,768]{1,0:T(8,128)(2,1)S(1)}, bf16[264,768]{1,0:T(8,128)(2,1)S(1)}, u32[]{:S(2)}, u32[]{:S(2)}) collective-permute-start(bf16[264,768]{1,0:T(8,128)(2,1)S(1)} %get-tuple-element.24), channel_id=1, source_target_pairs={{1,0},{2,1},{3,2},{4,3},{5,4},{6,5},{7,6},{8,7},{9,8},{10,9},{11,1... | collective-permute-start | bytes 1216520 | tf_op jit(solution)/shard_map/ppermute | solution.py:451
  8.3 9.8 %all-to-all-start = ((s32[8,1,320]{2,1,0:T(1,128)}), s32[8,1,320]{2,1,0:T(1,128)S(1)}, u32[]{:S(2)}, u32[]{:S(2)}) async-start(s32[8,1,320]{2,1,0:T(1,128)} %get-tuple-element.26), calls=%async_computation | async-start | bytes 24576 | tf_op jit(solution)/shard_map/all_to_all | solution.py:439
  12.8 0.9 copy-start.1
  25.1 8.8 %copy-start = (bf16[1,512,768]{2,1,0:T(8,128)(2,1)S(1)}, bf16[1,512,768]{2,1,0:T(8,128)(2,1)}, u32[]{:S(2)}) copy-start(bf16[1,512,768]{2,1,0:T(8,128)(2,1)} %param.10) | copy-start | bytes 2359300
  25.1 8.8 %copy-start.2 = (s32[1,512]{1,0:T(1,128)S(1)}, s32[1,512]{1,0:T(1,128)}, u32[]{:S(2)}) copy-start(s32[1,512]{1,0:T(1,128)} %tokens_ref.1) | copy-start | bytes 6148
  25.1 24.8 %all-to-all-start.2 = ((bf16[128,8,384]{2,1,0:T(8,128)(2,1)}), bf16[128,8,384]{2,1,0:T(8,128)(2,1)S(1)}, u32[]{:S(2)}, u32[]{:S(2)}) async-start(bf16[128,8,384]{2,1,0:T(8,128)(2,1)} %bitcast.5), calls=%async_computation.2 | async-start | bytes 1572864 | tf_op jit(solution)/shard_map/all_to_all | solution.py:475
  49.9 20.4 %all-to-all-start.1 = ((bf16[4,784,128]{2,1,0:T(8,128)(2,1)}), bf16[4,784,128]{2,1,0:T(8,128)(2,1)S(1)}, u32[]{:S(2)}, u32[]{:S(2)}) async-start(bf16[4,784,128]{2,1,0:T(8,128)(2,1)} %get-tuple-element.29), calls=%async_computation.1 | async-start | bytes 1605632 | tf_op jit(solution)/shard_map/all_to_all | solution.py:509
  55.6 5.8 %collective-permute-start.3 = (bf16[640,128]{1,0:T(8,128)(2,1)S(1)}, bf16[640,128]{1,0:T(8,128)(2,1)S(1)}, u32[]{:S(2)}, u32[]{:S(2)}) collective-permute-start(bf16[640,128]{1,0:T(8,128)(2,1)S(1)} %get-tuple-element.33.refs_0_), channel_id=1, source_target_pairs={{0,12},{1,13},{2,14},{3,15},{4,0},{5,1},{6,2},{7,3},{8,4},{9,5},{1... | collective-permute-start | bytes 491528 | tf_op jit(solution)/shard_map/ppermute | solution.py:527
  56.6 13.7 %collective-permute-start.5 = (bf16[640,256]{1,0:T(8,128)(2,1)S(1)}, bf16[640,256]{1,0:T(8,128)(2,1)S(1)}, u32[]{:S(2)}, u32[]{:S(2)}) collective-permute-start(bf16[640,256]{1,0:T(8,128)(2,1)S(1)} %get-tuple-element.32.refs_0_), channel_id=1, source_target_pairs={{0,4},{1,5},{2,6},{3,7},{4,8},{5,9},{6,10},{7,11},{8,12},{9,13},{1... | collective-permute-start | bytes 983048 | tf_op jit(solution)/shard_map/ppermute | solution.py:527
  57.7 12.6 %collective-permute-start.2 = (bf16[640,128]{1,0:T(8,128)(2,1)S(1)}, bf16[640,128]{1,0:T(8,128)(2,1)S(1)}, u32[]{:S(2)}, u32[]{:S(2)}) collective-permute-start(bf16[640,128]{1,0:T(8,128)(2,1)S(1)} %get-tuple-element.33.refs_0_), channel_id=1, source_target_pairs={{0,4},{1,5},{2,6},{3,7},{4,8},{5,9},{6,10},{7,11},{8,12},{9,13},{1... | collective-permute-start | bytes 491528 | tf_op jit(solution)/shard_map/ppermute | solution.py:527
  61.3 8.9 %collective-permute-start.4 = (bf16[640,128]{1,0:T(8,128)(2,1)S(1)}, bf16[640,128]{1,0:T(8,128)(2,1)S(1)}, u32[]{:S(2)}, u32[]{:S(2)}) collective-permute-start(bf16[640,128]{1,0:T(8,128)(2,1)S(1)} %collective-permute-done.3.refs_3_), channel_id=1, source_target_pairs={{0,12},{1,13},{2,14},{3,15},{4,0},{5,1},{6,2},{7,3},{8,4},{9,5},{1... | collective-permute-start | bytes 491528 | tf_op jit(solution)/shard_map/ppermute | solution.py:527
  63.5 16.1 %collective-permute-start.7 = (bf16[640,256]{1,0:T(8,128)(2,1)S(1)}, bf16[640,256]{1,0:T(8,128)(2,1)S(1)}, u32[]{:S(2)}, u32[]{:S(2)}) collective-permute-start(bf16[640,256]{1,0:T(8,128)(2,1)S(1)} %get-tuple-element.32.refs_0_), channel_id=1, source_target_pairs={{0,12},{1,13},{2,14},{3,15},{4,0},{5,1},{6,2},{7,3},{8,4},{9,5},{1... | collective-permute-start | bytes 983048 | tf_op jit(solution)/shard_map/ppermute | solution.py:527
  70.3 9.4 %collective-permute-start.6 = (bf16[640,256]{1,0:T(8,128)(2,1)S(1)}, bf16[640,256]{1,0:T(8,128)(2,1)S(1)}, u32[]{:S(2)}, u32[]{:S(2)}) collective-permute-start(bf16[640,256]{1,0:T(8,128)(2,1)S(1)} %collective-permute-done.5.refs_1_), channel_id=1, source_target_pairs={{0,4},{1,5},{2,6},{3,7},{4,8},{5,9},{6,10},{7,11},{8,12},{9,13},{1... | collective-permute-start | bytes 983048 | tf_op jit(solution)/shard_map/ppermute | solution.py:527
  79.7 38.9 %copy-start.4 = (bf16[512,768]{1,0:T(8,128)(2,1)S(1)}, bf16[512,768]{1,0:T(8,128)(2,1)}, u32[]{:S(2)}) copy-start(bf16[512,768]{1,0:T(8,128)(2,1)} %get-tuple-element.25.middle_ref) | copy-start | bytes 2359300
  99.3 19.3 %copy-start.3 = (bf16[768,768]{1,0:T(8,128)(2,1)S(1)}, bf16[768,768]{1,0:T(8,128)(2,1)}, u32[]{:S(2)}) copy-start(bf16[768,768]{1,0:T(8,128)(2,1)} %weight_ref.1) | copy-start | bytes 3538948
  99.3 9.0 %collective-permute-start.9 = (f32[1,384]{1,0:T(1,128)S(1)}, f32[1,384]{1,0:T(1,128)S(1)}, u32[]{:S(2)}, u32[]{:S(2)}) collective-permute-start(f32[1,384]{1,0:T(1,128)S(1)} %get-tuple-element.41), channel_id=1, source_target_pairs={{0,1},{1,2},{2,3},{3,0},{4,5},{5,6},{6,7},{7,4},{8,9},{9,10},{10,1... | collective-permute-start | bytes 4616 | tf_op jit(solution)/shard_map/ppermute | solution.py:568
  100.8 7.6 %collective-permute-start.10 = (f32[1,384]{1,0:T(1,128)S(1)}, f32[1,384]{1,0:T(1,128)S(1)}, u32[]{:S(2)}, u32[]{:S(2)}) collective-permute-start(f32[1,384]{1,0:T(1,128)S(1)} %get-tuple-element.41), channel_id=1, source_target_pairs={{0,3},{1,0},{2,1},{3,2},{4,7},{5,4},{6,5},{7,6},{8,11},{9,8},{10,9... | collective-permute-start | bytes 4616 | tf_op jit(solution)/shard_map/ppermute | solution.py:568
  101.3 7.0 %collective-permute-start.8 = (f32[1,384]{1,0:T(1,128)S(1)}, f32[1,384]{1,0:T(1,128)S(1)}, u32[]{:S(2)}, u32[]{:S(2)}) collective-permute-start(f32[1,384]{1,0:T(1,128)S(1)} %get-tuple-element.41), channel_id=1, source_target_pairs={{0,2},{1,3},{2,0},{3,1},{4,6},{5,7},{6,4},{7,5},{8,10},{9,11},{10,... | collective-permute-start | bytes 4616 | tf_op jit(solution)/shard_map/ppermute | solution.py:568
  103.4 15.2 %all-to-all-start.3 = ((bf16[4,784,128]{2,1,0:T(8,128)(2,1)}), bf16[4,784,128]{2,1,0:T(8,128)(2,1)S(1)}, u32[]{:S(2)}, u32[]{:S(2)}) async-start(bf16[4,784,128]{2,1,0:T(8,128)(2,1)} %get-tuple-element.40), calls=%async_computation.3 | async-start | bytes 1605632 | tf_op jit(solution)/shard_map/all_to_all | solution.py:509
  108.3 5.1 %collective-permute-start.12 = (f32[1,384]{1,0:T(1,128)S(1)}, f32[1,384]{1,0:T(1,128)S(1)}, u32[]{:S(2)}, u32[]{:S(2)}) collective-permute-start(f32[1,384]{1,0:T(1,128)S(1)} %add_add_fusion.1), channel_id=1, source_target_pairs={{0,4},{1,5},{2,6},{3,7},{4,8},{5,9},{6,10},{7,11},{8,12},{9,13},{1... | collective-permute-start | bytes 4616 | tf_op jit(solution)/shard_map/ppermute | solution.py:527
  108.5 5.0 %collective-permute-start.13 = (f32[1,384]{1,0:T(1,128)S(1)}, f32[1,384]{1,0:T(1,128)S(1)}, u32[]{:S(2)}, u32[]{:S(2)}) collective-permute-start(f32[1,384]{1,0:T(1,128)S(1)} %add_add_fusion.1), channel_id=1, source_target_pairs={{0,12},{1,13},{2,14},{3,15},{4,0},{5,1},{6,2},{7,3},{8,4},{9,5},{1... | collective-permute-start | bytes 4616 | tf_op jit(solution)/shard_map/ppermute | solution.py:527
  111.7 5.1 %collective-permute-start.11 = (f32[1,384]{1,0:T(1,128)S(1)}, f32[1,384]{1,0:T(1,128)S(1)}, u32[]{:S(2)}, u32[]{:S(2)}) collective-permute-start(f32[1,384]{1,0:T(1,128)S(1)} %add_add_fusion.1), channel_id=1, source_target_pairs={{0,8},{1,9},{2,10},{3,11},{4,12},{5,13},{6,14},{7,15},{8,0},{9,1},... | collective-permute-start | bytes 4616 | tf_op jit(solution)/shard_map/ppermute | solution.py:527
